TPU v7x, 512 devices: a whole 4x8x8 slice. The times are simulated.
512 devices in a mesh: grp: 16 (over z, core), dom: 32 (over x, y).
Axes of the slice: x: 4, y: 8, z: 8, core: 2. Of those that a mesh axis runs over, the one named last changes fastest.
Arguments:
- leaf_load: bfloat16 [32, 16, 1024, 128], P('dom', 'grp'), may hold values from -6 to 6
- leaf_map: bfloat16 [32, 16, 1024, 1024], P('dom', 'grp'), may hold values from -0.1875 to 0.1875
- group_map: bfloat16 [32, 4096, 4096], P('dom', 'grp'), may hold values from -0.09375 to 0.09375
- node_index: int32 [32, 16, 1024], P('dom', 'grp'), may hold values from 0 to 4095, as said below
- west_coupling: float32 [32, 256, 256], P('dom'), may hold values from -1.5 to 1.5
- east_coupling: float32 [32, 256, 256], P('dom'), may hold values from -1.5 to 1.5
Outputs:
- leaf_solution: bfloat16 [32, 16, 1024, 128], P('dom', 'grp')
Inputs may be any that keep to these rules, and one draw needn't show every extreme that they name: `node_index`: each leaf's list names 1024 different interface nodes of its group.
All inputs are finite; a program needn't handle non-finite values.
Results may differ from a plain program's by a relative error of at most 0.015.
Values may be sent and summed in bfloat16 or wider, within the bound.
No kernel may reach another device: no remote copies, remote signals or barrier semaphores. Data moves between devices by JAX's collectives and lax.ppermute only.
A program may use at most 128 MiB of HBM per device.

v0:
```python
import jax
import jax.numpy as jnp
from jax import lax
from jax.sharding import PartitionSpec as P


def carried_in(part, axis, combine, identity, reverse):
    count = lax.axis_size(axis)
    place = lax.axis_index(axis)
    ahead = count - 1 - place if reverse else place
    gathered = jax.tree.map(lambda a: lax.all_gather(a, axis), part)
    state = jax.tree.map(lambda a, e: jnp.zeros_like(a) + jnp.asarray(e, a.dtype), part, identity)

    def one(turn, state):
        source = count - 1 - turn if reverse else turn
        return combine(
            state, jax.tree.map(lambda a: lax.dynamic_index_in_dim(a, source, 0, False), gathered)
        )

    return lax.fori_loop(0, ahead, one, state)


def compose(earlier, follower):
    early_map, early_value = earlier
    late_map, late_value = follower
    joined_map = jnp.dot(
        late_map, early_map, precision=lax.Precision.HIGHEST, preferred_element_type=jnp.float32
    )
    joined_value = (
        jnp.dot(
            late_map,
            early_value,
            precision=lax.Precision.HIGHEST,
            preferred_element_type=jnp.float32,
        )
        + late_value
    )
    return (joined_map, joined_value)


def on_device(leaf_load, leaf_map, group_map, node_index, west_coupling, east_coupling):
    exact_mode = lax.Precision.HIGHEST
    columns = leaf_load.shape[3]
    interface = group_map.shape[2]
    face_nodes = west_coupling.shape[1]
    stride = interface // face_nodes
    local_map = leaf_map[0, 0]
    local_load = leaf_load[0, 0]
    local_index = node_index[0, 0]
    contrib = jnp.dot(local_map, local_load, preferred_element_type=jnp.float32).astype(
        jnp.bfloat16
    )
    scattered = (
        jnp.zeros((interface, columns), jnp.float32)
        .at[local_index]
        .add(contrib.astype(jnp.float32))
    )
    summed_loads = lax.psum(scattered.astype(jnp.bfloat16), "grp")
    rows_map = group_map[0]
    row_count = rows_map.shape[0]
    blocks = row_count // stride
    initial_rows = jnp.dot(rows_map, summed_loads, preferred_element_type=jnp.float32)
    block_view = rows_map.reshape(blocks, stride, face_nodes, stride)
    column_view = rows_map.reshape(row_count, face_nodes, stride)
    west_columns = column_view[:, :, 0].astype(jnp.float32)
    east_columns = column_view[:, :, 1].astype(jnp.float32)
    east_west = block_view[:, 1, :, 0].astype(jnp.float32)
    west_east = block_view[:, 0, :, 1].astype(jnp.float32)
    identity_map = jnp.eye(face_nodes, dtype=jnp.float32)
    zero_values = jnp.zeros((face_nodes, columns), jnp.float32)
    forward_maps = jnp.dot(east_west, west_coupling[0], precision=exact_mode)
    east_values = initial_rows.reshape(blocks, stride, columns)[:, 1]
    face_maps, face_values = (
        lax.all_gather(forward_maps, "grp", axis=0, tiled=True),
        lax.all_gather(east_values, "grp", axis=0, tiled=True),
    )
    _, incoming = carried_in(
        (face_maps, face_values), "dom", compose, (identity_map, zero_values), False
    )
    swept_rows = initial_rows + jnp.dot(
        west_columns,
        jnp.dot(west_coupling[0], incoming, precision=exact_mode),
        precision=exact_mode,
    )
    backward_maps = jnp.dot(west_east, east_coupling[0], precision=exact_mode)
    west_values = swept_rows.reshape(blocks, stride, columns)[:, 0]
    back_maps, back_values = (
        lax.all_gather(backward_maps, "grp", axis=0, tiled=True),
        lax.all_gather(west_values, "grp", axis=0, tiled=True),
    )
    _, outgoing = carried_in(
        (back_maps, back_values), "dom", compose, (identity_map, zero_values), True
    )
    final_rows = swept_rows + jnp.dot(
        east_columns,
        jnp.dot(east_coupling[0], outgoing, precision=exact_mode),
        precision=exact_mode,
    )
    gathered = lax.all_gather(final_rows.astype(jnp.bfloat16), "grp", axis=0, tiled=True)
    picked = gathered[local_index]
    result = lax.dot_general(
        local_map, picked, (((0,), (0,)), ((), ())), preferred_element_type=jnp.float32
    )
    result = result + local_load.astype(jnp.float32)
    return result.astype(jnp.bfloat16)[None, None]


def solution(mesh):
    return jax.shard_map(
        on_device,
        mesh=mesh,
        in_specs=(
            P("dom", "grp", None, None),
            P("dom", "grp", None, None),
            P("dom", "grp", None),
            P("dom", "grp", None),
            P("dom", None, None),
            P("dom", None, None),
        ),
        out_specs=P("dom", "grp", None, None),
        check_vma=False,
    )
```

profile of v0, /device:TPU:1, one launch (start us, length us, event | category | flops | bytes accessed | tf_op | source)
XLA Modules:
  0.0 639.1 jit_solution(5721224680582235260)
XLA Ops:
  8.1 1.6 fusion.21
  9.8 7.4 %scatter_custom_fusion = f32[4096,128]{1,0:T(8,128)} fusion(s32[1024]{0:T(1024)S(1)} %bitcast.114, f32[1024,128]{1,0:T(8,128)S(1)} %fusion.21, f32[]{:T(128)} %constant.56.clone.1), kind=kCustom, calls=%fused_computation.30 | custom fusion | flops 131072 | bytes 2097156 | tf_op jit(solution)/shard_map/scatter-add | solution.py:56
  17.2 2.7 convert_element_type.25
  20.0 123.9 %all-reduce.2.cloned.1.call-done = bf16[4096,128]{1,0:T(8,128)(2,1)} async-done(((bf16[4096,128]{1,0:T(8,128)(2,1)}), bf16[4096,128]{1,0:T(8,128)(2,1)}) %all-reduce.2.cloned.1.call-update) | async-done | bytes 1048592 | tf_op jit(solution)/shard_map/psum | solution.py:58
  143.9 2.7 fusion.30
  146.8 16.8 %all-gather.1 = f32[256,1,128]{2,1,0:T(1,128)} all-gather(f32[16,1,128]{2,1,0:T(1,128)S(1)} %slice.27), channel_id=3, replica_groups=mesh['grp'=16,'dom'=32] {'grp'}, dimensions={0}, use_global_device_ids=true | all-gather | bytes 139264 | tf_op jit(solution)/shard_map/all_gather | solution.py:75
  163.6 16.8 %reshape_squeeze.6 = bf16[16,16,256,16]{3,2,1,0:T(8,128)(2,1)} reshape(bf16[1,256,4096]{2,1,0:T(8,128)(2,1)} %param.12) | data formatting | bytes 4194304 | tf_op jit(solution)/shard_map/reshape;squeeze | solution.py:63
  180.4 2.6 slice_reduce_fusion
  183.2 18.9 %all_gather.39 = f32[256,256]{1,0:T(8,128)} all-gather(f32[16,256]{1,0:T(8,128)S(1)} %fusion.45), channel_id=1, replica_groups=mesh['grp'=16,'dom'=32] {'grp'}, dimensions={0}, use_global_device_ids=true | all-gather | bytes 278528 | tf_op jit(solution)/shard_map/all_gather | solution.py:74
  202.4 16.7 %all_gather.45 = f32[256,256]{1,0:T(8,128)} all-gather(f32[16,256]{1,0:T(8,128)S(1)} %fusion.41), channel_id=1, replica_groups=mesh['grp'=16,'dom'=32] {'grp'}, dimensions={0}, use_global_device_ids=true | all-gather | bytes 278528 | tf_op jit(solution)/shard_map/all_gather | solution.py:88
  219.2 4.1 copy.22
  223.3 2.0 fusion.49
  225.5 21.1 %all-gather.16.cloned.1.call-done = f32[8192,1,128]{2,1,0:T(1,128)} async-done(((f32[256,1,128]{2,1,0:T(1,128)}), f32[8192,1,128]{2,1,0:T(1,128)}) %all-gather.16.cloned.1.call-update) | async-done | bytes 4194320 | tf_op jit(solution)/shard_map/all_gather | solution.py:11
  246.6 106.2 %all-gather.14.cloned.1.call-done = f32[8192,256]{1,0:T(8,128)} async-done(((f32[256,256]{1,0:T(8,128)}), f32[8192,256]{1,0:T(8,128)}) %all-gather.14.cloned.1.call-update) | async-done | bytes 8388624 | tf_op jit(solution)/shard_map/all_gather | solution.py:11
  353.6 21.1 %all-gather.4 = f32[256,1,128]{2,1,0:T(1,128)} all-gather(f32[16,1,128]{2,1,0:T(1,128)S(1)} %slice.30), channel_id=6, replica_groups=mesh['grp'=16,'dom'=32] {'grp'}, dimensions={0}, use_global_device_ids=true | all-gather | bytes 139264 | tf_op jit(solution)/shard_map/all_gather | solution.py:89
  374.9 81.4 %all-gather.18.cloned.1.call-done = f32[8192,256]{1,0:T(8,128)} async-done(((f32[256,256]{1,0:T(8,128)}), f32[8192,256]{1,0:T(8,128)}) %all-gather.18.cloned.1.call-update) | async-done | bytes 8388624 | tf_op jit(solution)/shard_map/all_gather | solution.py:11
  456.3 84.8 %all-gather.20.cloned.1.call-done = f32[8192,1,128]{2,1,0:T(1,128)} async-done(((f32[256,1,128]{2,1,0:T(1,128)}), f32[8192,1,128]{2,1,0:T(1,128)}) %all-gather.20.cloned.1.call-update) | async-done | bytes 4194320 | tf_op jit(solution)/shard_map/all_gather | solution.py:11
  541.1 43.8 %while.27 = (s32[]{:T(128)}, f32[256,128]{1,0:T(8,128)S(1)}, s32[]{:T(128)}, f32[32,256,256]{2,1,0:T(8,128)}, f32[32,256,128]{2,1,0:T(8,128)}, /*index=5*/s32[]{:T(128)}, s32[]{:T(128)}, s32[]{:T(128)}, s32[]{:T(128)}) while((s32[]{:T(128)}, f32[256,128]{1,0:T(8,128)S(1)}, s32[]{:T(128)}, f32[32,256,256]{2,1,0:T(8,128)}, ...), condition=%wide.region_5.6_spmd, body=%wide.region_4.5_spmd.sunk | while | flops 100696072 | bytes 918675 | solution.py:20
  541.1 1.4 convolution_add_fusion.5
  544.0 1.4 convolution_add_fusion.5
  548.2 1.4 convolution_add_fusion.5
  549.6 1.4 convolution_add_fusion.5
  556.7 1.4 convolution_add_fusion.5
  558.1 1.4 convolution_add_fusion.5
  565.2 1.4 convolution_add_fusion.5
  566.6 1.4 convolution_add_fusion.5
  573.6 1.4 convolution_add_fusion.5
  575.1 1.4 convolution_add_fusion.5
  587.1 38.1 %all-gather.12.cloned.1.call-done = bf16[4096,128]{0,1:T(8,128)(2,1)} async-done(((bf16[256,128]{0,1:T(8,128)(2,1)}), bf16[4096,128]{0,1:T(8,128)(2,1)}) %all-gather.12.cloned.1.call-update) | async-done | bytes 1048592 | tf_op jit(solution)/shard_map/all_gather | solution.py:99
  625.2 1.6 copy.26
  626.8 3.2 gather_fusion
  630.0 1.4 fusion.27
  (91 shorter events, 35.5 us)
Async XLA Ops:
  6.5 1.6 copy-start
  6.5 137.4 %all-reduce.2.cloned.1.call-start = ((), (), s32[]{:S(2)}) async-start(), calls=%async_computation | async-start | bytes 2097152 | tf_op jit(solution)/shard_map/psum | solution.py:58
  19.9 226.7 %all-gather.16.cloned.1.call-start = ((), (), s32[]{:S(2)}) async-start(), calls=%async_computation.3 | async-start | bytes 4325376 | tf_op jit(solution)/shard_map/all_gather | solution.py:11
  163.5 189.2 %all-gather.14.cloned.1.call-start = ((), (), s32[]{:S(2)}) async-start(), calls=%async_computation.2 | async-start | bytes 8650752 | tf_op jit(solution)/shard_map/all_gather | solution.py:11
  180.4 2.6 copy-start.1
  180.4 21.8 %copy-start.2 = (f32[1,256,256]{2,1,0:T(8,128)S(1)}, f32[1,256,256]{2,1,0:T(8,128)}, u32[]{:S(2)}) copy-start(f32[1,256,256]{2,1,0:T(8,128)} %param.15) | copy-start | bytes 786436
  202.1 254.1 %all-gather.18.cloned.1.call-start = ((), (), s32[]{:S(2)}) async-start(), calls=%async_computation.4 | async-start | bytes 8650752 | tf_op jit(solution)/shard_map/all_gather | solution.py:11
  219.1 321.9 %all-gather.20.cloned.1.call-start = ((), (), s32[]{:S(2)}) async-start(), calls=%async_computation.5 | async-start | bytes 4325376 | tf_op jit(solution)/shard_map/all_gather | solution.py:11
  374.7 250.5 %all-gather.12.cloned.1.call-start = ((), (), s32[]{:S(2)}) async-start(), calls=%async_computation.1 | async-start | bytes 1114112 | tf_op jit(solution)/shard_map/all_gather | solution.py:99
  541.1 45.2 %copy-start.3 = (bf16[1,1,1024,128]{3,2,1,0:T(8,128)(2,1)S(1)}, bf16[1,1,1024,128]{3,2,1,0:T(8,128)(2,1)}, u32[]{:S(2)}) copy-start(bf16[1,1,1024,128]{3,2,1,0:T(8,128)(2,1)} %param.10) | copy-start | bytes 786436
Sparse Core Ops, SparseCore 0:
  20.0 123.8 all-reduce.1
  163.7 82.8 all-gather.15
  249.8 102.9 all-gather.13
  355.8 100.4 all-gather.17
  459.3 81.7 all-gather.19
  586.4 38.7 all-gather.11
where the time goes:
time: 641 us; the launch traced here: 639 us
  waiting for transfers between devices  456 us (71%)
  blocking collectives  73.4 us (11%)
  matrix products  50.5 us (8%)
  local copies, waits for them, and re-layouts  33.6 us (5%)
  between operations  13.6 us (2%)
  other arithmetic  10.9 us (2%)
    all_gather x4, waiting for transfers between devices, carried_in(): gathered = jax.tree.map(lambda a: lax.all_gather(a, axis), part)  293 us
    psum x1, waiting for transfers between devices, on_device(): summed_loads = lax.psum(scattered.astype(jnp.bfloat16), 'grp')  124 us
    dot_general x31, matrix products, compose(): jnp.dot(late_map, early_value, precision=lax.Precision.HIGHEST, preferred...  42.3 us
    all_gather x1, waiting for transfers between devices, on_device(): lax.all_gather(final_rows.astype(jnp.bfloat16), 'grp', axis=0, tiled=True)  38.1 us
    all_gather x1, blocking collectives, on_device(): lax.all_gather(west_values, 'grp', axis=0, tiled=True)  21.1 us
    all_gather x1, blocking collectives, on_device(): lax.all_gather(forward_maps, 'grp', axis=0, tiled=True)  18.9 us
    another operation x1, local copies, waits for them, and re-layouts, on_device(): block_view = rows_map.reshape(blocks, stride, face_nodes, stride)  16.8 us
    all_gather x1, blocking collectives, on_device(): lax.all_gather(east_values, 'grp', axis=0, tiled=True)  16.8 us
  transfers between devices with their start and end apart: 6, of which 6 were waited for; matrix products, arithmetic and copies ran while one was open for 4% of the time, Pallas kernels for 0%

commit v1 on v0

v1 whole, which is shorter than its diff:
```python
import functools

import jax
import jax.numpy as jnp
from jax import lax
from jax.experimental import pallas as pl
from jax.experimental.pallas import tpu as pltpu
from jax.sharding import Mesh
from jax.sharding import PartitionSpec as P

F32 = jnp.float32
BF16 = jnp.bfloat16
GRP = ("z", "c")
NT = (((1,), (1,)), ((), ()))
VM = pl.BlockSpec(memory_space=pltpu.VMEM)
SM = pl.BlockSpec(memory_space=pltpu.SMEM)
PARAMS = pltpu.CompilerParams(vmem_limit_bytes=56 * 1024 * 1024)


def call(kernel, name, outs, scratch, smem, cost, *args):
    specs = [SM] * smem + [VM] * (len(args) - smem)
    flops, moved = cost
    return pl.pallas_call(
        kernel,
        name=name,
        out_shape=outs,
        in_specs=specs,
        out_specs=jax.tree.map(lambda _: VM, outs),
        scratch_shapes=scratch,
        compiler_params=PARAMS,
        cost_estimate=pl.CostEstimate(flops=flops, bytes_accessed=moved, transcendentals=0),
    )(*args)


def spread_rows(pos, map_ref, load_ref, keep_ref, send_ref, contrib, rows):
    contrib[...] = (
        jnp.dot(map_ref[...], load_ref[...], preferred_element_type=F32).astype(BF16).astype(F32)
    )
    rows[...] = jnp.zeros_like(rows)
    count = contrib.shape[0]
    unroll = 16

    def some(turn, carry):
        base = pl.multiple_of(turn * unroll, unroll)
        for k in range(unroll):
            rows[pl.ds(pos[base + k], 1), :] = contrib[pl.ds(base + k, 1), :]
        return carry

    lax.fori_loop(0, count // unroll, some, 0)
    half = keep_ref.shape[0]
    keep_ref[...] = rows[:half].astype(BF16)
    send_ref[...] = rows[half:].astype(BF16)


def first_rows(core, map_ref, own_ref, other_ref, initial_ref, faces_ref, acc, *, width, stride):
    side = core[0]
    pairs = own_ref.shape[0] // width
    acc[...] = jnp.zeros_like(acc)
    for z in range(pairs):
        mine = pl.ds(pl.multiple_of((2 * z + side) * width, width), width)
        theirs = pl.ds(pl.multiple_of((2 * z + 1 - side) * width, width), width)
        block = slice(z * width, (z + 1) * width)
        acc[...] += jnp.dot(map_ref[:, mine], own_ref[block], preferred_element_type=F32)
        acc[...] += jnp.dot(map_ref[:, theirs], other_ref[block], preferred_element_type=F32)
    initial_ref[...] = acc[...]
    nodes = acc.shape[0] // stride
    west = acc[pl.ds(0, nodes, stride=stride), :]
    east = acc[pl.ds(1, nodes, stride=stride), :]
    both = jnp.concatenate([east, west], axis=0)
    lanes = both.shape[1]
    peers = faces_ref.shape[0]
    part = lanes // peers
    for g in range(peers):
        turned = both if g == 0 else pltpu.roll(both, lanes - part * g, axis=1)
        faces_ref[g] = turned.astype(BF16)


def face_columns(got_ref, out_ref, order, *, nodes, part):
    peers = got_ref.shape[0]
    for g in range(peers):
        both = got_ref[g].astype(F32)
        order[pl.ds(g * nodes, nodes), :] = both[:nodes]
        order[pl.ds((peers + g) * nodes, nodes), :] = both[nodes:]
    line = order[...].T[:part].astype(BF16)
    for y in range(out_ref.shape[0]):
        out_ref[y] = line


def halves(value):
    high = value.astype(BF16)
    low = (value - high.astype(F32)).astype(BF16)
    return high, low


def exact_right(left, value):
    high, low = halves(value)
    return jnp.dot(left, high, preferred_element_type=F32) + jnp.dot(
        left, low, preferred_element_type=F32
    )


def exact_rows(value, right):
    rows = value.shape[0]
    high, low = halves(value)
    both = lax.dot_general(
        jnp.concatenate([high, low], axis=0), right, NT, preferred_element_type=F32
    )
    return both[:rows] + both[rows:]


def block_maps(place, maps_ref, joined_ref, own_ref, state, right, through):
    count = maps_ref.shape[0]
    n = maps_ref.shape[2]
    here = place[0]
    unit = (
        lax.broadcasted_iota(jnp.int32, (n, n), 0) == lax.broadcasted_iota(jnp.int32, (n, n), 1)
    ).astype(F32)
    state[...] = unit

    def onward(j, carry):
        value = state[...]

        @pl.when(j == here)
        def _():
            own_ref[0:n] = value.astype(own_ref.dtype)

        both = exact_right(maps_ref[j, 0 : 2 * n, :], value)
        state[...] = both[:n]
        through[j] = both[n:]
        return carry

    lax.fori_loop(0, count, onward, 0)
    joined_ref[0:n] = state[...].astype(BF16)
    right[:, 0:n] = unit
    right[:, n : 2 * n] = jnp.zeros((n, n), F32)

    def back(turn, carry):
        j = count - 1 - turn
        value = right[...]

        @pl.when(j == here)
        def _():
            own_ref[n : 2 * n] = value[:, 0:n].astype(own_ref.dtype)
            own_ref[2 * n : 3 * n] = value[:, n : 2 * n].astype(own_ref.dtype)

        both = exact_right(maps_ref[j, 2 * n : 3 * n, :], value)
        right[:, 0:n] = both[:, 0:n]
        right[:, n : 2 * n] = both[:, n : 2 * n] + through[j]
        return carry

    lax.fori_loop(0, count, back, 0)
    joined_ref[n : 2 * n] = right[:, 0:n].astype(BF16)
    joined_ref[2 * n : 3 * n] = right[:, n : 2 * n].astype(BF16)


def block_values(place, faces_ref, maps_ref, ends_ref, own_ref):
    count, part, _ = faces_ref.shape
    n = maps_ref.shape[2]
    here = place[0]
    value = jnp.zeros((part, n), F32)
    sources = []
    for j in range(count):

        @pl.when(here == j)
        def _(value=value):
            own_ref[:, 0:n] = value

        both = exact_rows(value, maps_ref[j, 0 : 2 * n, :]) if j else None
        given = faces_ref[j].astype(F32)
        if j:
            value = given[:, 0:n] + both[:, 0:n]
            sources.append(given[:, n : 2 * n] + both[:, n : 2 * n])
        else:
            value = given[:, 0:n]
            sources.append(given[:, n : 2 * n])
    east = value
    value = jnp.zeros((part, n), F32)
    for j in range(count - 1, -1, -1):

        @pl.when(here == j)
        def _(value=value):
            own_ref[:, n : 2 * n] = value

        value = sources[j] + (
            exact_rows(value, maps_ref[j, 2 * n : 3 * n, :]) if j < count - 1 else 0.0
        )
    ends = jnp.concatenate([east, value], axis=1).astype(BF16)
    for x in range(ends_ref.shape[0]):
        ends_ref[x] = ends


def meet_values(place, ends_ref, joined_ref, maps_ref, own_ref, out_ref, entering):
    count, part, _ = ends_ref.shape
    n = joined_ref.shape[2]
    here = place[0]
    east = jnp.zeros((part, n), F32)
    sources = []
    for b in range(count):

        @pl.when(here == b)
        def _(east=east):
            entering[:, 0:n] = east

        end = ends_ref[b].astype(F32)
        source = end[:, n : 2 * n]
        if b:
            source = source + exact_rows(east, joined_ref[b, 2 * n : 3 * n, :])
        sources.append(source)
        east = end[:, 0:n] + (exact_rows(east, joined_ref[b, 0:n, :]) if b else 0.0)
    west = jnp.zeros((part, n), F32)
    for b in range(count - 1, -1, -1):

        @pl.when(here == b)
        def _(west=west):
            entering[:, n : 2 * n] = west

        west = sources[b] + (
            exact_rows(west, joined_ref[b, n : 2 * n, :]) if b < count - 1 else 0.0
        )
    east = entering[:, 0:n]
    west = entering[:, n : 2 * n]
    own = own_ref[...]
    met_east = own[:, 0:n] + exact_rows(east, maps_ref[0:n])
    met_west = (
        own[:, n : 2 * n]
        + exact_rows(west, maps_ref[n : 2 * n])
        + exact_rows(east, maps_ref[2 * n : 3 * n])
    )
    met = jnp.concatenate([met_east, met_west], axis=1).astype(BF16)
    for g in range(out_ref.shape[0]):
        out_ref[g] = met


def leaf_result(pos, own_ref, other_ref, map_ref, load_ref, out_ref, rows, picked):
    half = own_ref.shape[0]
    rows[0:half] = own_ref[...].astype(F32)
    rows[half : 2 * half] = other_ref[...].astype(F32)
    count = picked.shape[0]
    unroll = 16

    def some(turn, carry):
        base = pl.multiple_of(turn * unroll, unroll)
        for k in range(unroll):
            picked[pl.ds(base + k, 1), :] = rows[pl.ds(pos[base + k], 1), :]
        return carry

    lax.fori_loop(0, count // unroll, some, 0)
    turned = picked[...].T.astype(BF16)
    result = jnp.dot(turned, map_ref[...], preferred_element_type=F32)
    out_ref[...] = (result.T + load_ref[...].astype(F32)).astype(BF16)


def on_device(leaf_load, leaf_map, group_map, node_index, west_coupling, east_coupling):
    local_map, local_load, nodes_of = leaf_map[0, 0], leaf_load[0, 0], node_index[0, 0]
    rows_map, west, east = group_map[0], west_coupling[0], east_coupling[0]
    nz, nc = lax.axis_size("z"), lax.axis_size("c")
    nx, ny = lax.axis_size("x"), lax.axis_size("y")
    peers = nz * nc
    leaf_nodes, columns = local_load.shape
    width, interface = rows_map.shape
    n = west.shape[0]
    stride = interface // n
    nodes = n // peers
    part = columns // peers
    half = interface // nc
    side = lax.axis_index("c")
    core = jnp.reshape(side, (1,)).astype(jnp.int32)
    at_y = jnp.reshape(lax.axis_index("y"), (1,)).astype(jnp.int32)
    at_x = jnp.reshape(lax.axis_index("x"), (1,)).astype(jnp.int32)
    swap = [(0, 1), (1, 0)]

    spot = lax.broadcasted_iota(jnp.int32, (interface, 2 * n), 0)
    want = lax.broadcasted_iota(jnp.int32, (interface, 2 * n), 1)
    want = jnp.where(want < n, want * stride, (want - n) * stride + 1)
    face_map = jnp.dot(rows_map, (spot == want).astype(BF16), preferred_element_type=F32)
    west_high, west_low = halves(west)
    east_high, east_low = halves(east)
    face_low = face_map.astype(BF16)
    coupled = jnp.concatenate(
        [
            jnp.dot(face_low[:, :n], west_high, preferred_element_type=F32)
            + jnp.dot(face_low[:, :n], west_low, preferred_element_type=F32),
            jnp.dot(face_low[:, n:], east_high, preferred_element_type=F32)
            + jnp.dot(face_low[:, n:], east_low, preferred_element_type=F32),
        ],
        axis=1,
    ).astype(BF16)
    steps = coupled.reshape(nodes, stride, 2 * n)
    slices = jnp.concatenate([steps[:, 1, :n], steps[:, 0, :n], steps[:, 0, n:]], axis=0)
    slices = jnp.broadcast_to(slices, (peers,) + slices.shape)
    slices = lax.all_to_all(slices, GRP, 0, 0)
    maps = slices.reshape(peers, 3, nodes, n).transpose(1, 0, 2, 3).reshape(3 * n, n)
    run_maps = lax.all_gather(maps, "y")

    owner = nodes_of // width
    pos = ((owner % nc) ^ side) * half + (owner // nc) * width + nodes_of % width
    keep, send = call(
        spread_rows,
        "spread_rows",
        (jax.ShapeDtypeStruct((half, columns), BF16),) * 2,
        [pltpu.VMEM((leaf_nodes, columns), F32), pltpu.VMEM((interface, columns), F32)],
        1,
        (2 * leaf_nodes * leaf_nodes * columns, 6 * leaf_nodes * leaf_nodes),
        pos,
        local_map,
        local_load,
    )
    got = lax.ppermute(send, "c", swap)
    paired = (keep.astype(F32) + got.astype(F32)).astype(BF16)
    parts = lax.all_to_all(paired.reshape(nz, width, columns), "z", 0, 0)
    loads = jnp.sum(parts.astype(F32), axis=0).astype(BF16)
    loads = lax.all_to_all(jnp.broadcast_to(loads, (nz, width, columns)), "z", 0, 0)
    loads_own = loads.reshape(half, columns)
    loads_other = lax.ppermute(loads_own, "c", swap)

    initial, faces = call(
        functools.partial(first_rows, width=width, stride=stride),
        "first_rows",
        (
            jax.ShapeDtypeStruct((width, columns), F32),
            jax.ShapeDtypeStruct((peers, 2 * nodes, columns), BF16),
        ),
        [pltpu.VMEM((width, columns), F32)],
        1,
        (2 * width * interface * columns, 2 * width * interface),
        core,
        rows_map,
        loads_own,
        loads_other,
    )
    faces = lax.all_to_all(faces, GRP, 0, 0)

    run_maps, loads_own = lax.optimization_barrier((run_maps, loads_own))
    joined, own_maps = call(
        block_maps,
        "block_maps",
        (jax.ShapeDtypeStruct((3 * n, n), BF16), jax.ShapeDtypeStruct((3 * n, n), BF16)),
        [
            pltpu.VMEM((n, n), F32),
            pltpu.VMEM((n, 2 * n), F32),
            pltpu.VMEM((ny, n, n), F32),
        ],
        1,
        (16 * ny * n**3, 6 * ny * n * n),
        at_y,
        run_maps,
    )
    all_joined = lax.all_gather(joined, "x")

    line = call(
        functools.partial(face_columns, nodes=nodes, part=part),
        "face_columns",
        jax.ShapeDtypeStruct((ny, part, 2 * n), BF16),
        [pltpu.VMEM((2 * n, columns), F32)],
        0,
        (1000, 4 * n * columns),
        faces,
    )
    line = lax.all_to_all(line, "y", 0, 0)
    ends, own_values = call(
        block_values,
        "block_values",
        (
            jax.ShapeDtypeStruct((nx, part, 2 * n), BF16),
            jax.ShapeDtypeStruct((part, 2 * n), F32),
        ),
        [],
        1,
        (12 * ny * n * n * 16, 6 * ny * n * n),
        at_y,
        line,
        run_maps,
    )
    ends = lax.all_to_all(ends, "x", 0, 0)
    met = call(
        meet_values,
        "meet_values",
        jax.ShapeDtypeStruct((peers, part, 2 * n), BF16),
        [pltpu.VMEM((part, 2 * n), F32)],
        1,
        (12 * nx * n * n * 16, 6 * nx * n * n),
        at_x,
        ends,
        all_joined,
        own_maps,
        own_values,
    )
    met = lax.all_to_all(met, GRP, 0, 0).reshape(columns, 2 * n)

    final = initial + lax.dot_general(coupled, met, NT, preferred_element_type=F32)
    final = jnp.broadcast_to(final.astype(BF16), (nz, width, columns))
    final_own = lax.all_to_all(final, "z", 0, 0).reshape(half, columns)
    final_other = lax.ppermute(final_own, "c", swap)
    result = call(
        leaf_result,
        "leaf_result",
        jax.ShapeDtypeStruct((leaf_nodes, columns), BF16),
        [pltpu.VMEM((interface, columns), F32), pltpu.VMEM((leaf_nodes, columns), F32)],
        1,
        (2 * leaf_nodes * leaf_nodes * columns, 2 * leaf_nodes * leaf_nodes),
        pos,
        final_own,
        final_other,
        local_map,
        local_load,
    )
    return result[None, None]


SPLITS = {(16, 32): (8, 2, 4, 8)}


def solution(mesh):
    shape = SPLITS.get(tuple(mesh.devices.shape), (2, 2, 2, 2))
    split = Mesh(mesh.devices.reshape(shape), ("z", "c", "x", "y"))
    grp, dom = ("z", "c"), ("x", "y")
    return jax.shard_map(
        on_device,
        mesh=split,
        in_specs=(
            P(dom, grp, None, None),
            P(dom, grp, None, None),
            P(dom, grp, None),
            P(dom, grp, None),
            P(dom, None, None),
            P(dom, None, None),
        ),
        out_specs=P(dom, grp, None, None),
        check_vma=False,
    )
```

time: 641 us -> 207 us (0.32)
  waiting for transfers between devices: 456 us -> 27.3 us
  matrix products: 50.5 us -> 4.06 us
  blocking collectives: 73.4 us -> 110 us
  Pallas kernels: 0 us -> 30.5 us
  local copies, waits for them, and re-layouts: 33.6 us -> 4.01 us
  starting transfers between devices: 0.21 us -> 14.3 us
  other arithmetic: 10.9 us -> 1.9 us
    all_gather x5 -> x2, waiting for transfers between devices: 332 us -> 0.01 us  [the longest x1 0.01 us: on_device(): run_maps = lax.all_gather(maps, 'y')]
    psum x1 -> x0, waiting for transfers between devices: 124 us -> none  [on_device(): summed_loads = lax.psum(scattered.astype(jnp.bfloat16), 'grp')]
    all_to_all x0 -> x6, blocking collectives: none -> 110 us  [the longest x1 26.1 us: on_device(): slices = lax.all_to_all(slices, GRP, 0, 0)]
    all_gather x4 -> x0, blocking collectives: 73.4 us -> none  [the longest x1 21.1 us: on_device(): lax.all_gather(west_values, 'grp', axis=0, tiled=True)]
    dot_general x40 -> x6, matrix products: 50.5 us -> 4.06 us  [the longest x1 2.95 us: on_device(): jnp.dot(rows_map, (spot == want).astype(BF16), preferred_element_type=F32)]
    pallas_call x0 -> x7, Pallas kernels: none -> 30.5 us  [call(): pl.pallas_call(kernel, name=name, out_shape=outs, in_specs=specs, out_spe...]
    all_to_all x0 -> x2, waiting for transfers between devices: none -> 22.1 us  [the longest x1 17.8 us: on_device(): lax.all_to_all(jnp.broadcast_to(loads, (nz, width, columns)), 'z', 0, 0)]
    another operation x1 -> x0, local copies, waits for them, and re-layouts: 16.8 us -> none  [on_device(): block_view = rows_map.reshape(blocks, stride, face_nodes, stride)]
  transfers between devices with their start and end apart: 6 -> 7, of which waited for: 6 -> 5; matrix products, arithmetic and copies ran while one was open for 4% -> 1% of each run, Pallas kernels for 0% -> 7%
where the time goes in v1:
time: 207 us; the launch traced here: 206 us
  blocking collectives  110 us (53%)
  Pallas kernels  30.5 us (15%)
  waiting for transfers between devices  27.3 us (13%)
  starting transfers between devices  14.3 us (7%)
  between operations  13.6 us (7%)
  matrix products  4.06 us (2%)
  local copies, waits for them, and re-layouts  4.01 us (2%)
    pallas_call x7, Pallas kernels, call(): pl.pallas_call(kernel, name=name, out_shape=outs, in_specs=specs, out_spe...  30.5 us
    all_to_all x1, blocking collectives, on_device(): slices = lax.all_to_all(slices, GRP, 0, 0)  26.1 us
    all_to_all x1, blocking collectives, on_device(): final_own = lax.all_to_all(final, 'z', 0, 0).reshape(half, columns)  20.4 us
    all_to_all x1, blocking collectives, on_device(): parts = lax.all_to_all(paired.reshape(nz, width, columns), 'z', 0, 0)  20.4 us
    all_to_all x1, waiting for transfers between devices, on_device(): lax.all_to_all(jnp.broadcast_to(loads, (nz, width, columns)), 'z', 0, 0)  17.8 us
    all_to_all x1, blocking collectives, on_device(): met = lax.all_to_all(met, GRP, 0, 0).reshape(columns, 2 * n)  15.1 us
    all_to_all x1, blocking collectives, on_device(): line = lax.all_to_all(line, 'y', 0, 0)  14.4 us
    all_to_all x1, blocking collectives, on_device(): faces = lax.all_to_all(faces, GRP, 0, 0)  13.5 us
  transfers between devices with their start and end apart: 7, of which 5 were waited for; matrix products, arithmetic and copies ran while one was open for 1% of the time, Pallas kernels for 7%

profile of v1, /device:TPU:1, one launch (start us, length us, event | category | flops | bytes accessed | tf_op | source)
XLA Modules:
  0.0 205.6 jit_solution(7242716535600736426)
XLA Ops:
  6.6 3.0 %fusion.9 = bf16[256,512]{0,1:T(8,128)(2,1)S(1)} fusion(s32[512]{0:T(512)S(1)} %get-tuple-element.26, s32[512]{0:T(512)S(1)} %get-tuple-element.25, pred[512]{0:T(512)(128)(4,1)S(1)} %iota_compare_fusion, bf16[1,256,4096]{2,1,0:T(8,128)(2,1)} %param.8), kind=kOutput, calls=%fused_computation.7 | convolution fusion | flops 1080164352 | bytes 2363904 | tf_op jit(solution)/shard_map/dot_general | solution.py:275
  9.8 0.2 fusion.13
  10.6 26.1 %all_to_all.40 = bf16[16,48,256]{2,1,0:T(8,128)(2,1)S(1)} all-to-all(bf16[16,48,256]{2,1,0:T(8,128)(2,1)S(1)} %broadcast_in_dim.13), channel_id=1, replica_groups=mesh['z'=8,'c'=2,'x'=4,'y'=8] {'z','c'}, dimensions={0} | all-to-all | bytes 786432 | tf_op jit(solution)/shard_map/all_to_all | solution.py:291
  36.7 0.8 copy.19
  37.5 0.6 fusion.32.pos
  38.2 4.5 %spread_rows.1 = (bf16[2048,128]{1,0:T(8,128)(2,1)}, bf16[2048,128]{1,0:T(8,128)(2,1)}) custom-call(s32[1024]{0:T(1024)} %fusion.32.pos, bf16[1024,1024]{1,0:T(8,128)(2,1)} %bitcast.72, bf16[1024,128]{1,0:T(8,128)(2,1)} %bitcast.83), custom_call_target="tpu_custom_call" | custom-call | flops 268435456 | bytes 6291456 | tf_op jit(solution)/shard_map/spread_rows/pallas_call | solution.py:23
  42.7 1.9 collective-permute-start
  44.6 2.1 %collective-permute-done = bf16[2048,128]{1,0:T(8,128)(2,1)S(1)} collective-permute-done((bf16[2048,128]{1,0:T(8,128)(2,1)}, bf16[2048,128]{1,0:T(8,128)(2,1)S(1)}, u32[]{:S(2)}, u32[]{:S(2)}) %collective-permute-start) | collective-permute-done | bytes 524320 | tf_op jit(solution)/shard_map/ppermute | solution.py:308
  46.7 1.2 add_convert_fusion
  47.9 20.4 %all_to_all.41 = bf16[8,256,128]{2,1,0:T(8,128)(2,1)S(1)} all-to-all(bf16[8,256,128]{2,1,0:T(8,128)(2,1)S(1)} %bitcast.74), channel_id=1, replica_groups=mesh['z'=8,'c'=2,'x'=4,'y'=8] {'z'}, dimensions={0} | all-to-all | bytes 1048576 | tf_op jit(solution)/shard_map/all_to_all | solution.py:310
  68.3 0.9 broadcast_in_dim.12
  69.2 3.5 %all-to-all-start.1 = ((bf16[8,256,128]{2,1,0:T(8,128)(2,1)}), bf16[8,256,128]{2,1,0:T(8,128)(2,1)S(1)}, u32[]{:S(2)}, u32[]{:S(2)}) async-start(bf16[8,256,128]{2,1,0:T(8,128)(2,1)} %broadcast_in_dim.12), calls=%async_computation.1 | async-start | bytes 1048576 | tf_op jit(solution)/shard_map/all_to_all | solution.py:312
  72.7 17.8 %all-to-all-done.1 = bf16[8,256,128]{2,1,0:T(8,128)(2,1)S(1)} async-done(((bf16[8,256,128]{2,1,0:T(8,128)(2,1)}), bf16[8,256,128]{2,1,0:T(8,128)(2,1)S(1)}, u32[]{:S(2)}, u32[]{:S(2)}) %all-to-all-start.1) | async-done | bytes 524320 | tf_op jit(solution)/shard_map/all_to_all | solution.py:312
  90.6 8.2 %block_maps.1 = (bf16[768,256]{1,0:T(8,128)(2,1)}, bf16[768,256]{1,0:T(8,128)(2,1)}) custom-call(s32[1]{0:T(128)} %bitcast.11.place, bf16[8,768,256]{2,1,0:T(8,128)(2,1)} %all-gather.4.cloned.1.call-done.maps_ref), custom_call_target="tpu_custom_call" | custom-call | flops 2147483648 | bytes 3145728 | tf_op jit(solution)/shard_map/block_maps/pallas_call | solution.py:23
  98.8 2.4 %collective-permute-start.1 = (bf16[2048,128]{1,0:T(8,128)(2,1)S(1)}, bf16[2048,128]{1,0:T(8,128)(2,1)S(1)}, u32[]{:S(2)}, u32[]{:S(2)}) collective-permute-start(bf16[2048,128]{1,0:T(8,128)(2,1)S(1)} %bitcast.76), channel_id=1, source_target_pairs={{0,32},{32,0},{1,33},{33,1},{2,34},{34,2},{3,35},{35,3},{4,36},{36... | collective-permute-start | bytes 1572872 | tf_op jit(solution)/shard_map/ppermute | solution.py:314
  101.2 1.5 collective-permute-done.1.other_ref
  102.7 0.8 copy-done.4
  103.5 3.3 %first_rows.1 = (f32[256,128]{1,0:T(8,128)}, bf16[16,32,128]{2,1,0:T(8,128)(2,1)}) custom-call(s32[1]{0:T(128)} %bitcast.1.core, bf16[256,4096]{1,0:T(8,128)(2,1)} %bitcast.75, bf16[2048,128]{1,0:T(8,128)(2,1)} %bitcast.77, bf16[2048,128]{1,0:T(8,128)(2,1)} %copy-done.4), custom_call_target="tpu_custom_call" | custom-call | flops 268435456 | bytes 2097152 | tf_op jit(solution)/shard_map/first_rows/pallas_call | solution.py:23
  106.8 13.5 %all_to_all.42.got_ref = bf16[16,32,128]{2,1,0:T(8,128)(2,1)} all-to-all(bf16[16,32,128]{2,1,0:T(8,128)(2,1)} %get-tuple-element.17), channel_id=1, replica_groups=mesh['z'=8,'c'=2,'x'=4,'y'=8] {'z','c'}, dimensions={0} | all-to-all | bytes 262144 | tf_op jit(solution)/shard_map/all_to_all | solution.py:331
  120.3 1.6 face_columns.1
  121.9 14.4 %all_to_all.43.faces_ref = bf16[8,8,512]{2,1,0:T(8,128)(2,1)} all-to-all(bf16[8,8,512]{2,1,0:T(8,128)(2,1)} %face_columns.1), channel_id=1, replica_groups=mesh['z'=8,'c'=2,'x'=4,'y'=8] {'y'}, dimensions={0} | all-to-all | bytes 131072 | tf_op jit(solution)/shard_map/all_to_all | solution.py:359
  136.3 5.1 %block_values.1 = (bf16[4,8,512]{2,1,0:T(8,128)(2,1)}, f32[8,512]{1,0:T(8,128)}) custom-call(s32[1]{0:T(128)} %bitcast.11.place, bf16[8,8,512]{2,1,0:T(8,128)(2,1)} %all_to_all.43.faces_ref, bf16[8,768,256]{2,1,0:T(8,128)(2,1)} %all-gather.4.cloned.1.call-done.maps_ref), custom_call_target="tpu_custom_call" | custom-call | flops 100663296 | bytes 3145728 | tf_op jit(solution)/shard_map/block_values/pallas_call | solution.py:23
  141.4 4.1 %all-to-all-start.5 = ((bf16[4,8,512]{2,1,0:T(8,128)(2,1)}), bf16[4,8,512]{2,1,0:T(8,128)(2,1)S(1)}, u32[]{:S(2)}, u32[]{:S(2)}) async-start(bf16[4,8,512]{2,1,0:T(8,128)(2,1)} %get-tuple-element.19), calls=%async_computation.5 | async-start | bytes 65536 | tf_op jit(solution)/shard_map/all_to_all | solution.py:374
  145.6 4.3 %all-to-all-done.5.ends_ref = bf16[4,8,512]{2,1,0:T(8,128)(2,1)S(1)} async-done(((bf16[4,8,512]{2,1,0:T(8,128)(2,1)}), bf16[4,8,512]{2,1,0:T(8,128)(2,1)S(1)}, u32[]{:S(2)}, u32[]{:S(2)}) %all-to-all-start.5) | async-done | bytes 32800 | tf_op jit(solution)/shard_map/all_to_all | solution.py:374
  149.9 0.6 copy-done.6
  150.5 3.3 %meet_values.1 = bf16[16,8,512]{2,1,0:T(8,128)(2,1)} custom-call(s32[1]{0:T(128)} %bitcast.10.place, bf16[4,8,512]{2,1,0:T(8,128)(2,1)} %copy-done.6, bf16[4,768,256]{2,1,0:T(8,128)(2,1)} %bitcast.80, bf16[768,256]{1,0:T(8,128)(2,1)} %get-tuple-element.21.maps_ref, f32[8,512]{1,0:T(8,128)} %get-tuple-element.22.own_ref), custom_call_target="tpu_custom_call" | custom-call | flops 50331648 | bytes 1572864 | tf_op jit(solution)/shard_map/meet_values/pallas_call | solution.py:23
  153.8 15.1 %all_to_all.44 = bf16[16,8,512]{2,1,0:T(8,128)(2,1)S(1)} all-to-all(bf16[16,8,512]{2,1,0:T(8,128)(2,1)} %meet_values.1), channel_id=1, replica_groups=mesh['z'=8,'c'=2,'x'=4,'y'=8] {'z','c'}, dimensions={0} | all-to-all | bytes 262144 | tf_op jit(solution)/shard_map/all_to_all | solution.py:388
  169.2 20.4 %all_to_all.45 = bf16[8,256,128]{2,1,0:T(8,128)(2,1)S(1)} all-to-all(bf16[8,256,128]{2,1,0:T(8,128)(2,1)S(1)} %broadcast_in_dim.14), channel_id=1, replica_groups=mesh['z'=8,'c'=2,'x'=4,'y'=8] {'z'}, dimensions={0} | all-to-all | bytes 1048576 | tf_op jit(solution)/shard_map/all_to_all | solution.py:392
  189.6 2.3 %collective-permute-start.2 = (bf16[2048,128]{1,0:T(8,128)(2,1)S(1)}, bf16[2048,128]{1,0:T(8,128)(2,1)S(1)}, u32[]{:S(2)}, u32[]{:S(2)}) collective-permute-start(bf16[2048,128]{1,0:T(8,128)(2,1)S(1)} %bitcast.78), channel_id=1, source_target_pairs={{0,32},{32,0},{1,33},{33,1},{2,34},{34,2},{3,35},{35,3},{4,36},{36... | collective-permute-start | bytes 1572872 | tf_op jit(solution)/shard_map/ppermute | solution.py:393
  191.9 1.5 collective-permute-done.2.other_ref
  193.5 0.8 copy-done.5
  194.3 4.5 %leaf_result.1 = bf16[1024,128]{1,0:T(8,128)(2,1)} custom-call(s32[1024]{0:T(1024)} %fusion.32.pos, bf16[2048,128]{1,0:T(8,128)(2,1)} %bitcast.79, bf16[2048,128]{1,0:T(8,128)(2,1)} %copy-done.5, bf16[1024,1024]{1,0:T(8,128)(2,1)} %bitcast.73, bf16[1024,128]{1,0:T(8,128)(2,1)} %bitcast.84), custom_call_target="tpu_custom_call" | custom-call | flops 268435456 | bytes 2097152 | tf_op jit(solution)/shard_map/leaf_result/pallas_call | solution.py:23
  (37 shorter events, 1.3 us)
Async XLA Ops:
  6.5 84.0 %all-gather.4.cloned.1.call-start = ((), (), s32[]{:S(2)}) async-start(), calls=%async_computation.8 | async-start | bytes 3538944 | tf_op jit(solution)/shard_map/all_gather | solution.py:293
  6.5 3.0 %copy-start.2 = (f32[1,256,256]{2,1,0:T(8,128)S(1)}, f32[1,256,256]{2,1,0:T(8,128)}, u32[]{:S(2)}) copy-start(f32[1,256,256]{2,1,0:T(8,128)} %param.11) | copy-start | bytes 786436
  6.6 3.4 %copy-start.3 = (f32[1,256,256]{2,1,0:T(8,128)S(1)}, f32[1,256,256]{2,1,0:T(8,128)}, u32[]{:S(2)}) copy-start(f32[1,256,256]{2,1,0:T(8,128)} %param.10) | copy-start | bytes 786436
  10.0 27.5 %copy-start.8 = (s32[1,1,1024]{2,1,0:T(1,128)S(1)}, s32[1,1,1024]{2,1,0:T(1,128)}, u32[]{:S(2)}) copy-start(s32[1,1,1024]{2,1,0:T(1,128)} %param.9) | copy-start | bytes 12292
  42.7 4.0 %collective-permute-start = (bf16[2048,128]{1,0:T(8,128)(2,1)}, bf16[2048,128]{1,0:T(8,128)(2,1)S(1)}, u32[]{:S(2)}, u32[]{:S(2)}) collective-permute-start(bf16[2048,128]{1,0:T(8,128)(2,1)} %get-tuple-element.15), channel_id=1, source_target_pairs={{0,32},{32,0},{1,33},{33,1},{2,34},{34,2},{3,35},{35,3},{4,36},{36... | collective-permute-start | bytes 1572872 | tf_op jit(solution)/shard_map/ppermute | solution.py:308
  69.2 21.4 %all-to-all-start.1 = ((bf16[8,256,128]{2,1,0:T(8,128)(2,1)}), bf16[8,256,128]{2,1,0:T(8,128)(2,1)S(1)}, u32[]{:S(2)}, u32[]{:S(2)}) async-start(bf16[8,256,128]{2,1,0:T(8,128)(2,1)} %broadcast_in_dim.12), calls=%async_computation.1 | async-start | bytes 1048576 | tf_op jit(solution)/shard_map/all_to_all | solution.py:312
  72.7 77.2 %all-gather.6.cloned.1.call-start = ((), (), s32[]{:S(2)}) async-start(), calls=%async_computation.9 | async-start | bytes 1966080 | tf_op jit(solution)/shard_map/all_gather | solution.py:348
  90.5 8.2 %copy-start = (bf16[8,256,128]{2,1,0:T(8,128)(2,1)}, bf16[8,256,128]{2,1,0:T(8,128)(2,1)S(1)}, u32[]{:S(2)}) copy-start(bf16[8,256,128]{2,1,0:T(8,128)(2,1)S(1)} %all-to-all-done.1) | copy-start | bytes 1572868
  98.8 3.9 %collective-permute-start.1 = (bf16[2048,128]{1,0:T(8,128)(2,1)S(1)}, bf16[2048,128]{1,0:T(8,128)(2,1)S(1)}, u32[]{:S(2)}, u32[]{:S(2)}) collective-permute-start(bf16[2048,128]{1,0:T(8,128)(2,1)S(1)} %bitcast.76), channel_id=1, source_target_pairs={{0,32},{32,0},{1,33},{33,1},{2,34},{34,2},{3,35},{35,3},{4,36},{36... | collective-permute-start | bytes 1572872 | tf_op jit(solution)/shard_map/ppermute | solution.py:314
  102.7 0.8 copy-start.4
  141.4 27.6 %copy-start.7 = (f32[256,128]{1,0:T(8,128)S(1)}, f32[256,128]{1,0:T(8,128)}, u32[]{:S(2)}) copy-start(f32[256,128]{1,0:T(8,128)} %get-tuple-element.16) | copy-start | bytes 393220
  141.4 8.4 %all-to-all-start.5 = ((bf16[4,8,512]{2,1,0:T(8,128)(2,1)}), bf16[4,8,512]{2,1,0:T(8,128)(2,1)S(1)}, u32[]{:S(2)}, u32[]{:S(2)}) async-start(bf16[4,8,512]{2,1,0:T(8,128)(2,1)} %get-tuple-element.19), calls=%async_computation.5 | async-start | bytes 65536 | tf_op jit(solution)/shard_map/all_to_all | solution.py:374
  149.9 0.6 copy-start.6
  189.6 3.9 %copy-start.1 = (bf16[8,256,128]{2,1,0:T(8,128)(2,1)}, bf16[8,256,128]{2,1,0:T(8,128)(2,1)S(1)}, u32[]{:S(2)}) copy-start(bf16[8,256,128]{2,1,0:T(8,128)(2,1)S(1)} %all_to_all.45) | copy-start | bytes 1572868
  189.6 3.9 %collective-permute-start.2 = (bf16[2048,128]{1,0:T(8,128)(2,1)S(1)}, bf16[2048,128]{1,0:T(8,128)(2,1)S(1)}, u32[]{:S(2)}, u32[]{:S(2)}) collective-permute-start(bf16[2048,128]{1,0:T(8,128)(2,1)S(1)} %bitcast.78), channel_id=1, source_target_pairs={{0,32},{32,0},{1,33},{33,1},{2,34},{34,2},{3,35},{35,3},{4,36},{36... | collective-permute-start | bytes 1572872 | tf_op jit(solution)/shard_map/ppermute | solution.py:393
  193.5 0.8 copy-start.5
Sparse Core Ops, SparseCore 0:
  37.7 43.0 all-gather.3
  98.9 27.6 all-gather.5

commit v2 on v1

--- a/solution.py
+++ b/solution.py
@@ -8,21 +8,21 @@
 from jax.sharding import Mesh
 from jax.sharding import PartitionSpec as P
 
+
 F32 = jnp.float32
 BF16 = jnp.bfloat16
 GRP = ("z", "c")
 NT = (((1,), (1,)), ((), ()))
 VM = pl.BlockSpec(memory_space=pltpu.VMEM)
 SM = pl.BlockSpec(memory_space=pltpu.SMEM)
-PARAMS = pltpu.CompilerParams(vmem_limit_bytes=56 * 1024 * 1024)
-
-
-def call(kernel, name, outs, scratch, smem, cost, *args):
+PARAMS = pltpu.CompilerParams(vmem_limit_bytes=16 * 1024 * 1024)
+
+
+def call(kernel, outs, scratch, smem, cost, *args):
     specs = [SM] * smem + [VM] * (len(args) - smem)
     flops, moved = cost
     return pl.pallas_call(
         kernel,
-        name=name,
         out_shape=outs,
         in_specs=specs,
         out_specs=jax.tree.map(lambda _: VM, outs),
@@ -32,6 +32,10 @@
     )(*args)
 
 
+def moved(value, axis):
+    return lax.all_to_all(value, axis, 0, 0)
+
+
 def spread_rows(pos, map_ref, load_ref, keep_ref, send_ref, contrib, rows):
     contrib[...] = (
         jnp.dot(map_ref[...], load_ref[...], preferred_element_type=F32).astype(BF16).astype(F32)
@@ -52,38 +56,46 @@
     send_ref[...] = rows[half:].astype(BF16)
 
 
-def first_rows(core, map_ref, own_ref, other_ref, initial_ref, faces_ref, acc, *, width, stride):
+def face_parts(parts_ref, rows_ref, loads_ref, out_ref, order):
+    total = parts_ref[0].astype(F32)
+    for z in range(1, parts_ref.shape[0]):
+        total = total + parts_ref[z].astype(F32)
+    loads = total.astype(BF16)
+    for z in range(loads_ref.shape[0]):
+        loads_ref[z] = loads
+    peers, both, _ = rows_ref.shape
+    nodes = both // 2
+    for g in range(peers):
+        order[g * nodes : (g + 1) * nodes] = rows_ref[g, 0:nodes]
+        order[(peers + g) * nodes : (peers + g + 1) * nodes] = rows_ref[g, nodes:both]
+    lines = lax.dot_general(total.T.astype(BF16), order[...], NT, preferred_element_type=F32)
+    part = out_ref.shape[1]
+    for g in range(peers):
+        out_ref[g] = lines[g * part : (g + 1) * part].astype(BF16)
+
+
+def face_sum(got_ref, out_ref):
+    total = got_ref[0].astype(F32)
+    for g in range(1, got_ref.shape[0]):
+        total = total + got_ref[g].astype(F32)
+    line = total.astype(BF16)
+    for y in range(out_ref.shape[0]):
+        out_ref[y] = line
+
+
+def first_rows(core, map_ref, own_ref, other_ref, initial_ref, *, width):
     side = core[0]
     pairs = own_ref.shape[0] // width
-    acc[...] = jnp.zeros_like(acc)
+    total = None
     for z in range(pairs):
         mine = pl.ds(pl.multiple_of((2 * z + side) * width, width), width)
         theirs = pl.ds(pl.multiple_of((2 * z + 1 - side) * width, width), width)
         block = slice(z * width, (z + 1) * width)
-        acc[...] += jnp.dot(map_ref[:, mine], own_ref[block], preferred_element_type=F32)
-        acc[...] += jnp.dot(map_ref[:, theirs], other_ref[block], preferred_element_type=F32)
-    initial_ref[...] = acc[...]
-    nodes = acc.shape[0] // stride
-    west = acc[pl.ds(0, nodes, stride=stride), :]
-    east = acc[pl.ds(1, nodes, stride=stride), :]
-    both = jnp.concatenate([east, west], axis=0)
-    lanes = both.shape[1]
-    peers = faces_ref.shape[0]
-    part = lanes // peers
-    for g in range(peers):
-        turned = both if g == 0 else pltpu.roll(both, lanes - part * g, axis=1)
-        faces_ref[g] = turned.astype(BF16)
-
-
-def face_columns(got_ref, out_ref, order, *, nodes, part):
-    peers = got_ref.shape[0]
-    for g in range(peers):
-        both = got_ref[g].astype(F32)
-        order[pl.ds(g * nodes, nodes), :] = both[:nodes]
-        order[pl.ds((peers + g) * nodes, nodes), :] = both[nodes:]
-    line = order[...].T[:part].astype(BF16)
-    for y in range(out_ref.shape[0]):
-        out_ref[y] = line
+        both = jnp.dot(map_ref[:, mine], own_ref[block], preferred_element_type=F32) + jnp.dot(
+            map_ref[:, theirs], other_ref[block], preferred_element_type=F32
+        )
+        total = both if total is None else total + both
+    initial_ref[...] = total
 
 
 def halves(value):
@@ -290,13 +302,15 @@
     slices = jnp.broadcast_to(slices, (peers,) + slices.shape)
     slices = lax.all_to_all(slices, GRP, 0, 0)
     maps = slices.reshape(peers, 3, nodes, n).transpose(1, 0, 2, 3).reshape(3 * n, n)
-    run_maps = lax.all_gather(maps, "y")
+    rows = rows_map.reshape(nodes, stride, interface)
+    rows = jnp.concatenate([rows[:, 1], rows[:, 0]], axis=0)
+    face_rows = rows.reshape(2 * nodes, peers, width).transpose(1, 0, 2)
+    face_rows = lax.all_to_all(face_rows, GRP, 0, 0)
 
     owner = nodes_of // width
     pos = ((owner % nc) ^ side) * half + (owner // nc) * width + nodes_of % width
     keep, send = call(
         spread_rows,
-        "spread_rows",
         (jax.ShapeDtypeStruct((half, columns), BF16),) * 2,
         [pltpu.VMEM((leaf_nodes, columns), F32), pltpu.VMEM((interface, columns), F32)],
         1,
@@ -305,35 +319,35 @@
         local_map,
         local_load,
     )
+    maps, send = lax.optimization_barrier((maps, send))
+    run_maps = lax.all_gather(maps, "y")
     got = lax.ppermute(send, "c", swap)
     paired = (keep.astype(F32) + got.astype(F32)).astype(BF16)
     parts = lax.all_to_all(paired.reshape(nz, width, columns), "z", 0, 0)
-    loads = jnp.sum(parts.astype(F32), axis=0).astype(BF16)
-    loads = lax.all_to_all(jnp.broadcast_to(loads, (nz, width, columns)), "z", 0, 0)
-    loads_own = loads.reshape(half, columns)
-    loads_other = lax.ppermute(loads_own, "c", swap)
-
-    initial, faces = call(
-        functools.partial(first_rows, width=width, stride=stride),
-        "first_rows",
+    loads, faces = call(
+        face_parts,
         (
-            jax.ShapeDtypeStruct((width, columns), F32),
-            jax.ShapeDtypeStruct((peers, 2 * nodes, columns), BF16),
+            jax.ShapeDtypeStruct((nz, width, columns), BF16),
+            jax.ShapeDtypeStruct((peers, part, 2 * n), BF16),
         ),
-        [pltpu.VMEM((width, columns), F32)],
-        1,
-        (2 * width * interface * columns, 2 * width * interface),
-        core,
-        rows_map,
-        loads_own,
-        loads_other,
+        [pltpu.VMEM((2 * n, width), BF16)],
+        0,
+        (4 * n * width * columns, 4 * n * width),
+        parts,
+        face_rows,
     )
     faces = lax.all_to_all(faces, GRP, 0, 0)
-
-    run_maps, loads_own = lax.optimization_barrier((run_maps, loads_own))
+    line = call(
+        face_sum,
+        jax.ShapeDtypeStruct((ny, part, 2 * n), BF16),
+        [],
+        0,
+        (1000, 4 * n * columns),
+        faces,
+    )
+
     joined, own_maps = call(
         block_maps,
-        "block_maps",
         (jax.ShapeDtypeStruct((3 * n, n), BF16), jax.ShapeDtypeStruct((3 * n, n), BF16)),
         [
             pltpu.VMEM((n, n), F32),
@@ -347,19 +361,9 @@
     )
     all_joined = lax.all_gather(joined, "x")
 
-    line = call(
-        functools.partial(face_columns, nodes=nodes, part=part),
-        "face_columns",
-        jax.ShapeDtypeStruct((ny, part, 2 * n), BF16),
-        [pltpu.VMEM((2 * n, columns), F32)],
-        0,
-        (1000, 4 * n * columns),
-        faces,
-    )
-    line = lax.all_to_all(line, "y", 0, 0)
+    line = moved(line, "y")
     ends, own_values = call(
         block_values,
-        "block_values",
         (
             jax.ShapeDtypeStruct((nx, part, 2 * n), BF16),
             jax.ShapeDtypeStruct((part, 2 * n), F32),
@@ -371,10 +375,23 @@
         line,
         run_maps,
     )
-    ends = lax.all_to_all(ends, "x", 0, 0)
+    ends = moved(ends, "x")
+    loads, ends = lax.optimization_barrier((loads, ends))
+    loads_own = moved(loads, "z").reshape(half, columns)
+    loads_other = lax.ppermute(loads_own, "c", swap)
+    initial = call(
+        functools.partial(first_rows, width=width),
+        jax.ShapeDtypeStruct((width, columns), F32),
+        [],
+        1,
+        (2 * width * interface * columns, 2 * width * interface),
+        core,
+        rows_map,
+        loads_own,
+        loads_other,
+    )
     met = call(
         meet_values,
-        "meet_values",
         jax.ShapeDtypeStruct((peers, part, 2 * n), BF16),
         [pltpu.VMEM((part, 2 * n), F32)],
         1,
@@ -393,7 +410,6 @@
     final_other = lax.ppermute(final_own, "c", swap)
     result = call(
         leaf_result,
-        "leaf_result",
         jax.ShapeDtypeStruct((leaf_nodes, columns), BF16),
         [pltpu.VMEM((interface, columns), F32), pltpu.VMEM((leaf_nodes, columns), F32)],
         1,

time: 207 us -> 210 us (1.014)
  blocking collectives: 110 us -> 73.2 us
  waiting for transfers between devices: 27.3 us -> 47.9 us
  starting transfers between devices: 14.3 us -> 34.3 us
  Pallas kernels: 30.5 us -> 18.1 us
  local copies, waits for them, and re-layouts: 4.01 us -> 14.2 us
    all_to_all x4 -> x3, blocking collectives: 75.9 us -> 35.1 us  [moved(): return lax.all_to_all(value, axis, 0, 0)]
    all_gather x1, waiting for transfers between devices: 0.01 us -> 18.7 us  [on_device(): run_maps = lax.all_gather(maps, 'y')]
    all_to_all x2 -> x4, starting transfers between devices: 7.63 us -> 23.2 us  [the longest x1 11.8 us: on_device(): slices = lax.all_to_all(slices, GRP, 0, 0)]
    pallas_call x7 -> x8, Pallas kernels: 30.5 us -> 18.1 us  [call(): pl.pallas_call(kernel, out_shape=outs, in_specs=specs, out_specs=jax.tree...]
    unnamed x21 -> x29, local copies, waits for them, and re-layouts: 2.24 us -> 9.83 us
    all_to_all x2 -> x4, waiting for transfers between devices: 22.1 us -> 27.6 us  [the longest x1 11 us: on_device(): slices = lax.all_to_all(slices, GRP, 0, 0)]
    ppermute x1, starting transfers between devices: 2.4 us -> 6.77 us  [on_device(): loads_other = lax.ppermute(loads_own, 'c', swap)]
    all_to_all x1, blocking collectives: 13.5 us -> 17.7 us  [on_device(): faces = lax.all_to_all(faces, GRP, 0, 0)]
  transfers between devices with their start and end apart: 7 -> 9, of which waited for: 5 -> 5; matrix products, arithmetic and copies ran while one was open for 1% -> 3% of each run, Pallas kernels for 7% -> 7%
where the time goes in v2:
time: 210 us; the launch traced here: 209 us
  blocking collectives  73.2 us (35%)
  waiting for transfers between devices  47.9 us (23%)
  starting transfers between devices  34.3 us (16%)
  Pallas kernels  18.1 us (9%)
  local copies, waits for them, and re-layouts  14.2 us (7%)
  between operations  13.7 us (7%)
  matrix products  5.09 us (2%)
  other arithmetic  2.77 us (1%)
    all_to_all x3, blocking collectives, moved(): return lax.all_to_all(value, axis, 0, 0)  35.1 us
    all_to_all x1, blocking collectives, on_device(): final_own = lax.all_to_all(final, 'z', 0, 0).reshape(half, columns)  20.4 us
    all_gather x1, waiting for transfers between devices, on_device(): run_maps = lax.all_gather(maps, 'y')  18.7 us
    pallas_call x8, Pallas kernels, call(): pl.pallas_call(kernel, out_shape=outs, in_specs=specs, out_specs=jax.tree...  18.1 us
    all_to_all x1, blocking collectives, on_device(): faces = lax.all_to_all(faces, GRP, 0, 0)  17.7 us
    all_to_all x1, starting transfers between devices, on_device(): slices = lax.all_to_all(slices, GRP, 0, 0)  11.8 us
    all_to_all x1, waiting for transfers between devices, on_device(): slices = lax.all_to_all(slices, GRP, 0, 0)  11 us
    unnamed x29, local copies, waits for them, and re-layouts  9.83 us
  transfers between devices with their start and end apart: 9, of which 5 were waited for; matrix products, arithmetic and copies ran while one was open for 3% of the time, Pallas kernels for 7%

profile of v2, /device:TPU:1, one launch (start us, length us, event | category | flops | bytes accessed | tf_op | source)
XLA Modules:
  0.0 209.3 jit_solution(3773999833994398692)
XLA Ops:
  6.6 3.0 %fusion.9 = bf16[256,512]{0,1:T(8,128)(2,1)S(1)} fusion(s32[512]{0:T(512)S(1)} %get-tuple-element.34, s32[512]{0:T(512)S(1)} %get-tuple-element.33, pred[512]{0:T(512)(128)(4,1)S(1)} %iota_compare_fusion, bf16[1,256,4096]{2,1,0:T(8,128)(2,1)} %param.8), kind=kOutput, calls=%fused_computation.7 | convolution fusion | flops 1080164352 | bytes 2363904 | tf_op jit(solution)/shard_map/dot_general | solution.py:287
  12.7 11.8 %all-to-all-start = ((bf16[16,48,256]{2,1,0:T(8,128)(2,1)}), bf16[16,48,256]{2,1,0:T(8,128)(2,1)S(1)}, u32[]{:S(2)}, u32[]{:S(2)}) async-start(bf16[16,48,256]{2,1,0:T(8,128)(2,1)} %broadcast_in_dim.9), calls=%async_computation | async-start | bytes 786432 | tf_op jit(solution)/shard_map/all_to_all | solution.py:303
  24.6 3.3 %shard_map.64 = (bf16[2048,128]{1,0:T(8,128)(2,1)S(1)}, bf16[2048,128]{1,0:T(8,128)(2,1)}) custom-call(s32[1024]{0:T(1024)S(1)} %fusion.32.pos, bf16[1024,1024]{1,0:T(8,128)(2,1)S(1)} %bitcast.82, bf16[1024,128]{1,0:T(8,128)(2,1)S(1)} %bitcast.93), custom_call_target="tpu_custom_call" | custom-call | flops 268435456 | bytes 6291456 | tf_op jit(solution)/shard_map/pallas_call | solution.py:24
  27.9 11.0 %all-to-all-done = bf16[16,48,256]{2,1,0:T(8,128)(2,1)S(1)} async-done(((bf16[16,48,256]{2,1,0:T(8,128)(2,1)}), bf16[16,48,256]{2,1,0:T(8,128)(2,1)S(1)}, u32[]{:S(2)}, u32[]{:S(2)}) %all-to-all-start) | async-done | bytes 393248 | tf_op jit(solution)/shard_map/all_to_all | solution.py:303
  39.0 0.8 copy.19
  39.8 1.9 collective-permute-start
  41.7 2.7 %slice_reduce_fusion.1 = (bf16[16,4096]{1,0:T(8,128)(2,1)S(1)}, bf16[16,4096]{1,0:T(8,128)(2,1)S(1)}) fusion(bf16[16,16,4096]{2,1,0:T(8,128)(2,1)} %bitcast.84), kind=kLoop, calls=%fused_computation.14 | loop fusion | bytes 524288 | tf_op jit(solution)/shard_map/slice | solution.py:306
  45.2 3.8 %all-to-all-start.2 = ((bf16[16,32,256]{2,1,0:T(8,128)(2,1)}), bf16[16,32,256]{2,1,0:T(8,128)(2,1)S(1)}, u32[]{:S(2)}, u32[]{:S(2)}) async-start(bf16[16,32,256]{2,1,0:T(8,128)(2,1)} %maximum_bitcast_fusion), calls=%async_computation.2 | async-start | bytes 524288 | tf_op jit(solution)/shard_map/all_to_all | solution.py:308
  49.0 2.0 add_convert_fusion
  51.0 9.8 %all-to-all-done.2.rows_ref = bf16[16,32,256]{2,1,0:T(8,128)(2,1)S(1)} async-done(((bf16[16,32,256]{2,1,0:T(8,128)(2,1)}), bf16[16,32,256]{2,1,0:T(8,128)(2,1)S(1)}, u32[]{:S(2)}, u32[]{:S(2)}) %all-to-all-start.2) | async-done | bytes 262176 | tf_op jit(solution)/shard_map/all_to_all | solution.py:308
  60.7 3.5 %all-to-all-start.1 = ((bf16[8,256,128]{2,1,0:T(8,128)(2,1)}), bf16[8,256,128]{2,1,0:T(8,128)(2,1)S(1)}, u32[]{:S(2)}, u32[]{:S(2)}) async-start(bf16[8,256,128]{2,1,0:T(8,128)(2,1)} %bitcast.95), calls=%async_computation.1 | async-start | bytes 1048576 | tf_op jit(solution)/shard_map/all_to_all | solution.py:326
  64.3 18.7 %all-gather.5.cloned.1.call-done = bf16[6144,256]{1,0:T(8,128)(2,1)} async-done(((bf16[768,256]{1,0:T(8,128)(2,1)}), bf16[6144,256]{1,0:T(8,128)(2,1)}) %all-gather.5.cloned.1.call-update) | async-done | bytes 3145744 | tf_op jit(solution)/shard_map/all_gather | solution.py:323
  83.0 1.9 copy-done.2
  84.9 6.2 %shard_map.69 = (bf16[768,256]{1,0:T(8,128)(2,1)}, bf16[768,256]{1,0:T(8,128)(2,1)S(1)}) custom-call(s32[1]{0:T(128)} %bitcast.19.place, bf16[8,768,256]{2,1,0:T(8,128)(2,1)S(1)} %bitcast.86), custom_call_target="tpu_custom_call" | custom-call | flops 2147483648 | bytes 3145728 | tf_op jit(solution)/shard_map/pallas_call | solution.py:24
  92.2 17.7 %all_to_all.45.got_ref = bf16[16,8,512]{2,1,0:T(8,128)(2,1)S(1)} all-to-all(bf16[16,8,512]{2,1,0:T(8,128)(2,1)S(1)} %get-tuple-element.21), channel_id=1, replica_groups=mesh['z'=8,'c'=2,'x'=4,'y'=8] {'z','c'}, dimensions={0} | all-to-all | bytes 262144 | tf_op jit(solution)/shard_map/all_to_all | solution.py:339
  109.9 11.0 %all_to_all.46.faces_ref = bf16[8,8,512]{2,1,0:T(8,128)(2,1)S(1)} all-to-all(bf16[8,8,512]{2,1,0:T(8,128)(2,1)S(1)} %shard_map.66), channel_id=1, replica_groups=mesh['z'=8,'c'=2,'x'=4,'y'=8] {'y'}, dimensions={0} | all-to-all | bytes 131072 | tf_op jit(solution)/shard_map/all_to_all | solution.py:36
  121.0 1.9 copy-done.3
  122.9 2.6 %shard_map.67 = (bf16[4,8,512]{2,1,0:T(8,128)(2,1)S(1)}, f32[8,512]{1,0:T(8,128)S(1)}) custom-call(s32[1]{0:T(128)} %bitcast.19.place, bf16[8,8,512]{2,1,0:T(8,128)(2,1)S(1)} %all_to_all.46.faces_ref, bf16[8,768,256]{2,1,0:T(8,128)(2,1)S(1)} %bitcast.87), custom_call_target="tpu_custom_call" | custom-call | flops 100663296 | bytes 3145728 | tf_op jit(solution)/shard_map/pallas_call | solution.py:24
  125.4 8.1 %all_to_all.47.ends_ref = bf16[4,8,512]{2,1,0:T(8,128)(2,1)S(1)} all-to-all(bf16[4,8,512]{2,1,0:T(8,128)(2,1)S(1)} %get-tuple-element.23), channel_id=1, replica_groups=mesh['z'=8,'c'=2,'x'=4,'y'=8] {'x'}, dimensions={0} | all-to-all | bytes 65536 | tf_op jit(solution)/shard_map/all_to_all | solution.py:36
  133.5 16.0 %all_to_all.48 = bf16[8,256,128]{2,1,0:T(8,128)(2,1)S(1)} all-to-all(bf16[8,256,128]{2,1,0:T(8,128)(2,1)S(1)} %get-tuple-element.24), channel_id=1, replica_groups=mesh['z'=8,'c'=2,'x'=4,'y'=8] {'z'}, dimensions={0} | all-to-all | bytes 1048576 | tf_op jit(solution)/shard_map/all_to_all | solution.py:36
  149.5 6.8 %collective-permute-start.1 = (bf16[2048,128]{1,0:T(8,128)(2,1)S(1)}, bf16[2048,128]{1,0:T(8,128)(2,1)S(1)}, u32[]{:S(2)}, u32[]{:S(2)}) collective-permute-start(bf16[2048,128]{1,0:T(8,128)(2,1)S(1)} %bitcast.88), channel_id=1, source_target_pairs={{0,32},{32,0},{1,33},{33,1},{2,34},{34,2},{3,35},{35,3},{4,36},{36... | collective-permute-start | bytes 1572872 | tf_op jit(solution)/shard_map/ppermute | solution.py:381
  156.3 1.4 copy-done.4
  157.7 1.0 copy-done.7
  158.7 1.8 shard_map.70
  160.5 4.1 %all-to-all-start.7 = ((bf16[16,8,512]{2,1,0:T(8,128)(2,1)}), bf16[16,8,512]{2,1,0:T(8,128)(2,1)}, u32[]{:S(2)}, u32[]{:S(2)}) async-start(bf16[16,8,512]{2,1,0:T(8,128)(2,1)} %shard_map.70), calls=%async_computation.7 | async-start | bytes 262144 | tf_op jit(solution)/shard_map/all_to_all | solution.py:405
  164.6 1.6 copy-done.1
  166.9 6.8 %all-to-all-done.7 = bf16[16,8,512]{2,1,0:T(8,128)(2,1)} async-done(((bf16[16,8,512]{2,1,0:T(8,128)(2,1)}), bf16[16,8,512]{2,1,0:T(8,128)(2,1)}, u32[]{:S(2)}, u32[]{:S(2)}) %all-to-all-start.7) | async-done | bytes 131104 | tf_op jit(solution)/shard_map/all_to_all | solution.py:405
  173.7 1.2 fusion.14
  175.1 20.4 %all_to_all.49 = bf16[8,256,128]{2,1,0:T(8,128)(2,1)S(1)} all-to-all(bf16[8,256,128]{2,1,0:T(8,128)(2,1)S(1)} %broadcast_in_dim.10), channel_id=1, replica_groups=mesh['z'=8,'c'=2,'x'=4,'y'=8] {'z'}, dimensions={0} | all-to-all | bytes 1048576 | tf_op jit(solution)/shard_map/all_to_all | solution.py:409
  195.5 2.3 %collective-permute-start.2 = (bf16[2048,128]{1,0:T(8,128)(2,1)S(1)}, bf16[2048,128]{1,0:T(8,128)(2,1)S(1)}, u32[]{:S(2)}, u32[]{:S(2)}) collective-permute-start(bf16[2048,128]{1,0:T(8,128)(2,1)S(1)} %bitcast.90), channel_id=1, source_target_pairs={{0,32},{32,0},{1,33},{33,1},{2,34},{34,2},{3,35},{35,3},{4,36},{36... | collective-permute-start | bytes 1572872 | tf_op jit(solution)/shard_map/ppermute | solution.py:410
  197.8 1.5 collective-permute-done.2.other_ref
  199.4 3.1 %shard_map.71 = bf16[1024,128]{1,0:T(8,128)(2,1)} custom-call(s32[1024]{0:T(1024)S(1)} %fusion.32.pos, bf16[2048,128]{1,0:T(8,128)(2,1)S(1)} %bitcast.91, bf16[2048,128]{1,0:T(8,128)(2,1)S(1)} %collective-permute-done.2.other_ref, bf16[1024,1024]{1,0:T(8,128)(2,1)S(1)} %bitcast.83, bf16[1024,128]{1,0:T(8,128)(2,1)S(1)} %bitcast.94), custom_call_target="tpu_custom_call" | custom-call | flops 268435456 | bytes 2097152 | tf_op jit(solution)/shard_map/pallas_call | solution.py:24
  (50 shorter events, 5.8 us)
Async XLA Ops:
  6.5 3.0 %copy-start.8 = (f32[1,256,256]{2,1,0:T(8,128)S(1)}, f32[1,256,256]{2,1,0:T(8,128)}, u32[]{:S(2)}) copy-start(f32[1,256,256]{2,1,0:T(8,128)} %param.11) | copy-start | bytes 786436
  6.5 4.1 %copy-start.9 = (f32[1,256,256]{2,1,0:T(8,128)S(1)}, f32[1,256,256]{2,1,0:T(8,128)}, u32[]{:S(2)}) copy-start(f32[1,256,256]{2,1,0:T(8,128)} %param.10) | copy-start | bytes 786436
  9.5 15.0 %copy-start.12 = (s32[1,1,1024]{2,1,0:T(1,128)S(1)}, s32[1,1,1024]{2,1,0:T(1,128)}, u32[]{:S(2)}) copy-start(s32[1,1,1024]{2,1,0:T(1,128)} %param.9) | copy-start | bytes 12292
  9.5 15.0 %copy-start = (bf16[1,1,1024,1024]{3,2,1,0:T(8,128)(2,1)S(1)}, bf16[1,1,1024,1024]{3,2,1,0:T(8,128)(2,1)}, u32[]{:S(2)}) copy-start(bf16[1,1,1024,1024]{3,2,1,0:T(8,128)(2,1)} %param.7) | copy-start | bytes 6291460
  9.6 15.0 %copy-start.5 = (bf16[1,1,1024,128]{3,2,1,0:T(8,128)(2,1)S(1)}, bf16[1,1,1024,128]{3,2,1,0:T(8,128)(2,1)}, u32[]{:S(2)}) copy-start(bf16[1,1,1024,128]{3,2,1,0:T(8,128)(2,1)} %param.6) | copy-start | bytes 786436
  10.0 0.7 copy-start.11
  11.1 0.7 copy-start.10
  12.7 26.3 %all-to-all-start = ((bf16[16,48,256]{2,1,0:T(8,128)(2,1)}), bf16[16,48,256]{2,1,0:T(8,128)(2,1)S(1)}, u32[]{:S(2)}, u32[]{:S(2)}) async-start(bf16[16,48,256]{2,1,0:T(8,128)(2,1)} %broadcast_in_dim.9), calls=%async_computation | async-start | bytes 786432 | tf_op jit(solution)/shard_map/all_to_all | solution.py:303
  24.5 58.6 %all-gather.5.cloned.1.call-start = ((), (), s32[]{:S(2)}) async-start(), calls=%async_computation.9 | async-start | bytes 3538944 | tf_op jit(solution)/shard_map/all_gather | solution.py:323
  39.8 9.2 %collective-permute-start = (bf16[2048,128]{1,0:T(8,128)(2,1)}, bf16[2048,128]{1,0:T(8,128)(2,1)}, u32[]{:S(2)}, u32[]{:S(2)}) collective-permute-start(bf16[2048,128]{1,0:T(8,128)(2,1)} %get-tuple-element.19), channel_id=1, source_target_pairs={{0,32},{32,0},{1,33},{33,1},{2,34},{34,2},{3,35},{35,3},{4,36},{36... | collective-permute-start | bytes 1572872 | tf_op jit(solution)/shard_map/ppermute | solution.py:324
  45.2 15.6 %all-to-all-start.2 = ((bf16[16,32,256]{2,1,0:T(8,128)(2,1)}), bf16[16,32,256]{2,1,0:T(8,128)(2,1)S(1)}, u32[]{:S(2)}, u32[]{:S(2)}) async-start(bf16[16,32,256]{2,1,0:T(8,128)(2,1)} %maximum_bitcast_fusion), calls=%async_computation.2 | async-start | bytes 524288 | tf_op jit(solution)/shard_map/all_to_all | solution.py:308
  60.7 31.2 %all-to-all-start.1 = ((bf16[8,256,128]{2,1,0:T(8,128)(2,1)}), bf16[8,256,128]{2,1,0:T(8,128)(2,1)S(1)}, u32[]{:S(2)}, u32[]{:S(2)}) async-start(bf16[8,256,128]{2,1,0:T(8,128)(2,1)} %bitcast.95), calls=%async_computation.1 | async-start | bytes 1048576 | tf_op jit(solution)/shard_map/all_to_all | solution.py:326
  64.2 92.0 %all-gather.7.cloned.1.call-start = ((), (), s32[]{:S(2)}) async-start(), calls=%async_computation.10 | async-start | bytes 1966080 | tf_op jit(solution)/shard_map/all_gather | solution.py:362
  83.0 1.9 copy-start.2
  91.1 0.8 copy-start.6
  121.0 1.9 copy-start.3
  149.5 15.1 %collective-permute-start.1 = (bf16[2048,128]{1,0:T(8,128)(2,1)S(1)}, bf16[2048,128]{1,0:T(8,128)(2,1)S(1)}, u32[]{:S(2)}, u32[]{:S(2)}) collective-permute-start(bf16[2048,128]{1,0:T(8,128)(2,1)S(1)} %bitcast.88), channel_id=1, source_target_pairs={{0,32},{32,0},{1,33},{33,1},{2,34},{34,2},{3,35},{35,3},{4,36},{36... | collective-permute-start | bytes 1572872 | tf_op jit(solution)/shard_map/ppermute | solution.py:381
  156.3 1.4 copy-start.4
  157.7 1.0 copy-start.7
  160.5 13.2 %all-to-all-start.7 = ((bf16[16,8,512]{2,1,0:T(8,128)(2,1)}), bf16[16,8,512]{2,1,0:T(8,128)(2,1)}, u32[]{:S(2)}, u32[]{:S(2)}) async-start(bf16[16,8,512]{2,1,0:T(8,128)(2,1)} %shard_map.70), calls=%async_computation.7 | async-start | bytes 262144 | tf_op jit(solution)/shard_map/all_to_all | solution.py:405
  164.6 1.6 copy-start.1
  195.5 3.9 %collective-permute-start.2 = (bf16[2048,128]{1,0:T(8,128)(2,1)S(1)}, bf16[2048,128]{1,0:T(8,128)(2,1)S(1)}, u32[]{:S(2)}, u32[]{:S(2)}) collective-permute-start(bf16[2048,128]{1,0:T(8,128)(2,1)S(1)} %bitcast.90), channel_id=1, source_target_pairs={{0,32},{32,0},{1,33},{33,1},{2,34},{34,2},{3,35},{35,3},{4,36},{36... | collective-permute-start | bytes 1572872 | tf_op jit(solution)/shard_map/ppermute | solution.py:410
Sparse Core Ops, SparseCore 0:
  39.9 43.0 all-gather.4
  92.0 31.5 all-gather.6

commit v3 on v2

--- a/solution.py
+++ b/solution.py
@@ -32,6 +32,10 @@
     )(*args)
 
 
+def ring(size, step):
+    return [(i, (i + step) % size) for i in range(size)]
+
+
 def moved(value, axis):
     return lax.all_to_all(value, axis, 0, 0)
 
@@ -56,18 +60,29 @@
     send_ref[...] = rows[half:].astype(BF16)
 
 
+def sort_maps(core, got_ref, maps_ref, half_ref):
+    peers, _, n = got_ref.shape
+    nodes = n // peers
+    for g in range(peers):
+        for k in range(3):
+            maps_ref[k * n + g * nodes : k * n + (g + 1) * nodes] = got_ref[
+                g, k * nodes : (k + 1) * nodes
+            ]
+    rows = half_ref.shape[0]
+    half_ref[...] = maps_ref[pl.ds(pl.multiple_of(core[0] * rows, rows), rows), :]
+
+
 def face_parts(parts_ref, rows_ref, loads_ref, out_ref, order):
     total = parts_ref[0].astype(F32)
     for z in range(1, parts_ref.shape[0]):
         total = total + parts_ref[z].astype(F32)
     loads = total.astype(BF16)
-    for z in range(loads_ref.shape[0]):
-        loads_ref[z] = loads
-    peers, both, _ = rows_ref.shape
-    nodes = both // 2
+    loads_ref[...] = loads
+    peers, five, _ = rows_ref.shape
+    nodes = five // 5
     for g in range(peers):
-        order[g * nodes : (g + 1) * nodes] = rows_ref[g, 0:nodes]
-        order[(peers + g) * nodes : (peers + g + 1) * nodes] = rows_ref[g, nodes:both]
+        order[g * nodes : (g + 1) * nodes] = rows_ref[g, 3 * nodes : 4 * nodes]
+        order[(peers + g) * nodes : (peers + g + 1) * nodes] = rows_ref[g, 4 * nodes : five]
     lines = lax.dot_general(total.T.astype(BF16), order[...], NT, preferred_element_type=F32)
     part = out_ref.shape[1]
     for g in range(peers):
@@ -83,14 +98,14 @@
         out_ref[y] = line
 
 
-def first_rows(core, map_ref, own_ref, other_ref, initial_ref, *, width):
-    side = core[0]
-    pairs = own_ref.shape[0] // width
+def first_rows(place, map_ref, own_ref, other_ref, initial_ref, *, width, masks):
+    side, here = place[0], place[1]
     total = None
-    for z in range(pairs):
-        mine = pl.ds(pl.multiple_of((2 * z + side) * width, width), width)
-        theirs = pl.ds(pl.multiple_of((2 * z + 1 - side) * width, width), width)
-        block = slice(z * width, (z + 1) * width)
+    for slot, mask in enumerate(masks):
+        pair = 2 * (here ^ mask)
+        mine = pl.ds(pl.multiple_of((pair + side) * width, width), width)
+        theirs = pl.ds(pl.multiple_of((pair + 1 - side) * width, width), width)
+        block = slice(slot * width, (slot + 1) * width)
         both = jnp.dot(map_ref[:, mine], own_ref[block], preferred_element_type=F32) + jnp.dot(
             map_ref[:, theirs], other_ref[block], preferred_element_type=F32
         )
@@ -98,6 +113,12 @@
     initial_ref[...] = total
 
 
+def lay_halves(target, side, slot, mine, other):
+    rows = mine.shape[0]
+    target[slot, pl.ds(pl.multiple_of(side * rows, rows), rows), :] = mine
+    target[slot, pl.ds(pl.multiple_of((1 - side) * rows, rows), rows), :] = other
+
+
 def halves(value):
     high = value.astype(BF16)
     low = (value - high.astype(F32)).astype(BF16)
@@ -120,10 +141,17 @@
     return both[:rows] + both[rows:]
 
 
-def block_maps(place, maps_ref, joined_ref, own_ref, state, right, through):
+def block_maps(place, own_maps_ref, *refs, steps):
+    mine, others = refs[: len(steps)], refs[len(steps) : -7]
+    maps_ref, joined_ref, half_ref, own_ref, state, right, through = refs[-7:]
     count = maps_ref.shape[0]
     n = maps_ref.shape[2]
-    here = place[0]
+    here, side = place[0], place[1]
+    maps_ref[here] = own_maps_ref[...]
+    rows = half_ref.shape[0]
+    pieces = [o[k * rows : (k + 1) * rows] for o in others for k in range(o.shape[0] // rows)]
+    for step, one, other in zip(steps, mine, pieces, strict=True):
+        lay_halves(maps_ref, side, lax.rem(here + step + count, count), one[...], other)
     unit = (
         lax.broadcasted_iota(jnp.int32, (n, n), 0) == lax.broadcasted_iota(jnp.int32, (n, n), 1)
     ).astype(F32)
@@ -163,6 +191,7 @@
     lax.fori_loop(0, count, back, 0)
     joined_ref[n : 2 * n] = right[:, 0:n].astype(BF16)
     joined_ref[2 * n : 3 * n] = right[:, n : 2 * n].astype(BF16)
+    half_ref[...] = joined_ref[pl.ds(pl.multiple_of(side * rows, rows), rows), :]
 
 
 def block_values(place, faces_ref, maps_ref, ends_ref, own_ref):
@@ -201,10 +230,17 @@
         ends_ref[x] = ends
 
 
-def meet_values(place, ends_ref, joined_ref, maps_ref, own_ref, out_ref, entering):
+def meet_values(place, ends_ref, own_joined_ref, *refs, steps):
+    mine = refs[: len(steps)]
+    others, maps_ref, own_ref, out_ref, entering, joined_ref = refs[len(steps) :]
     count, part, _ = ends_ref.shape
     n = joined_ref.shape[2]
-    here = place[0]
+    here, side = place[0], place[1]
+    joined_ref[here] = own_joined_ref[...]
+    rows = mine[0].shape[0]
+    for k, step in enumerate(steps):
+        other = others[k * rows : (k + 1) * rows]
+        lay_halves(joined_ref, side, lax.rem(here + step + count, count), mine[k][...], other)
     east = jnp.zeros((part, n), F32)
     sources = []
     for b in range(count):
@@ -276,9 +312,11 @@
     part = columns // peers
     half = interface // nc
     side = lax.axis_index("c")
-    core = jnp.reshape(side, (1,)).astype(jnp.int32)
-    at_y = jnp.reshape(lax.axis_index("y"), (1,)).astype(jnp.int32)
-    at_x = jnp.reshape(lax.axis_index("x"), (1,)).astype(jnp.int32)
+    core = side.astype(jnp.int32)
+    at_y = jnp.stack([lax.axis_index("y").astype(jnp.int32), core])
+    at_x = jnp.stack([lax.axis_index("x").astype(jnp.int32), core])
+    at_z = jnp.stack([core, lax.axis_index("z").astype(jnp.int32)])
+    core = core.reshape((1,))
     swap = [(0, 1), (1, 0)]
 
     spot = lax.broadcasted_iota(jnp.int32, (interface, 2 * n), 0)
@@ -300,12 +338,10 @@
     steps = coupled.reshape(nodes, stride, 2 * n)
     slices = jnp.concatenate([steps[:, 1, :n], steps[:, 0, :n], steps[:, 0, n:]], axis=0)
     slices = jnp.broadcast_to(slices, (peers,) + slices.shape)
-    slices = lax.all_to_all(slices, GRP, 0, 0)
-    maps = slices.reshape(peers, 3, nodes, n).transpose(1, 0, 2, 3).reshape(3 * n, n)
     rows = rows_map.reshape(nodes, stride, interface)
     rows = jnp.concatenate([rows[:, 1], rows[:, 0]], axis=0)
-    face_rows = rows.reshape(2 * nodes, peers, width).transpose(1, 0, 2)
-    face_rows = lax.all_to_all(face_rows, GRP, 0, 0)
+    rows = rows.reshape(2 * nodes, peers, width).transpose(1, 0, 2)
+    pieces = lax.all_to_all(jnp.concatenate([slices, rows], axis=1), GRP, 0, 0)
 
     owner = nodes_of // width
     pos = ((owner % nc) ^ side) * half + (owner // nc) * width + nodes_of % width
@@ -319,22 +355,48 @@
         local_map,
         local_load,
     )
-    maps, send = lax.optimization_barrier((maps, send))
-    run_maps = lax.all_gather(maps, "y")
     got = lax.ppermute(send, "c", swap)
     paired = (keep.astype(F32) + got.astype(F32)).astype(BF16)
+    pieces, paired = lax.optimization_barrier((pieces, paired))
+    maps, half_maps = call(
+        sort_maps,
+        (jax.ShapeDtypeStruct((3 * n, n), BF16), jax.ShapeDtypeStruct((3 * n // nc, n), BF16)),
+        [],
+        1,
+        (1000, 16 * n * n),
+        core,
+        pieces,
+    )
+
+    y_steps, y_mine = [], []
+    up = down = half_maps
+    for k in range(1, ny // 2 + 1):
+        up = lax.ppermute(up, "y", ring(ny, 1))
+        y_steps.append(-k)
+        y_mine.append(up)
+        if k < ny - k:
+            down = lax.ppermute(down, "y", ring(ny, -1))
+            y_steps.append(k)
+            y_mine.append(down)
+    near = (len(y_mine) + 1) // 2
+    y_others = [
+        lax.ppermute(jnp.concatenate(part_of, axis=0), "c", swap)
+        for part_of in (y_mine[:near], y_mine[near:])
+        if part_of
+    ]
+
     parts = lax.all_to_all(paired.reshape(nz, width, columns), "z", 0, 0)
     loads, faces = call(
         face_parts,
         (
-            jax.ShapeDtypeStruct((nz, width, columns), BF16),
+            jax.ShapeDtypeStruct((width, columns), BF16),
             jax.ShapeDtypeStruct((peers, part, 2 * n), BF16),
         ),
         [pltpu.VMEM((2 * n, width), BF16)],
         0,
         (4 * n * width * columns, 4 * n * width),
         parts,
-        face_rows,
+        pieces,
     )
     faces = lax.all_to_all(faces, GRP, 0, 0)
     line = call(
@@ -346,9 +408,14 @@
         faces,
     )
 
-    joined, own_maps = call(
-        block_maps,
-        (jax.ShapeDtypeStruct((3 * n, n), BF16), jax.ShapeDtypeStruct((3 * n, n), BF16)),
+    run_maps, joined, half_joined, own_maps = call(
+        functools.partial(block_maps, steps=tuple(y_steps)),
+        (
+            jax.ShapeDtypeStruct((ny, 3 * n, n), BF16),
+            jax.ShapeDtypeStruct((3 * n, n), BF16),
+            jax.ShapeDtypeStruct((3 * n // nc, n), BF16),
+            jax.ShapeDtypeStruct((3 * n, n), BF16),
+        ),
         [
             pltpu.VMEM((n, n), F32),
             pltpu.VMEM((n, 2 * n), F32),
@@ -357,9 +424,34 @@
         1,
         (16 * ny * n**3, 6 * ny * n * n),
         at_y,
-        run_maps,
-    )
-    all_joined = lax.all_gather(joined, "x")
+        maps,
+        *y_mine,
+        *y_others,
+    )
+    x_steps = [-1] + ([1] if nx > 2 else []) + ([-2] if nx > 3 else [])
+    x_mine = [lax.ppermute(half_joined, "x", ring(nx, -step)) for step in x_steps]
+    x_others = lax.ppermute(jnp.concatenate(x_mine, axis=0), "c", swap)
+
+    masks = [0]
+    loads_own = loads
+    far = nz // 2
+    while far:
+        met_loads = lax.ppermute(loads_own, "z", [(z, z ^ far) for z in range(nz)])
+        loads_own = jnp.concatenate([loads_own, met_loads], axis=0)
+        masks += [mask ^ far for mask in masks]
+        far //= 2
+    loads_other = lax.ppermute(loads_own, "c", swap)
+    initial = call(
+        functools.partial(first_rows, width=width, masks=tuple(masks)),
+        jax.ShapeDtypeStruct((width, columns), F32),
+        [],
+        1,
+        (2 * width * interface * columns, 2 * width * interface),
+        at_z,
+        rows_map,
+        loads_own,
+        loads_other,
+    )
 
     line = moved(line, "y")
     ends, own_values = call(
@@ -376,29 +468,17 @@
         run_maps,
     )
     ends = moved(ends, "x")
-    loads, ends = lax.optimization_barrier((loads, ends))
-    loads_own = moved(loads, "z").reshape(half, columns)
-    loads_other = lax.ppermute(loads_own, "c", swap)
-    initial = call(
-        functools.partial(first_rows, width=width),
-        jax.ShapeDtypeStruct((width, columns), F32),
-        [],
-        1,
-        (2 * width * interface * columns, 2 * width * interface),
-        core,
-        rows_map,
-        loads_own,
-        loads_other,
-    )
     met = call(
-        meet_values,
+        functools.partial(meet_values, steps=tuple(x_steps)),
         jax.ShapeDtypeStruct((peers, part, 2 * n), BF16),
-        [pltpu.VMEM((part, 2 * n), F32)],
+        [pltpu.VMEM((part, 2 * n), F32), pltpu.VMEM((nx, 3 * n, n), BF16)],
         1,
         (12 * nx * n * n * 16, 6 * nx * n * n),
         at_x,
         ends,
-        all_joined,
+        joined,
+        *x_mine,
+        x_others,
         own_maps,
         own_values,
     )

time: 210 us -> 222 us (1.057)
  starting transfers between devices: 34.3 us -> 104 us
  blocking collectives: 73.2 us -> 20.4 us
  between operations: 13.7 us -> 0.66 us
  waiting for transfers between devices: 47.9 us -> 39 us
  local copies, waits for them, and re-layouts: 14.2 us -> 21.1 us
  other arithmetic: 2.77 us -> 8.71 us
  Pallas kernels: 18.1 us -> 21.9 us
    ppermute x0 -> x16, starting transfers between devices: none -> 58.7 us  [the longest x3 14.8 us: on_device(): met_loads = lax.ppermute(loads_own, 'z', [(z, z ^ far) for z in range(nz)])]
    all_to_all x4 -> x0, blocking collectives: 52.8 us -> none  [the longest x3 35.1 us: moved(): return lax.all_to_all(value, axis, 0, 0)]
    all_gather x2 -> x0, waiting for transfers between devices: 18.8 us -> none  [the longest x1 18.7 us: on_device(): run_maps = lax.all_gather(maps, 'y')]
    all_to_all x2 -> x4, starting transfers between devices: 15.6 us -> 26 us  [the longest x1 11.8 us: on_device(): pieces = lax.all_to_all(jnp.concatenate([slices, rows], axis=1), GRP, 0, 0)]
    unnamed x29 -> x66, local copies, waits for them, and re-layouts: 9.83 us -> 18.2 us
    concatenate x0 -> x6, other arithmetic: none -> 7.47 us  [the longest x2 4.02 us: on_device(): jnp.concatenate(part_of, axis=0)]
    ppermute x0 -> x16, waiting for transfers between devices: none -> 6.33 us  [the longest x4 5.34 us: on_device(): up = lax.ppermute(up, 'y', ring(ny, 1))]
    pallas_call x8 -> x9, Pallas kernels: 18.1 us -> 21.9 us  [call(): pl.pallas_call(kernel, out_shape=outs, in_specs=specs, out_specs=jax.tree...]
  transfers between devices with their start and end apart: 9 -> 25, of which waited for: 5 -> 10; matrix products, arithmetic and copies ran while one was open for 3% -> 4% of each run, Pallas kernels for 7% -> 9%
where the time goes in v3:
time: 222 us; the launch traced here: 220 us
  starting transfers between devices  104 us (47%)
  waiting for transfers between devices  39 us (18%)
  Pallas kernels  21.9 us (10%)
  local copies, waits for them, and re-layouts  21.1 us (10%)
  blocking collectives  20.4 us (9%)
  other arithmetic  8.71 us (4%)
  matrix products  4.05 us (2%)
    pallas_call x9, Pallas kernels, call(): pl.pallas_call(kernel, out_shape=outs, in_specs=specs, out_specs=jax.tree...  21.9 us
    all_to_all x1, blocking collectives, on_device(): final_own = lax.all_to_all(final, 'z', 0, 0).reshape(half, columns)  20.4 us
    unnamed x66, local copies, waits for them, and re-layouts  18.2 us
    ppermute x3, starting transfers between devices, on_device(): met_loads = lax.ppermute(loads_own, 'z', [(z, z ^ far) for z in range(nz)])  14.8 us
    ppermute x3, starting transfers between devices, on_device(): down = lax.ppermute(down, 'y', ring(ny, -1))  12.7 us
    all_to_all x1, waiting for transfers between devices, on_device(): pieces = lax.all_to_all(jnp.concatenate([slices, rows], axis=1), GRP, 0, 0)  12.6 us
    all_to_all x1, starting transfers between devices, on_device(): pieces = lax.all_to_all(jnp.concatenate([slices, rows], axis=1), GRP, 0, 0)  11.8 us
    all_to_all x2, waiting for transfers between devices, moved(): return lax.all_to_all(value, axis, 0, 0)  11.4 us
  transfers between devices with their start and end apart: 25, of which 10 were waited for; matrix products, arithmetic and copies ran while one was open for 4% of the time, Pallas kernels for 9%

profile of v3, /device:TPU:1, one launch (start us, length us, event | category | flops | bytes accessed | tf_op | source)
XLA Modules:
  0.0 219.8 jit_solution(6866686128428847423)
XLA Ops:
  0.0 2.9 %fusion.9 = bf16[256,512]{0,1:T(8,128)(2,1)S(1)} fusion(s32[512]{0:T(512)S(1)} %get-tuple-element.40, s32[512]{0:T(512)S(1)} %get-tuple-element.39, pred[512]{0:T(512)(128)(4,1)S(1)} %iota_compare_fusion, bf16[1,256,4096]{2,1,0:T(8,128)(2,1)} %param.8), kind=kOutput, calls=%fused_computation.7 | convolution fusion | flops 1080164352 | bytes 2363904 | tf_op jit(solution)/shard_map/dot_general | solution.py:325
  4.5 2.7 %slice_reduce_fusion.1 = (bf16[16,4096]{1,0:T(8,128)(2,1)S(1)}, bf16[16,4096]{1,0:T(8,128)(2,1)S(1)}) fusion(bf16[16,16,4096]{2,1,0:T(8,128)(2,1)} %bitcast.78), kind=kLoop, calls=%fused_computation.18 | loop fusion | bytes 524288 | tf_op jit(solution)/shard_map/slice | solution.py:342
  8.2 11.8 %all-to-all-start = ((bf16[16,80,256]{2,1,0:T(8,128)(2,1)}), bf16[16,80,256]{2,1,0:T(8,128)(2,1)S(1)}, u32[]{:S(2)}, u32[]{:S(2)}) async-start(bf16[16,80,256]{2,1,0:T(8,128)(2,1)} %pad_maximum_fusion.1), calls=%async_computation | async-start | bytes 1310720 | tf_op jit(solution)/shard_map/all_to_all | solution.py:344
  20.1 2.6 %shard_map.64 = (bf16[2048,128]{1,0:T(8,128)(2,1)S(1)}, bf16[2048,128]{1,0:T(8,128)(2,1)S(1)}) custom-call(s32[1024]{0:T(1024)S(1)} %fusion.32.pos, bf16[1024,1024]{1,0:T(8,128)(2,1)S(1)} %bitcast.76, bf16[1024,128]{1,0:T(8,128)(2,1)S(1)} %bitcast.82), custom_call_target="tpu_custom_call" | custom-call | flops 268435456 | bytes 6291456 | tf_op jit(solution)/shard_map/pallas_call | solution.py:24
  27.4 12.6 %all-to-all-done.rows_ref.got_ref = bf16[16,80,256]{2,1,0:T(8,128)(2,1)S(1)} async-done(((bf16[16,80,256]{2,1,0:T(8,128)(2,1)}), bf16[16,80,256]{2,1,0:T(8,128)(2,1)S(1)}, u32[]{:S(2)}, u32[]{:S(2)}) %all-to-all-start) | async-done | bytes 655392 | tf_op jit(solution)/shard_map/all_to_all | solution.py:344
  40.8 3.2 %collective-permute-start.5 = (bf16[384,256]{1,0:T(8,128)(2,1)S(1)}, bf16[384,256]{1,0:T(8,128)(2,1)S(1)}, u32[]{:S(2)}, u32[]{:S(2)}) collective-permute-start(bf16[384,256]{1,0:T(8,128)(2,1)S(1)} %get-tuple-element.26), channel_id=1, source_target_pairs={{0,1},{1,2},{2,3},{3,4},{4,5},{5,6},{6,7},{7,0},{8,9},{9,10},{10,1... | collective-permute-start | bytes 589832 | tf_op jit(solution)/shard_map/ppermute | solution.py:374
  44.0 3.8 %collective-permute-start.6 = (bf16[384,256]{1,0:T(8,128)(2,1)S(1)}, bf16[384,256]{1,0:T(8,128)(2,1)}, u32[]{:S(2)}, u32[]{:S(2)}) collective-permute-start(bf16[384,256]{1,0:T(8,128)(2,1)S(1)} %get-tuple-element.26), channel_id=1, source_target_pairs={{0,7},{1,0},{2,1},{3,2},{4,3},{5,4},{6,5},{7,6},{8,15},{9,8},{10,9... | collective-permute-start | bytes 589832 | tf_op jit(solution)/shard_map/ppermute | solution.py:378
  52.4 4.3 %collective-permute-start.8 = (bf16[384,256]{1,0:T(8,128)(2,1)}, bf16[384,256]{1,0:T(8,128)(2,1)}, u32[]{:S(2)}, u32[]{:S(2)}) collective-permute-start(bf16[384,256]{1,0:T(8,128)(2,1)} %collective-permute-done.6.refs_1_), channel_id=1, source_target_pairs={{0,7},{1,0},{2,1},{3,2},{4,3},{5,4},{6,5},{7,6},{8,15},{9,8},{10,9... | collective-permute-start | bytes 589832 | tf_op jit(solution)/shard_map/ppermute | solution.py:378
  56.8 3.1 %collective-permute-done.7.refs_2_ = bf16[384,256]{1,0:T(8,128)(2,1)} collective-permute-done((bf16[384,256]{1,0:T(8,128)(2,1)S(1)}, bf16[384,256]{1,0:T(8,128)(2,1)}, u32[]{:S(2)}, u32[]{:S(2)}) %collective-permute-start.7) | collective-permute-done | bytes 196640 | tf_op jit(solution)/shard_map/ppermute | solution.py:374
  61.8 3.5 %all-to-all-start.1 = ((bf16[8,256,128]{2,1,0:T(8,128)(2,1)}), bf16[8,256,128]{2,1,0:T(8,128)(2,1)S(1)}, u32[]{:S(2)}, u32[]{:S(2)}) async-start(bf16[8,256,128]{2,1,0:T(8,128)(2,1)} %bitcast.84), calls=%async_computation.1 | async-start | bytes 1048576 | tf_op jit(solution)/shard_map/all_to_all | solution.py:388
  65.4 4.6 %collective-permute-start.10 = (bf16[384,256]{1,0:T(8,128)(2,1)}, bf16[384,256]{1,0:T(8,128)(2,1)S(1)}, u32[]{:S(2)}, u32[]{:S(2)}) collective-permute-start(bf16[384,256]{1,0:T(8,128)(2,1)} %collective-permute-done.8.refs_3_), channel_id=1, source_target_pairs={{0,7},{1,0},{2,1},{3,2},{4,3},{5,4},{6,5},{7,6},{8,15},{9,8},{10,9... | collective-permute-start | bytes 589832 | tf_op jit(solution)/shard_map/ppermute | solution.py:378
  74.0 3.6 %collective-permute-start.12 = (bf16[1536,256]{1,0:T(8,128)(2,1)}, bf16[1536,256]{1,0:T(8,128)(2,1)}, u32[]{:S(2)}, u32[]{:S(2)}) collective-permute-start(bf16[1536,256]{1,0:T(8,128)(2,1)} %pad_maximum_fusion), channel_id=1, source_target_pairs={{0,32},{32,0},{1,33},{33,1},{2,34},{34,2},{3,35},{35,3},{4,36},{36... | collective-permute-start | bytes 2359304 | tf_op jit(solution)/shard_map/ppermute | solution.py:383
  80.6 4.5 %collective-permute-start.13 = (bf16[1152,256]{1,0:T(8,128)(2,1)}, bf16[1152,256]{1,0:T(8,128)(2,1)}, u32[]{:S(2)}, u32[]{:S(2)}) collective-permute-start(bf16[1152,256]{1,0:T(8,128)(2,1)} %pad_maximum_fusion.2), channel_id=1, source_target_pairs={{0,32},{32,0},{1,33},{33,1},{2,34},{34,2},{3,35},{35,3},{4,36},{36... | collective-permute-start | bytes 1769480 | tf_op jit(solution)/shard_map/ppermute | solution.py:383
  86.5 7.5 %collective-permute-start.1 = (bf16[256,128]{1,0:T(8,128)(2,1)}, bf16[256,128]{1,0:T(8,128)(2,1)S(1)}, u32[]{:S(2)}, u32[]{:S(2)}) collective-permute-start(bf16[256,128]{1,0:T(8,128)(2,1)} %get-tuple-element.23), channel_id=1, source_target_pairs={{0,256},{64,320},{128,384},{192,448},{256,0},{320,64},{384,128},{4... | collective-permute-start | bytes 196616 | tf_op jit(solution)/shard_map/ppermute | solution.py:439
  94.1 4.2 %all-to-all-start.2 = ((bf16[16,8,512]{2,1,0:T(8,128)(2,1)}), bf16[16,8,512]{2,1,0:T(8,128)(2,1)}, u32[]{:S(2)}, u32[]{:S(2)}) async-start(bf16[16,8,512]{2,1,0:T(8,128)(2,1)} %copy-done.17), calls=%async_computation.2 | async-start | bytes 262144 | tf_op jit(solution)/shard_map/all_to_all | solution.py:401
  99.1 4.2 %collective-permute-start.2 = (bf16[512,128]{1,0:T(8,128)(2,1)S(1)}, bf16[512,128]{1,0:T(8,128)(2,1)S(1)}, u32[]{:S(2)}, u32[]{:S(2)}) collective-permute-start(bf16[512,128]{1,0:T(8,128)(2,1)S(1)} %pad_maximum_fusion.5), channel_id=1, source_target_pairs={{0,128},{64,192},{128,0},{192,64},{256,384},{320,448},{384,256},{4... | collective-permute-start | bytes 393224 | tf_op jit(solution)/shard_map/ppermute | solution.py:439
  107.1 7.3 %shard_map.69 = (bf16[8,768,256]{2,1,0:T(8,128)(2,1)S(1)}, bf16[768,256]{1,0:T(8,128)(2,1)S(1)}, bf16[384,256]{1,0:T(8,128)(2,1)S(1)}, bf16[768,256]{1,0:T(8,128)(2,1)S(1)}) custom-call(s32[2]{0:T(128)S(1)} %pad_add_fusion.2.place, bf16[768,256]{1,0:T(8,128)(2,1)S(1)} %copy-done.22, bf16[384,256]{1,0:T(8,128)(2,1)S(1)} %copy-done.12, ...), custom_call_target="tpu_custom_call" | custom-call | flops 2147483648 | bytes 3145728 | tf_op jit(solution)/shard_map/pallas_call | solution.py:24
  116.1 4.6 %collective-permute-start.16 = (bf16[384,256]{1,0:T(8,128)(2,1)S(1)}, bf16[384,256]{1,0:T(8,128)(2,1)S(1)}, u32[]{:S(2)}, u32[]{:S(2)}) collective-permute-start(bf16[384,256]{1,0:T(8,128)(2,1)S(1)} %get-tuple-element.30), channel_id=1, source_target_pairs={{0,16},{8,24},{16,0},{24,8},{1,17},{9,25},{17,1},{25,9},{2,18},{10... | collective-permute-start | bytes 589832 | tf_op jit(solution)/shard_map/ppermute | solution.py:432
  120.8 2.8 %collective-permute-start.15 = (bf16[384,256]{1,0:T(8,128)(2,1)S(1)}, bf16[384,256]{1,0:T(8,128)(2,1)S(1)}, u32[]{:S(2)}, u32[]{:S(2)}) collective-permute-start(bf16[384,256]{1,0:T(8,128)(2,1)S(1)} %get-tuple-element.30), channel_id=1, source_target_pairs={{0,24},{8,0},{16,8},{24,16},{1,25},{9,1},{17,9},{25,17},{2,26},{10... | collective-permute-start | bytes 589832 | tf_op jit(solution)/shard_map/ppermute | solution.py:432
  123.5 2.5 %collective-permute-start.14 = (bf16[384,256]{1,0:T(8,128)(2,1)S(1)}, bf16[384,256]{1,0:T(8,128)(2,1)S(1)}, u32[]{:S(2)}, u32[]{:S(2)}) collective-permute-start(bf16[384,256]{1,0:T(8,128)(2,1)S(1)} %get-tuple-element.30), channel_id=1, source_target_pairs={{0,8},{8,16},{16,24},{24,0},{1,9},{9,17},{17,25},{25,1},{2,10},{10... | collective-permute-start | bytes 589832 | tf_op jit(solution)/shard_map/ppermute | solution.py:432
  127.8 3.1 %collective-permute-start.3 = (bf16[1024,128]{1,0:T(8,128)(2,1)S(1)}, bf16[1024,128]{1,0:T(8,128)(2,1)S(1)}, u32[]{:S(2)}, u32[]{:S(2)}) collective-permute-start(bf16[1024,128]{1,0:T(8,128)(2,1)S(1)} %pad_maximum_fusion.4), channel_id=1, source_target_pairs={{0,64},{64,0},{128,192},{192,128},{256,320},{320,256},{384,448},{4... | collective-permute-start | bytes 786440 | tf_op jit(solution)/shard_map/ppermute | solution.py:439
  132.7 4.0 %collective-permute-start.17 = (bf16[1152,256]{1,0:T(8,128)(2,1)}, bf16[1152,256]{1,0:T(8,128)(2,1)}, u32[]{:S(2)}, u32[]{:S(2)}) collective-permute-start(bf16[1152,256]{1,0:T(8,128)(2,1)} %pad_maximum_fusion.3), channel_id=1, source_target_pairs={{0,32},{32,0},{1,33},{33,1},{2,34},{34,2},{3,35},{35,3},{4,36},{36... | collective-permute-start | bytes 1769480 | tf_op jit(solution)/shard_map/ppermute | solution.py:433
  136.8 3.5 %collective-permute-start.4 = (bf16[2048,128]{1,0:T(8,128)(2,1)S(1)}, bf16[2048,128]{1,0:T(8,128)(2,1)}, u32[]{:S(2)}, u32[]{:S(2)}) collective-permute-start(bf16[2048,128]{1,0:T(8,128)(2,1)S(1)} %constant_dynamic-update-slice_fusion.own_ref), channel_id=1, source_target_pairs={{0,32},{32,0},{1,33},{33,1},{2,34},{34,2},{3,35},{35,3},{4,36},{36... | collective-permute-start | bytes 1572872 | tf_op jit(solution)/shard_map/ppermute | solution.py:443
  141.9 6.6 %all-to-all-start.3 = ((bf16[8,8,512]{2,1,0:T(8,128)(2,1)}), bf16[8,8,512]{2,1,0:T(8,128)(2,1)S(1)}, u32[]{:S(2)}, u32[]{:S(2)}) async-start(bf16[8,8,512]{2,1,0:T(8,128)(2,1)} %copy-done.10), calls=%async_computation.3 | async-start | bytes 131072 | tf_op jit(solution)/shard_map/all_to_all | solution.py:40
  148.5 7.1 %all-to-all-done.3.faces_ref = bf16[8,8,512]{2,1,0:T(8,128)(2,1)S(1)} async-done(((bf16[8,8,512]{2,1,0:T(8,128)(2,1)}), bf16[8,8,512]{2,1,0:T(8,128)(2,1)S(1)}, u32[]{:S(2)}, u32[]{:S(2)}) %all-to-all-start.3) | async-done | bytes 65568 | tf_op jit(solution)/shard_map/all_to_all | solution.py:40
  157.6 3.1 %shard_map.70 = (bf16[4,8,512]{2,1,0:T(8,128)(2,1)S(1)}, f32[8,512]{1,0:T(8,128)S(1)}) custom-call(s32[2]{0:T(128)S(1)} %pad_add_fusion.2.place, bf16[8,8,512]{2,1,0:T(8,128)(2,1)S(1)} %all-to-all-done.3.faces_ref, bf16[8,768,256]{2,1,0:T(8,128)(2,1)S(1)} %copy-done.3), custom_call_target="tpu_custom_call" | custom-call | flops 100663296 | bytes 3145728 | tf_op jit(solution)/shard_map/pallas_call | solution.py:24
  161.9 3.3 %all-to-all-start.4 = ((bf16[4,8,512]{2,1,0:T(8,128)(2,1)}), bf16[4,8,512]{2,1,0:T(8,128)(2,1)S(1)}, u32[]{:S(2)}, u32[]{:S(2)}) async-start(bf16[4,8,512]{2,1,0:T(8,128)(2,1)} %copy-done.18), calls=%async_computation.4 | async-start | bytes 65536 | tf_op jit(solution)/shard_map/all_to_all | solution.py:40
  165.3 4.2 %all-to-all-done.4.ends_ref = bf16[4,8,512]{2,1,0:T(8,128)(2,1)S(1)} async-done(((bf16[4,8,512]{2,1,0:T(8,128)(2,1)}), bf16[4,8,512]{2,1,0:T(8,128)(2,1)S(1)}, u32[]{:S(2)}, u32[]{:S(2)}) %all-to-all-start.4) | async-done | bytes 32800 | tf_op jit(solution)/shard_map/all_to_all | solution.py:40
  175.3 7.9 %all-to-all-start.5 = ((bf16[16,8,512]{2,1,0:T(8,128)(2,1)}), bf16[16,8,512]{2,1,0:T(8,128)(2,1)S(1)}, u32[]{:S(2)}, u32[]{:S(2)}) async-start(bf16[16,8,512]{2,1,0:T(8,128)(2,1)} %copy-done.5), calls=%async_computation.5 | async-start | bytes 262144 | tf_op jit(solution)/shard_map/all_to_all | solution.py:485
  186.7 5.4 %all-to-all-done.5 = bf16[16,8,512]{2,1,0:T(8,128)(2,1)S(1)} async-done(((bf16[16,8,512]{2,1,0:T(8,128)(2,1)}), bf16[16,8,512]{2,1,0:T(8,128)(2,1)S(1)}, u32[]{:S(2)}, u32[]{:S(2)}) %all-to-all-start.5) | async-done | bytes 131104 | tf_op jit(solution)/shard_map/all_to_all | solution.py:485
  192.4 20.4 %all_to_all.35 = bf16[8,256,128]{2,1,0:T(8,128)(2,1)S(1)} all-to-all(bf16[8,256,128]{2,1,0:T(8,128)(2,1)S(1)} %broadcast_in_dim.10), channel_id=1, replica_groups=mesh['z'=8,'c'=2,'x'=4,'y'=8] {'z'}, dimensions={0} | all-to-all | bytes 1048576 | tf_op jit(solution)/shard_map/all_to_all | solution.py:489
  216.7 3.1 %shard_map.72 = bf16[1024,128]{1,0:T(8,128)(2,1)} custom-call(s32[1024]{0:T(1024)S(1)} %fusion.32.pos, bf16[2048,128]{1,0:T(8,128)(2,1)S(1)} %bitcast.81, bf16[2048,128]{1,0:T(8,128)(2,1)S(1)} %collective-permute-done.18.other_ref, bf16[1024,1024]{1,0:T(8,128)(2,1)S(1)} %bitcast.77, bf16[1024,128]{1,0:T(8,128)(2,1)S(1)} %bitcast.83), custom_call_target="tpu_custom_call" | custom-call | flops 268435456 | bytes 2097152 | tf_op jit(solution)/shard_map/pallas_call | solution.py:24
  (123 shorter events, 50.9 us)
Async XLA Ops:
  7.2 12.8 %copy-start.29 = (s32[1,1,1024]{2,1,0:T(1,128)S(1)}, s32[1,1,1024]{2,1,0:T(1,128)}, u32[]{:S(2)}) copy-start(s32[1,1,1024]{2,1,0:T(1,128)} %param.9) | copy-start | bytes 12292
  7.2 12.8 %copy-start = (bf16[1,1,1024,1024]{3,2,1,0:T(8,128)(2,1)S(1)}, bf16[1,1,1024,1024]{3,2,1,0:T(8,128)(2,1)}, u32[]{:S(2)}) copy-start(bf16[1,1,1024,1024]{3,2,1,0:T(8,128)(2,1)} %param.7) | copy-start | bytes 6291460
  7.3 12.8 %copy-start.4 = (bf16[1,1,1024,128]{3,2,1,0:T(8,128)(2,1)S(1)}, bf16[1,1,1024,128]{3,2,1,0:T(8,128)(2,1)}, u32[]{:S(2)}) copy-start(bf16[1,1,1024,128]{3,2,1,0:T(8,128)(2,1)} %param.6) | copy-start | bytes 786436
  8.2 31.8 %all-to-all-start = ((bf16[16,80,256]{2,1,0:T(8,128)(2,1)}), bf16[16,80,256]{2,1,0:T(8,128)(2,1)S(1)}, u32[]{:S(2)}, u32[]{:S(2)}) async-start(bf16[16,80,256]{2,1,0:T(8,128)(2,1)} %pad_maximum_fusion.1), calls=%async_computation | async-start | bytes 1310720 | tf_op jit(solution)/shard_map/all_to_all | solution.py:344
  22.7 3.8 %collective-permute-start = (bf16[2048,128]{1,0:T(8,128)(2,1)S(1)}, bf16[2048,128]{1,0:T(8,128)(2,1)S(1)}, u32[]{:S(2)}, u32[]{:S(2)}) collective-permute-start(bf16[2048,128]{1,0:T(8,128)(2,1)S(1)} %get-tuple-element.20), channel_id=1, source_target_pairs={{0,32},{32,0},{1,33},{33,1},{2,34},{34,2},{3,35},{35,3},{4,36},{36... | collective-permute-start | bytes 1572872 | tf_op jit(solution)/shard_map/ppermute | solution.py:358
  40.8 8.9 %collective-permute-start.5 = (bf16[384,256]{1,0:T(8,128)(2,1)S(1)}, bf16[384,256]{1,0:T(8,128)(2,1)S(1)}, u32[]{:S(2)}, u32[]{:S(2)}) collective-permute-start(bf16[384,256]{1,0:T(8,128)(2,1)S(1)} %get-tuple-element.26), channel_id=1, source_target_pairs={{0,1},{1,2},{2,3},{3,4},{4,5},{5,6},{6,7},{7,0},{8,9},{9,10},{10,1... | collective-permute-start | bytes 589832 | tf_op jit(solution)/shard_map/ppermute | solution.py:374
  44.0 8.5 %collective-permute-start.6 = (bf16[384,256]{1,0:T(8,128)(2,1)S(1)}, bf16[384,256]{1,0:T(8,128)(2,1)}, u32[]{:S(2)}, u32[]{:S(2)}) collective-permute-start(bf16[384,256]{1,0:T(8,128)(2,1)S(1)} %get-tuple-element.26), channel_id=1, source_target_pairs={{0,7},{1,0},{2,1},{3,2},{4,3},{5,4},{6,5},{7,6},{8,15},{9,8},{10,9... | collective-permute-start | bytes 589832 | tf_op jit(solution)/shard_map/ppermute | solution.py:378
  50.3 9.6 %collective-permute-start.7 = (bf16[384,256]{1,0:T(8,128)(2,1)S(1)}, bf16[384,256]{1,0:T(8,128)(2,1)}, u32[]{:S(2)}, u32[]{:S(2)}) collective-permute-start(bf16[384,256]{1,0:T(8,128)(2,1)S(1)} %collective-permute-done.5.refs_0_), channel_id=1, source_target_pairs={{0,1},{1,2},{2,3},{3,4},{4,5},{5,6},{6,7},{7,0},{8,9},{9,10},{10,1... | collective-permute-start | bytes 589832 | tf_op jit(solution)/shard_map/ppermute | solution.py:374
  52.4 12.9 %collective-permute-start.8 = (bf16[384,256]{1,0:T(8,128)(2,1)}, bf16[384,256]{1,0:T(8,128)(2,1)}, u32[]{:S(2)}, u32[]{:S(2)}) collective-permute-start(bf16[384,256]{1,0:T(8,128)(2,1)} %collective-permute-done.6.refs_1_), channel_id=1, source_target_pairs={{0,7},{1,0},{2,1},{3,2},{4,3},{5,4},{6,5},{7,6},{8,15},{9,8},{10,9... | collective-permute-start | bytes 589832 | tf_op jit(solution)/shard_map/ppermute | solution.py:378
  59.9 10.0 %collective-permute-start.9 = (bf16[384,256]{1,0:T(8,128)(2,1)}, bf16[384,256]{1,0:T(8,128)(2,1)}, u32[]{:S(2)}, u32[]{:S(2)}) collective-permute-start(bf16[384,256]{1,0:T(8,128)(2,1)} %collective-permute-done.7.refs_2_), channel_id=1, source_target_pairs={{0,1},{1,2},{2,3},{3,4},{4,5},{5,6},{6,7},{7,0},{8,9},{9,10},{10,1... | collective-permute-start | bytes 589832 | tf_op jit(solution)/shard_map/ppermute | solution.py:374
  61.8 23.3 %all-to-all-start.1 = ((bf16[8,256,128]{2,1,0:T(8,128)(2,1)}), bf16[8,256,128]{2,1,0:T(8,128)(2,1)S(1)}, u32[]{:S(2)}, u32[]{:S(2)}) async-start(bf16[8,256,128]{2,1,0:T(8,128)(2,1)} %bitcast.84), calls=%async_computation.1 | async-start | bytes 1048576 | tf_op jit(solution)/shard_map/all_to_all | solution.py:388
  65.4 12.3 %collective-permute-start.10 = (bf16[384,256]{1,0:T(8,128)(2,1)}, bf16[384,256]{1,0:T(8,128)(2,1)S(1)}, u32[]{:S(2)}, u32[]{:S(2)}) collective-permute-start(bf16[384,256]{1,0:T(8,128)(2,1)} %collective-permute-done.8.refs_3_), channel_id=1, source_target_pairs={{0,7},{1,0},{2,1},{3,2},{4,3},{5,4},{6,5},{7,6},{8,15},{9,8},{10,9... | collective-permute-start | bytes 589832 | tf_op jit(solution)/shard_map/ppermute | solution.py:378
  69.9 8.1 %collective-permute-start.11 = (bf16[384,256]{1,0:T(8,128)(2,1)}, bf16[384,256]{1,0:T(8,128)(2,1)S(1)}, u32[]{:S(2)}, u32[]{:S(2)}) collective-permute-start(bf16[384,256]{1,0:T(8,128)(2,1)} %collective-permute-done.9.refs_4_), channel_id=1, source_target_pairs={{0,1},{1,2},{2,3},{3,4},{4,5},{5,6},{6,7},{7,0},{8,9},{9,10},{10,1... | collective-permute-start | bytes 589832 | tf_op jit(solution)/shard_map/ppermute | solution.py:374
  74.0 29.3 %collective-permute-start.12 = (bf16[1536,256]{1,0:T(8,128)(2,1)}, bf16[1536,256]{1,0:T(8,128)(2,1)}, u32[]{:S(2)}, u32[]{:S(2)}) collective-permute-start(bf16[1536,256]{1,0:T(8,128)(2,1)} %pad_maximum_fusion), channel_id=1, source_target_pairs={{0,32},{32,0},{1,33},{33,1},{2,34},{34,2},{3,35},{35,3},{4,36},{36... | collective-permute-start | bytes 2359304 | tf_op jit(solution)/shard_map/ppermute | solution.py:383
  80.6 22.7 %collective-permute-start.13 = (bf16[1152,256]{1,0:T(8,128)(2,1)}, bf16[1152,256]{1,0:T(8,128)(2,1)}, u32[]{:S(2)}, u32[]{:S(2)}) collective-permute-start(bf16[1152,256]{1,0:T(8,128)(2,1)} %pad_maximum_fusion.2), channel_id=1, source_target_pairs={{0,32},{32,0},{1,33},{33,1},{2,34},{34,2},{3,35},{35,3},{4,36},{36... | collective-permute-start | bytes 1769480 | tf_op jit(solution)/shard_map/ppermute | solution.py:383
  86.5 11.8 %collective-permute-start.1 = (bf16[256,128]{1,0:T(8,128)(2,1)}, bf16[256,128]{1,0:T(8,128)(2,1)S(1)}, u32[]{:S(2)}, u32[]{:S(2)}) collective-permute-start(bf16[256,128]{1,0:T(8,128)(2,1)} %get-tuple-element.23), channel_id=1, source_target_pairs={{0,256},{64,320},{128,384},{192,448},{256,0},{320,64},{384,128},{4... | collective-permute-start | bytes 196616 | tf_op jit(solution)/shard_map/ppermute | solution.py:439
  94.1 46.3 %all-to-all-start.2 = ((bf16[16,8,512]{2,1,0:T(8,128)(2,1)}), bf16[16,8,512]{2,1,0:T(8,128)(2,1)}, u32[]{:S(2)}, u32[]{:S(2)}) async-start(bf16[16,8,512]{2,1,0:T(8,128)(2,1)} %copy-done.17), calls=%async_computation.2 | async-start | bytes 262144 | tf_op jit(solution)/shard_map/all_to_all | solution.py:401
  99.1 27.8 %collective-permute-start.2 = (bf16[512,128]{1,0:T(8,128)(2,1)S(1)}, bf16[512,128]{1,0:T(8,128)(2,1)S(1)}, u32[]{:S(2)}, u32[]{:S(2)}) collective-permute-start(bf16[512,128]{1,0:T(8,128)(2,1)S(1)} %pad_maximum_fusion.5), channel_id=1, source_target_pairs={{0,128},{64,192},{128,0},{192,64},{256,384},{320,448},{384,256},{4... | collective-permute-start | bytes 393224 | tf_op jit(solution)/shard_map/ppermute | solution.py:439
  116.1 20.7 %copy-start.6 = (bf16[768,256]{1,0:T(8,128)(2,1)}, bf16[768,256]{1,0:T(8,128)(2,1)S(1)}, u32[]{:S(2)}) copy-start(bf16[768,256]{1,0:T(8,128)(2,1)S(1)} %get-tuple-element.29.own_joined_ref) | copy-start | bytes 1179652
  116.1 20.7 %copy-start.8 = (bf16[768,256]{1,0:T(8,128)(2,1)}, bf16[768,256]{1,0:T(8,128)(2,1)S(1)}, u32[]{:S(2)}) copy-start(bf16[768,256]{1,0:T(8,128)(2,1)S(1)} %get-tuple-element.31.refs_4_) | copy-start | bytes 1179652
  116.1 14.8 %collective-permute-start.16 = (bf16[384,256]{1,0:T(8,128)(2,1)S(1)}, bf16[384,256]{1,0:T(8,128)(2,1)S(1)}, u32[]{:S(2)}, u32[]{:S(2)}) collective-permute-start(bf16[384,256]{1,0:T(8,128)(2,1)S(1)} %get-tuple-element.30), channel_id=1, source_target_pairs={{0,16},{8,24},{16,0},{24,8},{1,17},{9,25},{17,1},{25,9},{2,18},{10... | collective-permute-start | bytes 589832 | tf_op jit(solution)/shard_map/ppermute | solution.py:432
  120.8 10.1 %collective-permute-start.15 = (bf16[384,256]{1,0:T(8,128)(2,1)S(1)}, bf16[384,256]{1,0:T(8,128)(2,1)S(1)}, u32[]{:S(2)}, u32[]{:S(2)}) collective-permute-start(bf16[384,256]{1,0:T(8,128)(2,1)S(1)} %get-tuple-element.30), channel_id=1, source_target_pairs={{0,24},{8,0},{16,8},{24,16},{1,25},{9,1},{17,9},{25,17},{2,26},{10... | collective-permute-start | bytes 589832 | tf_op jit(solution)/shard_map/ppermute | solution.py:432
  123.5 8.3 %collective-permute-start.14 = (bf16[384,256]{1,0:T(8,128)(2,1)S(1)}, bf16[384,256]{1,0:T(8,128)(2,1)S(1)}, u32[]{:S(2)}, u32[]{:S(2)}) collective-permute-start(bf16[384,256]{1,0:T(8,128)(2,1)S(1)} %get-tuple-element.30), channel_id=1, source_target_pairs={{0,8},{8,16},{16,24},{24,0},{1,9},{9,17},{17,25},{25,1},{2,10},{10... | collective-permute-start | bytes 589832 | tf_op jit(solution)/shard_map/ppermute | solution.py:432
  127.8 9.0 %collective-permute-start.3 = (bf16[1024,128]{1,0:T(8,128)(2,1)S(1)}, bf16[1024,128]{1,0:T(8,128)(2,1)S(1)}, u32[]{:S(2)}, u32[]{:S(2)}) collective-permute-start(bf16[1024,128]{1,0:T(8,128)(2,1)S(1)} %pad_maximum_fusion.4), channel_id=1, source_target_pairs={{0,64},{64,0},{128,192},{192,128},{256,320},{320,256},{384,448},{4... | collective-permute-start | bytes 786440 | tf_op jit(solution)/shard_map/ppermute | solution.py:439
  132.7 36.8 %collective-permute-start.17 = (bf16[1152,256]{1,0:T(8,128)(2,1)}, bf16[1152,256]{1,0:T(8,128)(2,1)}, u32[]{:S(2)}, u32[]{:S(2)}) collective-permute-start(bf16[1152,256]{1,0:T(8,128)(2,1)} %pad_maximum_fusion.3), channel_id=1, source_target_pairs={{0,32},{32,0},{1,33},{33,1},{2,34},{34,2},{3,35},{35,3},{4,36},{36... | collective-permute-start | bytes 1769480 | tf_op jit(solution)/shard_map/ppermute | solution.py:433
  136.8 46.4 %collective-permute-start.4 = (bf16[2048,128]{1,0:T(8,128)(2,1)S(1)}, bf16[2048,128]{1,0:T(8,128)(2,1)}, u32[]{:S(2)}, u32[]{:S(2)}) collective-permute-start(bf16[2048,128]{1,0:T(8,128)(2,1)S(1)} %constant_dynamic-update-slice_fusion.own_ref), channel_id=1, source_target_pairs={{0,32},{32,0},{1,33},{33,1},{2,34},{34,2},{3,35},{35,3},{4,36},{36... | collective-permute-start | bytes 1572872 | tf_op jit(solution)/shard_map/ppermute | solution.py:443
  141.9 13.7 %all-to-all-start.3 = ((bf16[8,8,512]{2,1,0:T(8,128)(2,1)}), bf16[8,8,512]{2,1,0:T(8,128)(2,1)S(1)}, u32[]{:S(2)}, u32[]{:S(2)}) async-start(bf16[8,8,512]{2,1,0:T(8,128)(2,1)} %copy-done.10), calls=%async_computation.3 | async-start | bytes 131072 | tf_op jit(solution)/shard_map/all_to_all | solution.py:40
  161.9 7.6 %all-to-all-start.4 = ((bf16[4,8,512]{2,1,0:T(8,128)(2,1)}), bf16[4,8,512]{2,1,0:T(8,128)(2,1)S(1)}, u32[]{:S(2)}, u32[]{:S(2)}) async-start(bf16[4,8,512]{2,1,0:T(8,128)(2,1)} %copy-done.18), calls=%async_computation.4 | async-start | bytes 65536 | tf_op jit(solution)/shard_map/all_to_all | solution.py:40
  175.3 16.8 %all-to-all-start.5 = ((bf16[16,8,512]{2,1,0:T(8,128)(2,1)}), bf16[16,8,512]{2,1,0:T(8,128)(2,1)S(1)}, u32[]{:S(2)}, u32[]{:S(2)}) async-start(bf16[16,8,512]{2,1,0:T(8,128)(2,1)} %copy-done.5), calls=%async_computation.5 | async-start | bytes 262144 | tf_op jit(solution)/shard_map/all_to_all | solution.py:485
  184.9 7.2 %copy-start.26 = (bf16[256,256]{1,0:T(8,128)(2,1)S(1)}, bf16[256,256]{1,0:T(8,128)(2,1)}, u32[]{:S(2)}) copy-start(bf16[256,256]{1,0:T(8,128)(2,1)} %copy-done.25) | copy-start | bytes 393220
  184.9 7.2 %copy-start.28 = (bf16[256,256]{1,0:T(8,128)(2,1)S(1)}, bf16[256,256]{1,0:T(8,128)(2,1)}, u32[]{:S(2)}) copy-start(bf16[256,256]{1,0:T(8,128)(2,1)} %copy-done.27) | copy-start | bytes 393220
  212.8 3.9 %collective-permute-start.18 = (bf16[2048,128]{1,0:T(8,128)(2,1)S(1)}, bf16[2048,128]{1,0:T(8,128)(2,1)S(1)}, u32[]{:S(2)}, u32[]{:S(2)}) collective-permute-start(bf16[2048,128]{1,0:T(8,128)(2,1)S(1)} %bitcast.80), channel_id=1, source_target_pairs={{0,32},{32,0},{1,33},{33,1},{2,34},{34,2},{3,35},{35,3},{4,36},{36... | collective-permute-start | bytes 1572872 | tf_op jit(solution)/shard_map/ppermute | solution.py:490
  (23 other events, 29.2 us)

commit v4 on v2

v4 whole, which is shorter than its diff:
```python
import functools

import jax
import jax.numpy as jnp
from jax import lax
from jax.experimental import pallas as pl
from jax.experimental.pallas import tpu as pltpu
from jax.sharding import Mesh
from jax.sharding import PartitionSpec as P


F32 = jnp.float32
BF16 = jnp.bfloat16
GRP = ("z", "c")
NT = (((1,), (1,)), ((), ()))
VM = pl.BlockSpec(memory_space=pltpu.VMEM)
SM = pl.BlockSpec(memory_space=pltpu.SMEM)
PARAMS = pltpu.CompilerParams(vmem_limit_bytes=16 * 1024 * 1024)


def call(kernel, name, outs, scratch, smem, cost, *args):
    specs = [SM] * smem + [VM] * (len(args) - smem)
    flops, moved = cost
    return pl.pallas_call(
        kernel,
        name=name,
        out_shape=outs,
        in_specs=specs,
        out_specs=jax.tree.map(lambda _: VM, outs),
        scratch_shapes=scratch,
        compiler_params=PARAMS,
        cost_estimate=pl.CostEstimate(flops=flops, bytes_accessed=moved, transcendentals=0),
    )(*args)


def spread_rows(pos, map_ref, load_ref, keep_ref, send_ref, contrib, rows):
    contrib[...] = (
        jnp.dot(map_ref[...], load_ref[...], preferred_element_type=F32).astype(BF16).astype(F32)
    )
    rows[...] = jnp.zeros_like(rows)
    count = contrib.shape[0]
    unroll = 16

    def some(turn, carry):
        base = pl.multiple_of(turn * unroll, unroll)
        for k in range(unroll):
            rows[pl.ds(pos[base + k], 1), :] = contrib[pl.ds(base + k, 1), :]
        return carry

    lax.fori_loop(0, count // unroll, some, 0)
    half = keep_ref.shape[0]
    keep_ref[...] = rows[:half].astype(BF16)
    send_ref[...] = rows[half:].astype(BF16)


def sort_maps(got_ref, maps_ref):
    peers, _, n = got_ref.shape
    nodes = n // peers
    for g in range(peers):
        for k in range(3):
            maps_ref[k * n + g * nodes : k * n + (g + 1) * nodes] = got_ref[
                g, k * nodes : (k + 1) * nodes
            ]


def face_parts(parts_ref, rows_ref, loads_ref, out_ref, order):
    total = parts_ref[0].astype(F32)
    for z in range(1, parts_ref.shape[0]):
        total = total + parts_ref[z].astype(F32)
    loads = total.astype(BF16)
    loads_ref[...] = loads
    peers, five, _ = rows_ref.shape
    nodes = five // 5
    for g in range(peers):
        order[g * nodes : (g + 1) * nodes] = rows_ref[g, 3 * nodes : 4 * nodes]
        order[(peers + g) * nodes : (peers + g + 1) * nodes] = rows_ref[g, 4 * nodes : five]
    lines = lax.dot_general(total.T.astype(BF16), order[...], NT, preferred_element_type=F32)
    part = out_ref.shape[1]
    for g in range(peers):
        out_ref[g] = lines[g * part : (g + 1) * part].astype(BF16)


def face_sum(got_ref, out_ref):
    total = got_ref[0].astype(F32)
    for g in range(1, got_ref.shape[0]):
        total = total + got_ref[g].astype(F32)
    line = total.astype(BF16)
    for y in range(out_ref.shape[0]):
        out_ref[y] = line


def halves(value):
    high = value.astype(BF16)
    low = (value - high.astype(F32)).astype(BF16)
    return high, low


def exact_right(left, value):
    high, low = halves(value)
    return jnp.dot(left, high, preferred_element_type=F32) + jnp.dot(
        left, low, preferred_element_type=F32
    )


def exact_rows(value, right):
    rows = value.shape[0]
    high, low = halves(value)
    both = lax.dot_general(
        jnp.concatenate([high, low], axis=0), right, NT, preferred_element_type=F32
    )
    return both[:rows] + both[rows:]


def run_block(place, faces_ref, maps_ref, ends_ref, own_maps_ref, own_ref, *scratch):
    state, right, through, given, sources = scratch
    count, part, _ = faces_ref.shape
    n = maps_ref.shape[2]
    here = place[0]
    unit = (
        lax.broadcasted_iota(jnp.int32, (n, n), 0) == lax.broadcasted_iota(jnp.int32, (n, n), 1)
    ).astype(F32)
    state[...] = unit
    right[:, 0:n] = unit
    right[:, n : 2 * n] = jnp.zeros((n, n), F32)
    given[...] = jnp.zeros_like(given)

    def onward(j, carry):
        value = state[...]
        east = given[:, 0:n]

        @pl.when(j == here)
        def _():
            own_maps_ref[0:n] = value.astype(BF16)
            own_ref[:, 0:n] = east

        maps = maps_ref[j, 0 : 2 * n, :]
        both = exact_right(maps, value)
        moved = faces_ref[j].astype(F32) + exact_rows(east, maps)
        state[...] = both[:n]
        through[j] = both[n:]
        given[:, 0:n] = moved[:, 0:n]
        sources[j] = moved[:, n : 2 * n]
        return carry

    lax.fori_loop(0, count, onward, 0)

    def back(turn, carry):
        j = count - 1 - turn
        value = right[...]
        west = given[:, n : 2 * n]

        @pl.when(j == here)
        def _():
            own_maps_ref[n : 2 * n] = value[:, 0:n].astype(BF16)
            own_maps_ref[2 * n : 3 * n] = value[:, n : 2 * n].astype(BF16)
            own_ref[:, n : 2 * n] = west

        maps = maps_ref[j, 2 * n : 3 * n, :]
        both = exact_right(maps, value)
        moved = sources[j] + exact_rows(west, maps)
        right[:, 0:n] = both[:, 0:n]
        right[:, n : 2 * n] = both[:, n : 2 * n] + through[j]
        given[:, n : 2 * n] = moved
        return carry

    lax.fori_loop(0, count, back, 0)
    ends = jnp.concatenate([given[:, 0:n], given[:, n : 2 * n]], axis=0).astype(BF16)
    for x in range(ends_ref.shape[0]):
        ends_ref[x, 0:n] = state[...].astype(BF16)
        ends_ref[x, n : 2 * n] = right[:, 0:n].astype(BF16)
        ends_ref[x, 2 * n : 3 * n] = right[:, n : 2 * n].astype(BF16)
        ends_ref[x, 3 * n : 3 * n + 2 * part] = ends


def meet_values(place, ends_ref, maps_ref, own_ref, out_ref, entering):
    count, _, n = ends_ref.shape
    part = own_ref.shape[0]
    here = place[0]
    east = jnp.zeros((part, n), F32)
    sources = []
    for b in range(count):

        @pl.when(here == b)
        def _(east=east):
            entering[:, 0:n] = east

        end = ends_ref[b, 3 * n : 3 * n + 2 * part].astype(F32)
        source = end[part : 2 * part]
        if b:
            source = source + exact_rows(east, ends_ref[b, 2 * n : 3 * n, :])
        sources.append(source)
        east = end[0:part] + (exact_rows(east, ends_ref[b, 0:n, :]) if b else 0.0)
    west = jnp.zeros((part, n), F32)
    for b in range(count - 1, -1, -1):

        @pl.when(here == b)
        def _(west=west):
            entering[:, n : 2 * n] = west

        west = sources[b] + (
            exact_rows(west, ends_ref[b, n : 2 * n, :]) if b < count - 1 else 0.0
        )
    east = entering[:, 0:n]
    west = entering[:, n : 2 * n]
    own = own_ref[...]
    met_east = own[:, 0:n] + exact_rows(east, maps_ref[0:n])
    met_west = (
        own[:, n : 2 * n]
        + exact_rows(west, maps_ref[n : 2 * n])
        + exact_rows(east, maps_ref[2 * n : 3 * n])
    )
    met = jnp.concatenate([met_east, met_west], axis=1).astype(BF16)
    for g in range(out_ref.shape[0]):
        out_ref[g] = met


def leaf_result(pos, own_ref, other_ref, map_ref, load_ref, out_ref, rows, picked):
    half = own_ref.shape[0]
    rows[0:half] = own_ref[...].astype(F32)
    rows[half : 2 * half] = other_ref[...].astype(F32)
    count = picked.shape[0]
    unroll = 16

    def some(turn, carry):
        base = pl.multiple_of(turn * unroll, unroll)
        for k in range(unroll):
            picked[pl.ds(base + k, 1), :] = rows[pl.ds(pos[base + k], 1), :]
        return carry

    lax.fori_loop(0, count // unroll, some, 0)
    turned = picked[...].T.astype(BF16)
    result = jnp.dot(turned, map_ref[...], preferred_element_type=F32)
    out_ref[...] = (result.T + load_ref[...].astype(F32)).astype(BF16)


def on_device(leaf_load, leaf_map, group_map, node_index, west_coupling, east_coupling):
    local_map, local_load, nodes_of = leaf_map[0, 0], leaf_load[0, 0], node_index[0, 0]
    rows_map, west, east = group_map[0], west_coupling[0], east_coupling[0]
    nz, nc = lax.axis_size("z"), lax.axis_size("c")
    nx, ny = lax.axis_size("x"), lax.axis_size("y")
    peers = nz * nc
    leaf_nodes, columns = local_load.shape
    width, interface = rows_map.shape
    n = west.shape[0]
    stride = interface // n
    nodes = n // peers
    part = columns // peers
    half = interface // nc
    side = lax.axis_index("c")
    at_y = jnp.reshape(lax.axis_index("y"), (1,)).astype(jnp.int32)
    at_x = jnp.reshape(lax.axis_index("x"), (1,)).astype(jnp.int32)
    swap = [(0, 1), (1, 0)]

    spot = lax.broadcasted_iota(jnp.int32, (interface, 2 * n), 0)
    want = lax.broadcasted_iota(jnp.int32, (interface, 2 * n), 1)
    want = jnp.where(want < n, want * stride, (want - n) * stride + 1)
    face_map = jnp.dot(rows_map, (spot == want).astype(BF16), preferred_element_type=F32)
    west_high, west_low = halves(west)
    east_high, east_low = halves(east)
    face_low = face_map.astype(BF16)
    coupled = jnp.concatenate(
        [
            jnp.dot(face_low[:, :n], west_high, preferred_element_type=F32)
            + jnp.dot(face_low[:, :n], west_low, preferred_element_type=F32),
            jnp.dot(face_low[:, n:], east_high, preferred_element_type=F32)
            + jnp.dot(face_low[:, n:], east_low, preferred_element_type=F32),
        ],
        axis=1,
    ).astype(BF16)
    steps = coupled.reshape(nodes, stride, 2 * n)
    slices = jnp.concatenate([steps[:, 1, :n], steps[:, 0, :n], steps[:, 0, n:]], axis=0)
    slices = jnp.broadcast_to(slices, (peers,) + slices.shape)
    rows = rows_map.reshape(nodes, stride, interface)
    rows = jnp.concatenate([rows[:, 1], rows[:, 0]], axis=0)
    rows = rows.reshape(2 * nodes, peers, width).transpose(1, 0, 2)
    pieces = lax.all_to_all(jnp.concatenate([slices, rows], axis=1), GRP, 0, 0)

    owner = nodes_of // width
    pos = ((owner % nc) ^ side) * half + (owner // nc) * width + nodes_of % width
    keep, send = call(
        spread_rows,
        "spread_rows",
        (jax.ShapeDtypeStruct((half, columns), BF16),) * 2,
        [pltpu.VMEM((leaf_nodes, columns), F32), pltpu.VMEM((interface, columns), F32)],
        1,
        (2 * leaf_nodes * leaf_nodes * columns, 6 * leaf_nodes * leaf_nodes),
        pos,
        local_map,
        local_load,
    )
    got = lax.ppermute(send, "c", swap)
    paired = (keep.astype(F32) + got.astype(F32)).astype(BF16)
    pieces, paired = lax.optimization_barrier((pieces, paired))
    maps = call(
        sort_maps,
        "sort_maps",
        jax.ShapeDtypeStruct((3 * n, n), BF16),
        [],
        0,
        (1000, 16 * n * n),
        pieces,
    )
    run_maps = lax.all_gather(maps, "y")

    parts = lax.all_to_all(paired.reshape(nz, width, columns), "z", 0, 0)
    loads, faces = call(
        face_parts,
        "face_parts",
        (
            jax.ShapeDtypeStruct((width, columns), BF16),
            jax.ShapeDtypeStruct((peers, part, 2 * n), BF16),
        ),
        [pltpu.VMEM((2 * n, width), BF16)],
        0,
        (4 * n * width * columns, 4 * n * width),
        parts,
        pieces,
    )
    faces = lax.all_to_all(faces, GRP, 0, 0)
    line = call(
        face_sum,
        "face_sum",
        jax.ShapeDtypeStruct((ny, part, 2 * n), BF16),
        [],
        0,
        (1000, 4 * n * columns),
        faces,
    )

    all_loads = lax.all_gather(loads, GRP, axis=0, tiled=True)

    line = lax.all_to_all(line, "y", 0, 0)
    ends, own_maps, own_values = call(
        run_block,
        "run_block",
        (
            jax.ShapeDtypeStruct((nx, 3 * n + 2 * part, n), BF16),
            jax.ShapeDtypeStruct((3 * n, n), BF16),
            jax.ShapeDtypeStruct((part, 2 * n), F32),
        ),
        [
            pltpu.VMEM((n, n), F32),
            pltpu.VMEM((n, 2 * n), F32),
            pltpu.VMEM((ny, n, n), F32),
            pltpu.VMEM((part, 2 * n), F32),
            pltpu.VMEM((ny, part, n), F32),
        ],
        1,
        (16 * ny * n**3, 6 * ny * n * n),
        at_y,
        line,
        run_maps,
    )
    ends = lax.all_to_all(ends, "x", 0, 0)
    met = call(
        meet_values,
        "meet_values",
        jax.ShapeDtypeStruct((peers, part, 2 * n), BF16),
        [pltpu.VMEM((part, 2 * n), F32)],
        1,
        (12 * nx * n * n * 16, 6 * nx * n * n),
        at_x,
        ends,
        own_maps,
        own_values,
    )
    met_blocks = lax.all_to_all(met, GRP, 0, 0)

    all_loads, _ = lax.optimization_barrier((all_loads, met))
    initial = jnp.dot(rows_map, all_loads, preferred_element_type=F32)
    met = met_blocks.reshape(columns, 2 * n)
    final = initial + lax.dot_general(coupled, met, NT, preferred_element_type=F32)
    final = jnp.broadcast_to(final.astype(BF16), (nz, width, columns))
    final_own = lax.all_to_all(final, "z", 0, 0).reshape(half, columns)
    final_other = lax.ppermute(final_own, "c", swap)
    result = call(
        leaf_result,
        "leaf_result",
        jax.ShapeDtypeStruct((leaf_nodes, columns), BF16),
        [pltpu.VMEM((interface, columns), F32), pltpu.VMEM((leaf_nodes, columns), F32)],
        1,
        (2 * leaf_nodes * leaf_nodes * columns, 2 * leaf_nodes * leaf_nodes),
        pos,
        final_own,
        final_other,
        local_map,
        local_load,
    )
    return result[None, None]


SPLITS = {(16, 32): (8, 2, 4, 8)}


def solution(mesh):
    shape = SPLITS.get(tuple(mesh.devices.shape), (2, 2, 2, 2))
    split = Mesh(mesh.devices.reshape(shape), ("z", "c", "x", "y"))
    grp, dom = ("z", "c"), ("x", "y")
    return jax.shard_map(
        on_device,
        mesh=split,
        in_specs=(
            P(dom, grp, None, None),
            P(dom, grp, None, None),
            P(dom, grp, None),
            P(dom, grp, None),
            P(dom, None, None),
            P(dom, None, None),
        ),
        out_specs=P(dom, grp, None, None),
        check_vma=False,
    )
```

time: 210 us -> 183 us (0.87)
  blocking collectives: 73.2 us -> 52.8 us
  local copies, waits for them, and re-layouts: 14.2 us -> 6.74 us
  waiting for transfers between devices: 47.9 us -> 50.3 us
    all_to_all x4, waiting for transfers between devices: 27.6 us -> 47 us  [the longest x1 20.1 us: on_device(): ends = lax.all_to_all(ends, 'x', 0, 0)]
    all_gather x1, waiting for transfers between devices: 18.7 us -> 0.01 us  [on_device(): run_maps = lax.all_gather(maps, 'y')]
    all_to_all x3 -> x1, blocking collectives: 35.1 us -> 20.3 us  [on_device(): parts = lax.all_to_all(paired.reshape(nz, width, columns), 'z', 0, 0)]
    ppermute x1 -> x0, starting transfers between devices: 6.77 us -> none  [on_device(): loads_other = lax.ppermute(loads_own, 'c', swap)]
    unnamed x29 -> x25, local copies, waits for them, and re-layouts: 9.83 us -> 3.71 us
    all_to_all x4, starting transfers between devices: 23.2 us -> 29.1 us  [the longest x1 11.8 us: on_device(): pieces = lax.all_to_all(jnp.concatenate([slices, rows], axis=1), GRP, 0, 0)]
    all_to_all x1, blocking collectives: 17.7 us -> 12.1 us  [on_device(): faces = lax.all_to_all(faces, GRP, 0, 0)]
    dot_general x0 -> x1, matrix products: none -> 2.73 us  [on_device(): initial = jnp.dot(rows_map, all_loads, preferred_element_type=F32)]
  transfers between devices with their start and end apart: 9 -> 8, of which waited for: 5 -> 6; matrix products, arithmetic and copies ran while one was open for 3% -> 2% of each run, Pallas kernels for 7% -> 7%
where the time goes in v4:
time: 183 us; the launch traced here: 182 us
  blocking collectives  52.8 us (29%)
  waiting for transfers between devices  50.3 us (27%)
  starting transfers between devices  33.5 us (18%)
  Pallas kernels  17.1 us (9%)
  between operations  13.7 us (7%)
  matrix products  6.8 us (4%)
  local copies, waits for them, and re-layouts  6.74 us (4%)
    all_to_all x1, blocking collectives, on_device(): final_own = lax.all_to_all(final, 'z', 0, 0).reshape(half, columns)  20.4 us
    all_to_all x1, blocking collectives, on_device(): parts = lax.all_to_all(paired.reshape(nz, width, columns), 'z', 0, 0)  20.3 us
    all_to_all x1, waiting for transfers between devices, on_device(): ends = lax.all_to_all(ends, 'x', 0, 0)  20.1 us
    pallas_call x7, Pallas kernels, call(): pl.pallas_call(kernel, name=name, out_shape=outs, in_specs=specs, out_spe...  17.1 us
    all_to_all x1, waiting for transfers between devices, on_device(): pieces = lax.all_to_all(jnp.concatenate([slices, rows], axis=1), GRP, 0, 0)  13.3 us
    all_to_all x1, blocking collectives, on_device(): faces = lax.all_to_all(faces, GRP, 0, 0)  12.1 us
    all_to_all x1, starting transfers between devices, on_device(): pieces = lax.all_to_all(jnp.concatenate([slices, rows], axis=1), GRP, 0, 0)  11.8 us
    all_to_all x1, waiting for transfers between devices, on_device(): line = lax.all_to_all(line, 'y', 0, 0)  7.47 us
  transfers between devices with their start and end apart: 8, of which 6 were waited for; matrix products, arithmetic and copies ran while one was open for 2% of the time, Pallas kernels for 7%

profile of v4, /device:TPU:1, one launch (start us, length us, event | category | flops | bytes accessed | tf_op | source)
XLA Modules:
  0.0 182.1 jit_solution(14671800279901153176)
XLA Ops:
  6.6 3.0 %fusion.14 = bf16[256,512]{0,1:T(8,128)(2,1)S(1)} fusion(bf16[1,256,4096]{2,1,0:T(8,128)(2,1)} %param.8, s32[512]{0:T(512)S(1)} %get-tuple-element.32, s32[512]{0:T(512)S(1)} %get-tuple-element.31, pred[512]{0:T(512)(128)(4,1)S(1)} %iota_compare_fusion), kind=kOutput, calls=%fused_computation.10 | convolution fusion | flops 1080164352 | bytes 2363904 | tf_op jit(solution)/shard_map/dot_general | solution.py:257
  9.8 0.2 fusion.19
  10.3 0.2 fusion.20
  10.6 0.5 copy-done.8
  11.2 2.8 %slice_reduce_fusion.1 = (bf16[16,4096]{1,0:T(8,128)(2,1)S(1)}, bf16[16,4096]{1,0:T(8,128)(2,1)S(1)}) fusion(bf16[16,16,4096]{2,1,0:T(8,128)(2,1)} %bitcast.93), kind=kLoop, calls=%fused_computation.21 | loop fusion | bytes 524288 | tf_op jit(solution)/shard_map/slice | solution.py:274
  14.1 0.9 pad_maximum_fusion
  15.0 11.8 %all-to-all-start = ((bf16[16,80,256]{2,1,0:T(8,128)(2,1)}), bf16[16,80,256]{2,1,0:T(8,128)(2,1)S(1)}, u32[]{:S(2)}, u32[]{:S(2)}) async-start(bf16[16,80,256]{2,1,0:T(8,128)(2,1)} %pad_maximum_fusion), calls=%async_computation | async-start | bytes 1310720 | tf_op jit(solution)/shard_map/all_to_all | solution.py:276
  26.9 2.6 %spread_rows.1 = (bf16[2048,128]{1,0:T(8,128)(2,1)S(1)}, bf16[2048,128]{1,0:T(8,128)(2,1)S(1)}) custom-call(s32[1024]{0:T(1024)S(1)} %fusion.42.pos, bf16[1024,1024]{1,0:T(8,128)(2,1)S(1)} %bitcast.86, bf16[1024,128]{1,0:T(8,128)(2,1)S(1)} %bitcast.90), custom_call_target="tpu_custom_call" | custom-call | flops 268435456 | bytes 6291456 | tf_op jit(solution)/shard_map/spread_rows/pallas_call | solution.py:24
  29.5 2.0 %collective-permute-start = (bf16[2048,128]{1,0:T(8,128)(2,1)S(1)}, bf16[2048,128]{1,0:T(8,128)(2,1)S(1)}, u32[]{:S(2)}, u32[]{:S(2)}) collective-permute-start(bf16[2048,128]{1,0:T(8,128)(2,1)S(1)} %get-tuple-element.16), channel_id=1, source_target_pairs={{0,32},{32,0},{1,33},{33,1},{2,34},{34,2},{3,35},{35,3},{4,36},{36... | collective-permute-start | bytes 1572872 | tf_op jit(solution)/shard_map/ppermute | solution.py:291
  31.5 1.8 collective-permute-done
  33.4 13.3 %all-to-all-done.rows_ref.got_ref = bf16[16,80,256]{2,1,0:T(8,128)(2,1)S(1)} async-done(((bf16[16,80,256]{2,1,0:T(8,128)(2,1)}), bf16[16,80,256]{2,1,0:T(8,128)(2,1)S(1)}, u32[]{:S(2)}, u32[]{:S(2)}) %all-to-all-start) | async-done | bytes 655392 | tf_op jit(solution)/shard_map/all_to_all | solution.py:276
  46.7 0.8 sort_maps.1
  47.6 20.3 %all_to_all.35.parts_ref = bf16[8,256,128]{2,1,0:T(8,128)(2,1)S(1)} all-to-all(bf16[8,256,128]{2,1,0:T(8,128)(2,1)S(1)} %bitcast.94), channel_id=1, replica_groups=mesh['z'=8,'c'=2,'x'=4,'y'=8] {'z'}, dimensions={0} | all-to-all | bytes 1048576 | tf_op jit(solution)/shard_map/all_to_all | solution.py:305
  67.9 0.7 face_parts.1
  68.6 12.1 %all_to_all.36.got_ref = bf16[16,8,512]{2,1,0:T(8,128)(2,1)S(1)} all-to-all(bf16[16,8,512]{2,1,0:T(8,128)(2,1)S(1)} %get-tuple-element.20), channel_id=1, replica_groups=mesh['z'=8,'c'=2,'x'=4,'y'=8] {'z','c'}, dimensions={0} | all-to-all | bytes 262144 | tf_op jit(solution)/shard_map/all_to_all | solution.py:319
  80.8 0.6 face_sum.1
  81.4 6.8 %all-to-all-start.3 = ((bf16[8,8,512]{2,1,0:T(8,128)(2,1)}), bf16[8,8,512]{2,1,0:T(8,128)(2,1)S(1)}, u32[]{:S(2)}, u32[]{:S(2)}) async-start(bf16[8,8,512]{2,1,0:T(8,128)(2,1)} %face_sum.1), calls=%async_computation.3 | async-start | bytes 131072 | tf_op jit(solution)/shard_map/all_to_all | solution.py:332
  88.2 7.5 %all-to-all-done.3.faces_ref = bf16[8,8,512]{2,1,0:T(8,128)(2,1)S(1)} async-done(((bf16[8,8,512]{2,1,0:T(8,128)(2,1)}), bf16[8,8,512]{2,1,0:T(8,128)(2,1)S(1)}, u32[]{:S(2)}, u32[]{:S(2)}) %all-to-all-start.3) | async-done | bytes 65568 | tf_op jit(solution)/shard_map/all_to_all | solution.py:332
  95.7 1.9 %copy-done.3 = bf16[6144,256]{1,0:T(8,128)(2,1)S(1)} copy-done((bf16[6144,256]{1,0:T(8,128)(2,1)S(1)}, bf16[6144,256]{1,0:T(8,128)(2,1)}, u32[]{:S(2)}) %copy-start.3) | copy-done | bytes 3145752
  97.6 6.0 %run_block.1 = (bf16[4,784,256]{2,1,0:T(8,128)(2,1)S(1)}, bf16[768,256]{1,0:T(8,128)(2,1)S(1)}, f32[8,512]{1,0:T(8,128)S(1)}) custom-call(s32[1]{0:T(128)} %bitcast.16.place, bf16[8,8,512]{2,1,0:T(8,128)(2,1)S(1)} %all-to-all-done.3.faces_ref, bf16[8,768,256]{2,1,0:T(8,128)(2,1)S(1)} %bitcast.92), custom_call_target="tpu_custom_call" | custom-call | flops 2147483648 | bytes 3145728 | tf_op jit(solution)/shard_map/run_block/pallas_call | solution.py:24
  103.6 1.1 copy-done.1
  104.8 4.4 %all-to-all-start.4 = ((bf16[4,784,256]{2,1,0:T(8,128)(2,1)}), bf16[4,784,256]{2,1,0:T(8,128)(2,1)}, u32[]{:S(2)}, u32[]{:S(2)}) async-start(bf16[4,784,256]{2,1,0:T(8,128)(2,1)} %copy-done.1), calls=%async_computation.4 | async-start | bytes 3211264 | tf_op jit(solution)/shard_map/all_to_all | solution.py:354
  109.2 20.1 %all-to-all-done.4.ends_ref = bf16[4,784,256]{2,1,0:T(8,128)(2,1)} async-done(((bf16[4,784,256]{2,1,0:T(8,128)(2,1)}), bf16[4,784,256]{2,1,0:T(8,128)(2,1)}, u32[]{:S(2)}, u32[]{:S(2)}) %all-to-all-start.4) | async-done | bytes 1605664 | tf_op jit(solution)/shard_map/all_to_all | solution.py:354
  129.2 3.3 %meet_values.1 = bf16[16,8,512]{2,1,0:T(8,128)(2,1)} custom-call(s32[1]{0:T(128)} %bitcast.15.place, bf16[4,784,256]{2,1,0:T(8,128)(2,1)} %all-to-all-done.4.ends_ref, bf16[768,256]{1,0:T(8,128)(2,1)S(1)} %get-tuple-element.22.maps_ref, f32[8,512]{1,0:T(8,128)S(1)} %get-tuple-element.23.own_ref), custom_call_target="tpu_custom_call" | custom-call | flops 50331648 | bytes 1572864 | tf_op jit(solution)/shard_map/meet_values/pallas_call | solution.py:24
  132.5 6.1 %all-to-all-start.5 = ((bf16[16,8,512]{2,1,0:T(8,128)(2,1)}), bf16[16,8,512]{2,1,0:T(8,128)(2,1)S(1)}, u32[]{:S(2)}, u32[]{:S(2)}) async-start(bf16[16,8,512]{2,1,0:T(8,128)(2,1)} %meet_values.1), calls=%async_computation.5 | async-start | bytes 262144 | tf_op jit(solution)/shard_map/all_to_all | solution.py:367
  138.6 2.7 %fusion.21 = f32[256,128]{0,1:T(8,128)S(1)} fusion(bf16[4096,128]{1,0:T(8,128)(2,1)} %all-gather.4.cloned.1.call-done, bf16[1,256,4096]{2,1,0:T(8,128)(2,1)} %param.8), kind=kOutput, calls=%fused_computation.16 | convolution fusion | flops 268435456 | bytes 3276800 | tf_op jit(solution)/shard_map/dot_general | solution.py:370
  141.3 6.1 %all-to-all-done.5 = bf16[16,8,512]{2,1,0:T(8,128)(2,1)S(1)} async-done(((bf16[16,8,512]{2,1,0:T(8,128)(2,1)}), bf16[16,8,512]{2,1,0:T(8,128)(2,1)S(1)}, u32[]{:S(2)}, u32[]{:S(2)}) %all-to-all-start.5) | async-done | bytes 131104 | tf_op jit(solution)/shard_map/all_to_all | solution.py:367
  147.5 0.2 fusion.24
  147.9 20.4 %all_to_all.37 = bf16[8,256,128]{2,1,0:T(8,128)(2,1)S(1)} all-to-all(bf16[8,256,128]{2,1,0:T(8,128)(2,1)S(1)} %broadcast_in_dim.10), channel_id=1, replica_groups=mesh['z'=8,'c'=2,'x'=4,'y'=8] {'z'}, dimensions={0} | all-to-all | bytes 1048576 | tf_op jit(solution)/shard_map/all_to_all | solution.py:374
  168.3 2.4 %collective-permute-start.1 = (bf16[2048,128]{1,0:T(8,128)(2,1)S(1)}, bf16[2048,128]{1,0:T(8,128)(2,1)S(1)}, u32[]{:S(2)}, u32[]{:S(2)}) collective-permute-start(bf16[2048,128]{1,0:T(8,128)(2,1)S(1)} %bitcast.88), channel_id=1, source_target_pairs={{0,32},{32,0},{1,33},{33,1},{2,34},{34,2},{3,35},{35,3},{4,36},{36... | collective-permute-start | bytes 1572872 | tf_op jit(solution)/shard_map/ppermute | solution.py:375
  170.7 1.5 collective-permute-done.1.other_ref
  172.2 3.1 %leaf_result.1 = bf16[1024,128]{1,0:T(8,128)(2,1)} custom-call(s32[1024]{0:T(1024)S(1)} %fusion.42.pos, bf16[2048,128]{1,0:T(8,128)(2,1)S(1)} %bitcast.89, bf16[2048,128]{1,0:T(8,128)(2,1)S(1)} %collective-permute-done.1.other_ref, bf16[1024,1024]{1,0:T(8,128)(2,1)S(1)} %bitcast.87, bf16[1024,128]{1,0:T(8,128)(2,1)S(1)} %bitcast.91), custom_call_target="tpu_custom_call" | custom-call | flops 268435456 | bytes 2097152 | tf_op jit(solution)/shard_map/leaf_result/pallas_call | solution.py:24
  (42 shorter events, 1.2 us)
Async XLA Ops:
  6.5 3.0 %copy-start.4 = (f32[1,256,256]{2,1,0:T(8,128)S(1)}, f32[1,256,256]{2,1,0:T(8,128)}, u32[]{:S(2)}) copy-start(f32[1,256,256]{2,1,0:T(8,128)} %param.10) | copy-start | bytes 786436
  6.5 3.5 %copy-start.5 = (f32[1,256,256]{2,1,0:T(8,128)S(1)}, f32[1,256,256]{2,1,0:T(8,128)}, u32[]{:S(2)}) copy-start(f32[1,256,256]{2,1,0:T(8,128)} %param.11) | copy-start | bytes 786436
  10.0 0.7 copy-start.6
  10.5 0.7 copy-start.8
  14.0 12.9 %copy-start.10 = (s32[1,1,1024]{2,1,0:T(1,128)S(1)}, s32[1,1,1024]{2,1,0:T(1,128)}, u32[]{:S(2)}) copy-start(s32[1,1,1024]{2,1,0:T(1,128)} %param.9) | copy-start | bytes 12292
  14.0 12.9 %copy-start = (bf16[1,1,1024,1024]{3,2,1,0:T(8,128)(2,1)S(1)}, bf16[1,1,1024,1024]{3,2,1,0:T(8,128)(2,1)}, u32[]{:S(2)}) copy-start(bf16[1,1,1024,1024]{3,2,1,0:T(8,128)(2,1)} %param.7) | copy-start | bytes 6291460
  14.0 12.9 %copy-start.2 = (bf16[1,1,1024,128]{3,2,1,0:T(8,128)(2,1)S(1)}, bf16[1,1,1024,128]{3,2,1,0:T(8,128)(2,1)}, u32[]{:S(2)}) copy-start(bf16[1,1,1024,128]{3,2,1,0:T(8,128)(2,1)} %param.6) | copy-start | bytes 786436
  15.0 31.8 %all-to-all-start = ((bf16[16,80,256]{2,1,0:T(8,128)(2,1)}), bf16[16,80,256]{2,1,0:T(8,128)(2,1)S(1)}, u32[]{:S(2)}, u32[]{:S(2)}) async-start(bf16[16,80,256]{2,1,0:T(8,128)(2,1)} %pad_maximum_fusion), calls=%async_computation | async-start | bytes 1310720 | tf_op jit(solution)/shard_map/all_to_all | solution.py:276
  26.8 68.9 %all-gather.6.cloned.1.call-start = ((), (), s32[]{:S(2)}) async-start(), calls=%async_computation.8 | async-start | bytes 3538944 | tf_op jit(solution)/shard_map/all_gather | solution.py:303
  29.5 3.8 %collective-permute-start = (bf16[2048,128]{1,0:T(8,128)(2,1)S(1)}, bf16[2048,128]{1,0:T(8,128)(2,1)S(1)}, u32[]{:S(2)}, u32[]{:S(2)}) collective-permute-start(bf16[2048,128]{1,0:T(8,128)(2,1)S(1)} %get-tuple-element.16), channel_id=1, source_target_pairs={{0,32},{32,0},{1,33},{33,1},{2,34},{34,2},{3,35},{35,3},{4,36},{36... | collective-permute-start | bytes 1572872 | tf_op jit(solution)/shard_map/ppermute | solution.py:291
  47.6 91.0 %all-gather.4.cloned.1.call-start = ((), (), s32[]{:S(2)}) async-start(), calls=%async_computation.7 | async-start | bytes 1114112 | tf_op jit(solution)/shard_map/all_gather | solution.py:330
  81.4 14.3 %all-to-all-start.3 = ((bf16[8,8,512]{2,1,0:T(8,128)(2,1)}), bf16[8,8,512]{2,1,0:T(8,128)(2,1)S(1)}, u32[]{:S(2)}, u32[]{:S(2)}) async-start(bf16[8,8,512]{2,1,0:T(8,128)(2,1)} %face_sum.1), calls=%async_computation.3 | async-start | bytes 131072 | tf_op jit(solution)/shard_map/all_to_all | solution.py:332
  95.7 1.9 %copy-start.3 = (bf16[6144,256]{1,0:T(8,128)(2,1)S(1)}, bf16[6144,256]{1,0:T(8,128)(2,1)}, u32[]{:S(2)}) copy-start(bf16[6144,256]{1,0:T(8,128)(2,1)} %all-gather.6.cloned.1.call-done) | copy-start | bytes 9437188
  103.6 1.2 copy-start.1
  104.8 24.4 %all-to-all-start.4 = ((bf16[4,784,256]{2,1,0:T(8,128)(2,1)}), bf16[4,784,256]{2,1,0:T(8,128)(2,1)}, u32[]{:S(2)}, u32[]{:S(2)}) async-start(bf16[4,784,256]{2,1,0:T(8,128)(2,1)} %copy-done.1), calls=%async_computation.4 | async-start | bytes 3211264 | tf_op jit(solution)/shard_map/all_to_all | solution.py:354
  132.5 15.0 %copy-start.7 = (bf16[256,256]{1,0:T(8,128)(2,1)S(1)}, bf16[256,256]{1,0:T(8,128)(2,1)}, u32[]{:S(2)}) copy-start(bf16[256,256]{1,0:T(8,128)(2,1)} %copy-done.6) | copy-start | bytes 393220
  132.5 15.0 %copy-start.9 = (bf16[256,256]{1,0:T(8,128)(2,1)S(1)}, bf16[256,256]{1,0:T(8,128)(2,1)}, u32[]{:S(2)}) copy-start(bf16[256,256]{1,0:T(8,128)(2,1)} %copy-done.8) | copy-start | bytes 393220
  132.5 15.0 %all-to-all-start.5 = ((bf16[16,8,512]{2,1,0:T(8,128)(2,1)}), bf16[16,8,512]{2,1,0:T(8,128)(2,1)S(1)}, u32[]{:S(2)}, u32[]{:S(2)}) async-start(bf16[16,8,512]{2,1,0:T(8,128)(2,1)} %meet_values.1), calls=%async_computation.5 | async-start | bytes 262144 | tf_op jit(solution)/shard_map/all_to_all | solution.py:367
  168.3 3.9 %collective-permute-start.1 = (bf16[2048,128]{1,0:T(8,128)(2,1)S(1)}, bf16[2048,128]{1,0:T(8,128)(2,1)S(1)}, u32[]{:S(2)}, u32[]{:S(2)}) collective-permute-start(bf16[2048,128]{1,0:T(8,128)(2,1)S(1)} %bitcast.88), channel_id=1, source_target_pairs={{0,32},{32,0},{1,33},{33,1},{2,34},{34,2},{3,35},{35,3},{4,36},{36... | collective-permute-start | bytes 1572872 | tf_op jit(solution)/shard_map/ppermute | solution.py:375
Sparse Core Ops, SparseCore 0:
  47.7 43.2 all-gather.5
  93.1 43.3 all-gather.3

commit v5 on v4

--- a/solution.py
+++ b/solution.py
@@ -8,18 +8,18 @@
 from jax.sharding import Mesh
 from jax.sharding import PartitionSpec as P
 
-
 F32 = jnp.float32
 BF16 = jnp.bfloat16
 GRP = ("z", "c")
 NT = (((1,), (1,)), ((), ()))
 VM = pl.BlockSpec(memory_space=pltpu.VMEM)
 SM = pl.BlockSpec(memory_space=pltpu.SMEM)
+FAR = pl.BlockSpec(memory_space=pltpu.HBM)
 PARAMS = pltpu.CompilerParams(vmem_limit_bytes=16 * 1024 * 1024)
 
 
-def call(kernel, name, outs, scratch, smem, cost, *args):
-    specs = [SM] * smem + [VM] * (len(args) - smem)
+def call(kernel, name, outs, scratch, smem, cost, *args, far=0):
+    specs = [SM] * smem + [VM] * (len(args) - smem - far) + [FAR] * far
     flops, moved = cost
     return pl.pallas_call(
         kernel,
@@ -51,6 +51,40 @@
     half = keep_ref.shape[0]
     keep_ref[...] = rows[:half].astype(BF16)
     send_ref[...] = rows[half:].astype(BF16)
+
+
+def first_pieces(map_ref, west_ref, east_ref, out_ref, rows, turned, *, stride):
+    count = map_ref.shape[0] // stride
+    for k in range(count):
+        pair = map_ref[k * stride : (k + 1) * stride, :].astype(F32)
+        rows[k : k + 1, :] = pair[0:1]
+        rows[count + k : count + k + 1, :] = pair[1:2]
+    turned[...] = rows[...].T
+    n = west_ref.shape[0]
+
+    def coupled(at, coupling):
+        picked = turned[pl.ds(at, n, stride=stride), :].T.astype(BF16)
+        high, low = halves(coupling)
+        return jnp.dot(picked, high, preferred_element_type=F32) + jnp.dot(
+            picked, low, preferred_element_type=F32
+        )
+
+    by_west = coupled(0, west_ref[...]).astype(BF16)
+    by_east = coupled(1, east_ref[...]).astype(BF16)
+    width = out_ref.shape[2]
+    for g in range(out_ref.shape[0]):
+        block = slice(g * width, (g + 1) * width)
+        out_ref[g, 0:count] = by_west[count:]
+        out_ref[g, count : 2 * count] = by_west[:count]
+        out_ref[g, 2 * count : 3 * count] = by_east[:count]
+        out_ref[g, 3 * count : 4 * count] = rows[count:, block].astype(BF16)
+        out_ref[g, 4 * count : 5 * count] = rows[:count, block].astype(BF16)
+
+
+def lay_halves(target, slot, side, mine, other):
+    rows = mine.shape[0]
+    target[slot, pl.ds(pl.multiple_of(side * rows, rows), rows), :] = mine
+    target[slot, pl.ds(pl.multiple_of((1 - side) * rows, rows), rows), :] = other
 
 
 def sort_maps(got_ref, maps_ref):
@@ -111,11 +145,17 @@
     return both[:rows] + both[rows:]
 
 
-def run_block(place, faces_ref, maps_ref, ends_ref, own_maps_ref, own_ref, *scratch):
-    state, right, through, given, sources = scratch
+def run_block(place, faces_ref, far_maps_ref, ends_ref, own_maps_ref, own_ref, *scratch):
+    state, right, through, given, sources, joined, maps_ref, done = scratch
     count, part, _ = faces_ref.shape
     n = maps_ref.shape[2]
-    here = place[0]
+    here, side = place[0], place[1]
+
+    def fetch(j):
+        return pltpu.make_async_copy(far_maps_ref.at[j], maps_ref.at[j], done.at[j])
+
+    for j in range(count):
+        fetch(j).start()
     unit = (
         lax.broadcasted_iota(jnp.int32, (n, n), 0) == lax.broadcasted_iota(jnp.int32, (n, n), 1)
     ).astype(F32)
@@ -133,6 +173,7 @@
             own_maps_ref[0:n] = value.astype(BF16)
             own_ref[:, 0:n] = east
 
+        fetch(j).wait()
         maps = maps_ref[j, 0 : 2 * n, :]
         both = exact_right(maps, value)
         moved = faces_ref[j].astype(F32) + exact_rows(east, maps)
@@ -165,17 +206,23 @@
 
     lax.fori_loop(0, count, back, 0)
     ends = jnp.concatenate([given[:, 0:n], given[:, n : 2 * n]], axis=0).astype(BF16)
+    joined[0:n] = state[...].astype(BF16)
+    joined[n : 2 * n] = right[:, 0:n].astype(BF16)
+    joined[2 * n : 3 * n] = right[:, n : 2 * n].astype(BF16)
+    rows = ends_ref.shape[1] - 2 * part
+    half = joined[pl.ds(pl.multiple_of(side * rows, rows), rows), :]
     for x in range(ends_ref.shape[0]):
-        ends_ref[x, 0:n] = state[...].astype(BF16)
-        ends_ref[x, n : 2 * n] = right[:, 0:n].astype(BF16)
-        ends_ref[x, 2 * n : 3 * n] = right[:, n : 2 * n].astype(BF16)
-        ends_ref[x, 3 * n : 3 * n + 2 * part] = ends
-
-
-def meet_values(place, ends_ref, maps_ref, own_ref, out_ref, entering):
+        ends_ref[x, 0:rows] = half
+        ends_ref[x, rows : rows + 2 * part] = ends
+
+
+def meet_values(place, ends_ref, other_ref, maps_ref, own_ref, out_ref, entering, joined_ref):
     count, _, n = ends_ref.shape
     part = own_ref.shape[0]
-    here = place[0]
+    here, side = place[0], place[1]
+    rows = ends_ref.shape[1] - 2 * part
+    for b in range(count):
+        lay_halves(joined_ref, b, side, ends_ref[b, 0:rows], other_ref[b, 0:rows])
     east = jnp.zeros((part, n), F32)
     sources = []
     for b in range(count):
@@ -184,12 +231,12 @@
         def _(east=east):
             entering[:, 0:n] = east
 
-        end = ends_ref[b, 3 * n : 3 * n + 2 * part].astype(F32)
+        end = ends_ref[b, rows : rows + 2 * part].astype(F32)
         source = end[part : 2 * part]
         if b:
-            source = source + exact_rows(east, ends_ref[b, 2 * n : 3 * n, :])
+            source = source + exact_rows(east, joined_ref[b, 2 * n : 3 * n, :])
         sources.append(source)
-        east = end[0:part] + (exact_rows(east, ends_ref[b, 0:n, :]) if b else 0.0)
+        east = end[0:part] + (exact_rows(east, joined_ref[b, 0:n, :]) if b else 0.0)
     west = jnp.zeros((part, n), F32)
     for b in range(count - 1, -1, -1):
 
@@ -198,7 +245,7 @@
             entering[:, n : 2 * n] = west
 
         west = sources[b] + (
-            exact_rows(west, ends_ref[b, n : 2 * n, :]) if b < count - 1 else 0.0
+            exact_rows(west, joined_ref[b, n : 2 * n, :]) if b < count - 1 else 0.0
         )
     east = entering[:, 0:n]
     west = entering[:, n : 2 * n]
@@ -247,33 +294,23 @@
     part = columns // peers
     half = interface // nc
     side = lax.axis_index("c")
-    at_y = jnp.reshape(lax.axis_index("y"), (1,)).astype(jnp.int32)
-    at_x = jnp.reshape(lax.axis_index("x"), (1,)).astype(jnp.int32)
+    core = side.astype(jnp.int32)
+    at_y = jnp.stack([lax.axis_index("y").astype(jnp.int32), core])
+    at_x = jnp.stack([lax.axis_index("x").astype(jnp.int32), core])
     swap = [(0, 1), (1, 0)]
 
-    spot = lax.broadcasted_iota(jnp.int32, (interface, 2 * n), 0)
-    want = lax.broadcasted_iota(jnp.int32, (interface, 2 * n), 1)
-    want = jnp.where(want < n, want * stride, (want - n) * stride + 1)
-    face_map = jnp.dot(rows_map, (spot == want).astype(BF16), preferred_element_type=F32)
-    west_high, west_low = halves(west)
-    east_high, east_low = halves(east)
-    face_low = face_map.astype(BF16)
-    coupled = jnp.concatenate(
-        [
-            jnp.dot(face_low[:, :n], west_high, preferred_element_type=F32)
-            + jnp.dot(face_low[:, :n], west_low, preferred_element_type=F32),
-            jnp.dot(face_low[:, n:], east_high, preferred_element_type=F32)
-            + jnp.dot(face_low[:, n:], east_low, preferred_element_type=F32),
-        ],
-        axis=1,
-    ).astype(BF16)
-    steps = coupled.reshape(nodes, stride, 2 * n)
-    slices = jnp.concatenate([steps[:, 1, :n], steps[:, 0, :n], steps[:, 0, n:]], axis=0)
-    slices = jnp.broadcast_to(slices, (peers,) + slices.shape)
-    rows = rows_map.reshape(nodes, stride, interface)
-    rows = jnp.concatenate([rows[:, 1], rows[:, 0]], axis=0)
-    rows = rows.reshape(2 * nodes, peers, width).transpose(1, 0, 2)
-    pieces = lax.all_to_all(jnp.concatenate([slices, rows], axis=1), GRP, 0, 0)
+    pieces = call(
+        functools.partial(first_pieces, stride=stride),
+        "first_pieces",
+        jax.ShapeDtypeStruct((peers, 5 * nodes, width), BF16),
+        [pltpu.VMEM((2 * nodes, interface), F32), pltpu.VMEM((interface, 2 * nodes), F32)],
+        0,
+        (8 * nodes * n * n, 2 * width * interface),
+        rows_map,
+        west,
+        east,
+    )
+    pieces = lax.all_to_all(pieces, GRP, 0, 0)
 
     owner = nodes_of // width
     pos = ((owner % nc) ^ side) * half + (owner // nc) * width + nodes_of % width
@@ -303,6 +340,24 @@
     run_maps = lax.all_gather(maps, "y")
 
     parts = lax.all_to_all(paired.reshape(nz, width, columns), "z", 0, 0)
+    late_map, _ = lax.optimization_barrier((rows_map, maps))
+    spot = lax.broadcasted_iota(jnp.int32, (interface, 2 * n), 0)
+    want = lax.broadcasted_iota(jnp.int32, (interface, 2 * n), 1)
+    want = jnp.where(want < n, want * stride, (want - n) * stride + 1)
+    face_map = jnp.dot(late_map, (spot == want).astype(BF16), preferred_element_type=F32)
+    face_map = face_map.astype(BF16)
+    west_high, west_low = halves(west)
+    east_high, east_low = halves(east)
+    coupled = jnp.concatenate(
+        [
+            jnp.dot(face_map[:, :n], west_high, preferred_element_type=F32)
+            + jnp.dot(face_map[:, :n], west_low, preferred_element_type=F32),
+            jnp.dot(face_map[:, n:], east_high, preferred_element_type=F32)
+            + jnp.dot(face_map[:, n:], east_low, preferred_element_type=F32),
+        ],
+        axis=1,
+    ).astype(BF16)
+
     loads, faces = call(
         face_parts,
         "face_parts",
@@ -334,7 +389,7 @@
         run_block,
         "run_block",
         (
-            jax.ShapeDtypeStruct((nx, 3 * n + 2 * part, n), BF16),
+            jax.ShapeDtypeStruct((nx, 3 * n // nc + 2 * part, n), BF16),
             jax.ShapeDtypeStruct((3 * n, n), BF16),
             jax.ShapeDtypeStruct((part, 2 * n), F32),
         ),
@@ -344,23 +399,29 @@
             pltpu.VMEM((ny, n, n), F32),
             pltpu.VMEM((part, 2 * n), F32),
             pltpu.VMEM((ny, part, n), F32),
+            pltpu.VMEM((3 * n, n), BF16),
+            pltpu.VMEM((ny, 3 * n, n), BF16),
+            pltpu.SemaphoreType.DMA((ny,)),
         ],
         1,
         (16 * ny * n**3, 6 * ny * n * n),
         at_y,
         line,
         run_maps,
+        far=1,
     )
     ends = lax.all_to_all(ends, "x", 0, 0)
+    other_ends = lax.ppermute(ends, "c", swap)
     met = call(
         meet_values,
         "meet_values",
         jax.ShapeDtypeStruct((peers, part, 2 * n), BF16),
-        [pltpu.VMEM((part, 2 * n), F32)],
+        [pltpu.VMEM((part, 2 * n), F32), pltpu.VMEM((nx, 3 * n, n), BF16)],
         1,
         (12 * nx * n * n * 16, 6 * nx * n * n),
         at_x,
         ends,
+        other_ends,
         own_maps,
         own_values,
     )

time: 183 us -> 180 us (0.984)
  blocking collectives: 52.8 us -> 40.7 us
  starting transfers between devices: 33.5 us -> 38.9 us
  Pallas kernels: 17.1 us -> 20.5 us
  matrix products: 6.8 us -> 8.72 us
    all_to_all x1 -> x0, blocking collectives: 12.1 us -> none  [on_device(): faces = lax.all_to_all(faces, GRP, 0, 0)]
    all_to_all x1, waiting for transfers between devices: 20.1 us -> 8.9 us  [on_device(): ends = lax.all_to_all(ends, 'x', 0, 0)]
    all_to_all x1 -> x2, waiting for transfers between devices: 13.3 us -> 21.8 us  [the longest x1 13.3 us: on_device(): pieces = lax.all_to_all(pieces, GRP, 0, 0)]
    ppermute x0 -> x1, starting transfers between devices: none -> 4.34 us  [on_device(): other_ends = lax.ppermute(ends, 'c', swap)]
    all_to_all x1 -> x2, starting transfers between devices: 11.8 us -> 15.7 us  [the longest x1 11.8 us: on_device(): pieces = lax.all_to_all(pieces, GRP, 0, 0)]
    pallas_call x7 -> x8, Pallas kernels: 17.1 us -> 20.5 us  [call(): pl.pallas_call(kernel, name=name, out_shape=outs, in_specs=specs, out_spe...]
    unnamed x25 -> x34, local copies, waits for them, and re-layouts: 3.71 us -> 7.07 us
    slice x3 -> x0, local copies, waits for them, and re-layouts: 2.81 us -> none  [the longest x1 2.77 us: on_device(): rows = jnp.concatenate([rows[:, 1], rows[:, 0]], axis=0)]
  transfers between devices with their start and end apart: 8 -> 10, of which waited for: 6 -> 7; matrix products, arithmetic and copies ran while one was open for 2% -> 5% of each run, Pallas kernels for 7% -> 8%
where the time goes in v5:
time: 180 us; the launch traced here: 179 us
  waiting for transfers between devices  48.8 us (27%)
  blocking collectives  40.7 us (23%)
  starting transfers between devices  38.9 us (22%)
  Pallas kernels  20.5 us (11%)
  between operations  13.6 us (8%)
  matrix products  8.72 us (5%)
  local copies, waits for them, and re-layouts  7.25 us (4%)
    pallas_call x8, Pallas kernels, call(): pl.pallas_call(kernel, name=name, out_shape=outs, in_specs=specs, out_spe...  20.5 us
    all_to_all x1, blocking collectives, on_device(): final_own = lax.all_to_all(final, 'z', 0, 0).reshape(half, columns)  20.4 us
    all_to_all x1, blocking collectives, on_device(): parts = lax.all_to_all(paired.reshape(nz, width, columns), 'z', 0, 0)  20.3 us
    all_to_all x1, waiting for transfers between devices, on_device(): pieces = lax.all_to_all(pieces, GRP, 0, 0)  13.3 us
    all_to_all x1, starting transfers between devices, on_device(): pieces = lax.all_to_all(pieces, GRP, 0, 0)  11.8 us
    all_to_all x1, waiting for transfers between devices, on_device(): ends = lax.all_to_all(ends, 'x', 0, 0)  8.9 us
    all_to_all x1, waiting for transfers between devices, on_device(): faces = lax.all_to_all(faces, GRP, 0, 0)  8.44 us
    all_to_all x1, waiting for transfers between devices, on_device(): line = lax.all_to_all(line, 'y', 0, 0)  7.36 us
  transfers between devices with their start and end apart: 10, of which 7 were waited for; matrix products, arithmetic and copies ran while one was open for 5% of the time, Pallas kernels for 8%

profile of v5, /device:TPU:1, one launch (start us, length us, event | category | flops | bytes accessed | tf_op | source)
XLA Modules:
  0.0 178.8 jit_solution(7272304977393743894)
XLA Ops:
  6.5 1.6 copy-done
  8.1 0.9 copy-done.4
  9.1 0.9 copy-done.6
  10.0 1.8 %first_pieces.1 = bf16[16,80,256]{2,1,0:T(8,128)(2,1)} custom-call(bf16[256,4096]{1,0:T(8,128)(2,1)S(1)} %bitcast.56, f32[256,256]{1,0:T(8,128)S(1)} %bitcast.60, f32[256,256]{1,0:T(8,128)S(1)} %bitcast.61), custom_call_target="tpu_custom_call" | custom-call | flops 8388608 | bytes 2097152 | tf_op jit(solution)/shard_map/first_pieces/pallas_call | solution.py:24
  11.8 11.8 %all-to-all-start = ((bf16[16,80,256]{2,1,0:T(8,128)(2,1)}), bf16[16,80,256]{2,1,0:T(8,128)(2,1)S(1)}, u32[]{:S(2)}, u32[]{:S(2)}) async-start(bf16[16,80,256]{2,1,0:T(8,128)(2,1)} %first_pieces.1), calls=%async_computation | async-start | bytes 1310720 | tf_op jit(solution)/shard_map/all_to_all | solution.py:313
  23.8 2.6 %spread_rows.1 = (bf16[2048,128]{1,0:T(8,128)(2,1)S(1)}, bf16[2048,128]{1,0:T(8,128)(2,1)S(1)}) custom-call(s32[1024]{0:T(1024)S(1)} %fusion.25.pos, bf16[1024,1024]{1,0:T(8,128)(2,1)S(1)} %bitcast.58, bf16[1024,128]{1,0:T(8,128)(2,1)S(1)} %bitcast.64), custom_call_target="tpu_custom_call" | custom-call | flops 268435456 | bytes 6291456 | tf_op jit(solution)/shard_map/spread_rows/pallas_call | solution.py:24
  26.3 2.0 %collective-permute-start = (bf16[2048,128]{1,0:T(8,128)(2,1)S(1)}, bf16[2048,128]{1,0:T(8,128)(2,1)S(1)}, u32[]{:S(2)}, u32[]{:S(2)}) collective-permute-start(bf16[2048,128]{1,0:T(8,128)(2,1)S(1)} %get-tuple-element.17), channel_id=1, source_target_pairs={{0,32},{32,0},{1,33},{33,1},{2,34},{34,2},{3,35},{35,3},{4,36},{36... | collective-permute-start | bytes 1572872 | tf_op jit(solution)/shard_map/ppermute | solution.py:328
  28.3 1.8 collective-permute-done
  30.3 13.3 %all-to-all-done.rows_ref.got_ref = bf16[16,80,256]{2,1,0:T(8,128)(2,1)S(1)} async-done(((bf16[16,80,256]{2,1,0:T(8,128)(2,1)}), bf16[16,80,256]{2,1,0:T(8,128)(2,1)S(1)}, u32[]{:S(2)}, u32[]{:S(2)}) %all-to-all-start) | async-done | bytes 655392 | tf_op jit(solution)/shard_map/all_to_all | solution.py:313
  44.4 20.3 %all_to_all.35.parts_ref = bf16[8,256,128]{2,1,0:T(8,128)(2,1)S(1)} all-to-all(bf16[8,256,128]{2,1,0:T(8,128)(2,1)S(1)} %bitcast.67), channel_id=1, replica_groups=mesh['z'=8,'c'=2,'x'=4,'y'=8] {'z'}, dimensions={0} | all-to-all | bytes 1048576 | tf_op jit(solution)/shard_map/all_to_all | solution.py:342
  64.7 0.9 face_parts.1
  65.7 3.9 %all-to-all-start.2 = ((bf16[16,8,512]{2,1,0:T(8,128)(2,1)}), bf16[16,8,512]{2,1,0:T(8,128)(2,1)S(1)}, u32[]{:S(2)}, u32[]{:S(2)}) async-start(bf16[16,8,512]{2,1,0:T(8,128)(2,1)} %get-tuple-element.21), calls=%async_computation.2 | async-start | bytes 262144 | tf_op jit(solution)/shard_map/all_to_all | solution.py:374
  70.3 8.4 %all-to-all-done.2.got_ref = bf16[16,8,512]{2,1,0:T(8,128)(2,1)S(1)} async-done(((bf16[16,8,512]{2,1,0:T(8,128)(2,1)}), bf16[16,8,512]{2,1,0:T(8,128)(2,1)S(1)}, u32[]{:S(2)}, u32[]{:S(2)}) %all-to-all-start.2) | async-done | bytes 131104 | tf_op jit(solution)/shard_map/all_to_all | solution.py:374
  79.3 6.8 %all-to-all-start.3 = ((bf16[8,8,512]{2,1,0:T(8,128)(2,1)}), bf16[8,8,512]{2,1,0:T(8,128)(2,1)S(1)}, u32[]{:S(2)}, u32[]{:S(2)}) async-start(bf16[8,8,512]{2,1,0:T(8,128)(2,1)} %face_sum.1), calls=%async_computation.3 | async-start | bytes 131072 | tf_op jit(solution)/shard_map/all_to_all | solution.py:387
  86.3 7.4 %all-to-all-done.3.faces_ref = bf16[8,8,512]{2,1,0:T(8,128)(2,1)S(1)} async-done(((bf16[8,8,512]{2,1,0:T(8,128)(2,1)}), bf16[8,8,512]{2,1,0:T(8,128)(2,1)S(1)}, u32[]{:S(2)}, u32[]{:S(2)}) %all-to-all-start.3) | async-done | bytes 65568 | tf_op jit(solution)/shard_map/all_to_all | solution.py:387
  93.6 1.9 %copy-done.13 = bf16[6144,256]{1,0:T(8,128)(2,1)S(1)} copy-done((bf16[6144,256]{1,0:T(8,128)(2,1)S(1)}, bf16[6144,256]{1,0:T(8,128)(2,1)}, u32[]{:S(2)}) %copy-start.13) | copy-done | bytes 3145752
  95.5 8.1 %run_block.1 = (bf16[4,400,256]{2,1,0:T(8,128)(2,1)S(1)}, bf16[768,256]{1,0:T(8,128)(2,1)S(1)}, f32[8,512]{1,0:T(8,128)S(1)}) custom-call(s32[2]{0:T(128)S(1)} %pad_add_fusion.1.place, bf16[8,8,512]{2,1,0:T(8,128)(2,1)S(1)} %all-to-all-done.3.faces_ref, bf16[8,768,256]{2,1,0:T(8,128)(2,1)S(1)} %bitcast.66), custom_call_target="tpu_custom_call" | custom-call | flops 2147483648 | bytes 3145728 | tf_op jit(solution)/shard_map/run_block/pallas_call | solution.py:24
  105.3 4.0 %all-to-all-start.4 = ((bf16[4,400,256]{2,1,0:T(8,128)(2,1)}), bf16[4,400,256]{2,1,0:T(8,128)(2,1)S(1)}, u32[]{:S(2)}, u32[]{:S(2)}) async-start(bf16[4,400,256]{2,1,0:T(8,128)(2,1)} %copy-done.10), calls=%async_computation.4 | async-start | bytes 1638400 | tf_op jit(solution)/shard_map/all_to_all | solution.py:413
  109.4 2.3 %fusion.4 = bf16[256,512]{1,0:T(8,128)(2,1)} fusion(bf16[256,4096]{1,0:T(8,128)(2,1)S(1)} %bitcast.57, s32[512]{0:T(512)S(1)} %get-tuple-element.28, s32[512]{0:T(512)S(1)} %get-tuple-element.27, pred[512]{0:T(512)(128)(4,1)S(1)} %iota_compare_fusion), kind=kOutput, calls=%fused_computation.5 | convolution fusion | flops 1078067200 | bytes 2363904 | tf_op jit(solution)/shard_map/dot_general | solution.py:347
  111.7 8.9 %all-to-all-done.4.ends_ref = bf16[4,400,256]{2,1,0:T(8,128)(2,1)S(1)} async-done(((bf16[4,400,256]{2,1,0:T(8,128)(2,1)}), bf16[4,400,256]{2,1,0:T(8,128)(2,1)S(1)}, u32[]{:S(2)}, u32[]{:S(2)}) %all-to-all-start.4) | async-done | bytes 819232 | tf_op jit(solution)/shard_map/all_to_all | solution.py:413
  120.6 4.3 %collective-permute-start.1 = (bf16[4,400,256]{2,1,0:T(8,128)(2,1)S(1)}, bf16[4,400,256]{2,1,0:T(8,128)(2,1)S(1)}, u32[]{:S(2)}, u32[]{:S(2)}) collective-permute-start(bf16[4,400,256]{2,1,0:T(8,128)(2,1)S(1)} %all-to-all-done.4.ends_ref), channel_id=1, source_target_pairs={{0,32},{32,0},{1,33},{33,1},{2,34},{34,2},{3,35},{35,3},{4,36},{36... | collective-permute-start | bytes 2457608 | tf_op jit(solution)/shard_map/ppermute | solution.py:414
  125.0 1.1 fusion.16
  126.1 1.1 fusion.13
  127.2 1.7 fusion.5
  129.1 2.5 %meet_values.1 = bf16[16,8,512]{2,1,0:T(8,128)(2,1)} custom-call(s32[2]{0:T(128)S(1)} %pad_add_fusion.place, bf16[4,400,256]{2,1,0:T(8,128)(2,1)S(1)} %all-to-all-done.4.ends_ref, bf16[4,400,256]{2,1,0:T(8,128)(2,1)S(1)} %collective-permute-done.1.other_ref, bf16[768,256]{1,0:T(8,128)(2,1)S(1)} %copy-done.12, f32[8,512]{1,0:T(8,128)S(1)} %get-tuple-element.24.own_ref), custom_call_target="tpu_custom_call" | custom-call | flops 50331648 | bytes 1572864 | tf_op jit(solution)/shard_map/meet_values/pallas_call | solution.py:24
  131.6 3.6 %all-to-all-start.5 = ((bf16[16,8,512]{2,1,0:T(8,128)(2,1)}), bf16[16,8,512]{2,1,0:T(8,128)(2,1)S(1)}, u32[]{:S(2)}, u32[]{:S(2)}) async-start(bf16[16,8,512]{2,1,0:T(8,128)(2,1)} %meet_values.1), calls=%async_computation.5 | async-start | bytes 262144 | tf_op jit(solution)/shard_map/all_to_all | solution.py:428
  135.3 2.1 %convolution_bitcast_fusion = f32[256,128]{0,1:T(8,128)S(1)} fusion(bf16[4096,128]{1,0:T(8,128)(2,1)} %all-gather.4.cloned.1.call-done, bf16[1,256,4096]{2,1,0:T(8,128)(2,1)S(1)} %copy-done.1), kind=kOutput, calls=%fused_computation.11 | convolution fusion | flops 268435456 | bytes 3276800 | tf_op jit(solution)/shard_map/dot_general | solution.py:431
  137.4 6.7 %all-to-all-done.5 = bf16[16,8,512]{2,1,0:T(8,128)(2,1)S(1)} async-done(((bf16[16,8,512]{2,1,0:T(8,128)(2,1)}), bf16[16,8,512]{2,1,0:T(8,128)(2,1)S(1)}, u32[]{:S(2)}, u32[]{:S(2)}) %all-to-all-start.5) | async-done | bytes 131104 | tf_op jit(solution)/shard_map/all_to_all | solution.py:428
  144.6 20.4 %all_to_all.36 = bf16[8,256,128]{2,1,0:T(8,128)(2,1)S(1)} all-to-all(bf16[8,256,128]{2,1,0:T(8,128)(2,1)S(1)} %broadcast_in_dim.6), channel_id=1, replica_groups=mesh['z'=8,'c'=2,'x'=4,'y'=8] {'z'}, dimensions={0} | all-to-all | bytes 1048576 | tf_op jit(solution)/shard_map/all_to_all | solution.py:435
  164.9 2.4 %collective-permute-start.2 = (bf16[2048,128]{1,0:T(8,128)(2,1)S(1)}, bf16[2048,128]{1,0:T(8,128)(2,1)S(1)}, u32[]{:S(2)}, u32[]{:S(2)}) collective-permute-start(bf16[2048,128]{1,0:T(8,128)(2,1)S(1)} %bitcast.62), channel_id=1, source_target_pairs={{0,32},{32,0},{1,33},{33,1},{2,34},{34,2},{3,35},{35,3},{4,36},{36... | collective-permute-start | bytes 1572872 | tf_op jit(solution)/shard_map/ppermute | solution.py:436
  167.3 1.5 collective-permute-done.2.other_ref
  168.8 3.1 %leaf_result.1 = bf16[1024,128]{1,0:T(8,128)(2,1)} custom-call(s32[1024]{0:T(1024)S(1)} %fusion.25.pos, bf16[2048,128]{1,0:T(8,128)(2,1)S(1)} %bitcast.63, bf16[2048,128]{1,0:T(8,128)(2,1)S(1)} %collective-permute-done.2.other_ref, bf16[1024,1024]{1,0:T(8,128)(2,1)S(1)} %bitcast.59, bf16[1024,128]{1,0:T(8,128)(2,1)S(1)} %bitcast.65), custom_call_target="tpu_custom_call" | custom-call | flops 268435456 | bytes 2097152 | tf_op jit(solution)/shard_map/leaf_result/pallas_call | solution.py:24
  (49 shorter events, 4.9 us)
Async XLA Ops:
  6.5 1.6 copy-start
  8.1 0.9 copy-start.4
  9.1 0.9 copy-start.6
  10.0 13.7 %copy-start.16 = (s32[1,1,1024]{2,1,0:T(1,128)S(1)}, s32[1,1,1024]{2,1,0:T(1,128)}, u32[]{:S(2)}) copy-start(s32[1,1,1024]{2,1,0:T(1,128)} %param.9) | copy-start | bytes 12292
  10.0 13.7 %copy-start.2 = (bf16[1,1,1024,1024]{3,2,1,0:T(8,128)(2,1)S(1)}, bf16[1,1,1024,1024]{3,2,1,0:T(8,128)(2,1)}, u32[]{:S(2)}) copy-start(bf16[1,1,1024,1024]{3,2,1,0:T(8,128)(2,1)} %param.7) | copy-start | bytes 6291460
  10.0 13.7 %copy-start.8 = (bf16[1,1,1024,128]{3,2,1,0:T(8,128)(2,1)S(1)}, bf16[1,1,1024,128]{3,2,1,0:T(8,128)(2,1)}, u32[]{:S(2)}) copy-start(bf16[1,1,1024,128]{3,2,1,0:T(8,128)(2,1)} %param.6) | copy-start | bytes 786436
  11.8 31.8 %all-to-all-start = ((bf16[16,80,256]{2,1,0:T(8,128)(2,1)}), bf16[16,80,256]{2,1,0:T(8,128)(2,1)S(1)}, u32[]{:S(2)}, u32[]{:S(2)}) async-start(bf16[16,80,256]{2,1,0:T(8,128)(2,1)} %first_pieces.1), calls=%async_computation | async-start | bytes 1310720 | tf_op jit(solution)/shard_map/all_to_all | solution.py:313
  23.7 70.0 %all-gather.6.cloned.1.call-start = ((), (), s32[]{:S(2)}) async-start(), calls=%async_computation.8 | async-start | bytes 3538944 | tf_op jit(solution)/shard_map/all_gather | solution.py:340
  26.3 3.8 %collective-permute-start = (bf16[2048,128]{1,0:T(8,128)(2,1)S(1)}, bf16[2048,128]{1,0:T(8,128)(2,1)S(1)}, u32[]{:S(2)}, u32[]{:S(2)}) collective-permute-start(bf16[2048,128]{1,0:T(8,128)(2,1)S(1)} %get-tuple-element.17), channel_id=1, source_target_pairs={{0,32},{32,0},{1,33},{33,1},{2,34},{34,2},{3,35},{35,3},{4,36},{36... | collective-permute-start | bytes 1572872 | tf_op jit(solution)/shard_map/ppermute | solution.py:328
  65.7 13.0 %all-to-all-start.2 = ((bf16[16,8,512]{2,1,0:T(8,128)(2,1)}), bf16[16,8,512]{2,1,0:T(8,128)(2,1)S(1)}, u32[]{:S(2)}, u32[]{:S(2)}) async-start(bf16[16,8,512]{2,1,0:T(8,128)(2,1)} %get-tuple-element.21), calls=%async_computation.2 | async-start | bytes 262144 | tf_op jit(solution)/shard_map/all_to_all | solution.py:374
  69.5 65.8 %all-gather.4.cloned.1.call-start = ((), (), s32[]{:S(2)}) async-start(), calls=%async_computation.7 | async-start | bytes 1114112 | tf_op jit(solution)/shard_map/all_gather | solution.py:385
  79.3 14.3 %all-to-all-start.3 = ((bf16[8,8,512]{2,1,0:T(8,128)(2,1)}), bf16[8,8,512]{2,1,0:T(8,128)(2,1)S(1)}, u32[]{:S(2)}, u32[]{:S(2)}) async-start(bf16[8,8,512]{2,1,0:T(8,128)(2,1)} %face_sum.1), calls=%async_computation.3 | async-start | bytes 131072 | tf_op jit(solution)/shard_map/all_to_all | solution.py:387
  93.6 1.9 %copy-start.13 = (bf16[6144,256]{1,0:T(8,128)(2,1)S(1)}, bf16[6144,256]{1,0:T(8,128)(2,1)}, u32[]{:S(2)}) copy-start(bf16[6144,256]{1,0:T(8,128)(2,1)} %all-gather.6.cloned.1.call-done) | copy-start | bytes 9437188
  95.5 13.9 %copy-start.1 = (bf16[1,256,4096]{2,1,0:T(8,128)(2,1)S(1)}, bf16[1,256,4096]{2,1,0:T(8,128)(2,1)}, u32[]{:S(2)}) copy-start(bf16[1,256,4096]{2,1,0:T(8,128)(2,1)} %param.8) | copy-start | bytes 6291460
  103.7 0.9 copy-start.10
  104.6 0.7 copy-start.11
  105.3 15.3 %all-to-all-start.4 = ((bf16[4,400,256]{2,1,0:T(8,128)(2,1)}), bf16[4,400,256]{2,1,0:T(8,128)(2,1)S(1)}, u32[]{:S(2)}, u32[]{:S(2)}) async-start(bf16[4,400,256]{2,1,0:T(8,128)(2,1)} %copy-done.10), calls=%async_computation.4 | async-start | bytes 1638400 | tf_op jit(solution)/shard_map/all_to_all | solution.py:413
  109.4 15.6 %copy-start.5 = (f32[1,256,256]{2,1,0:T(8,128)S(1)}, f32[1,256,256]{2,1,0:T(8,128)}, u32[]{:S(2)}) copy-start(f32[1,256,256]{2,1,0:T(8,128)} %param.10) | copy-start | bytes 786436
  109.4 16.7 %copy-start.7 = (f32[1,256,256]{2,1,0:T(8,128)S(1)}, f32[1,256,256]{2,1,0:T(8,128)}, u32[]{:S(2)}) copy-start(f32[1,256,256]{2,1,0:T(8,128)} %param.11) | copy-start | bytes 786436
  120.6 8.3 %copy-start.14 = (bf16[256,512]{1,0:T(8,128)(2,1)S(1)}, bf16[256,512]{1,0:T(8,128)(2,1)}, u32[]{:S(2)}) copy-start(bf16[256,512]{1,0:T(8,128)(2,1)} %fusion.4) | copy-start | bytes 786436
  120.6 8.5 %copy-start.12 = (bf16[768,256]{1,0:T(8,128)(2,1)S(1)}, bf16[768,256]{1,0:T(8,128)(2,1)}, u32[]{:S(2)}) copy-start(bf16[768,256]{1,0:T(8,128)(2,1)} %copy-done.11) | copy-start | bytes 1179652
  120.6 8.5 %collective-permute-start.1 = (bf16[4,400,256]{2,1,0:T(8,128)(2,1)S(1)}, bf16[4,400,256]{2,1,0:T(8,128)(2,1)S(1)}, u32[]{:S(2)}, u32[]{:S(2)}) collective-permute-start(bf16[4,400,256]{2,1,0:T(8,128)(2,1)S(1)} %all-to-all-done.4.ends_ref), channel_id=1, source_target_pairs={{0,32},{32,0},{1,33},{33,1},{2,34},{34,2},{3,35},{35,3},{4,36},{36... | collective-permute-start | bytes 2457608 | tf_op jit(solution)/shard_map/ppermute | solution.py:414
  131.6 12.5 %copy-start.15 = (bf16[256,256]{1,0:T(8,128)(2,1)S(1)}, bf16[256,256]{1,0:T(8,128)(2,1)}, u32[]{:S(2)}) copy-start(bf16[256,256]{1,0:T(8,128)(2,1)} %fusion.5) | copy-start | bytes 393220
  131.6 12.5 %all-to-all-start.5 = ((bf16[16,8,512]{2,1,0:T(8,128)(2,1)}), bf16[16,8,512]{2,1,0:T(8,128)(2,1)S(1)}, u32[]{:S(2)}, u32[]{:S(2)}) async-start(bf16[16,8,512]{2,1,0:T(8,128)(2,1)} %meet_values.1), calls=%async_computation.5 | async-start | bytes 262144 | tf_op jit(solution)/shard_map/all_to_all | solution.py:428
  135.2 33.6 %copy-start.9 = (bf16[1,1,1024,128]{3,2,1,0:T(8,128)(2,1)S(1)}, bf16[1,1,1024,128]{3,2,1,0:T(8,128)(2,1)}, u32[]{:S(2)}) copy-start(bf16[1,1,1024,128]{3,2,1,0:T(8,128)(2,1)} %param.6) | copy-start | bytes 786436
  137.4 31.4 %copy-start.3 = (bf16[1,1,1024,1024]{3,2,1,0:T(8,128)(2,1)S(1)}, bf16[1,1,1024,1024]{3,2,1,0:T(8,128)(2,1)}, u32[]{:S(2)}) copy-start(bf16[1,1,1024,1024]{3,2,1,0:T(8,128)(2,1)} %param.7) | copy-start | bytes 6291460
  164.9 3.9 %collective-permute-start.2 = (bf16[2048,128]{1,0:T(8,128)(2,1)S(1)}, bf16[2048,128]{1,0:T(8,128)(2,1)S(1)}, u32[]{:S(2)}, u32[]{:S(2)}) collective-permute-start(bf16[2048,128]{1,0:T(8,128)(2,1)S(1)} %bitcast.62), channel_id=1, source_target_pairs={{0,32},{32,0},{1,33},{33,1},{2,34},{34,2},{3,35},{35,3},{4,36},{36... | collective-permute-start | bytes 1572872 | tf_op jit(solution)/shard_map/ppermute | solution.py:436
Sparse Core Ops, SparseCore 0:
  44.5 43.2 all-gather.5
  90.0 43.4 all-gather.3

commit v6 on v5

--- a/solution.py
+++ b/solution.py
@@ -8,29 +8,32 @@
 from jax.sharding import Mesh
 from jax.sharding import PartitionSpec as P
 
+
 F32 = jnp.float32
 BF16 = jnp.bfloat16
 GRP = ("z", "c")
 NT = (((1,), (1,)), ((), ()))
 VM = pl.BlockSpec(memory_space=pltpu.VMEM)
 SM = pl.BlockSpec(memory_space=pltpu.SMEM)
-FAR = pl.BlockSpec(memory_space=pltpu.HBM)
-PARAMS = pltpu.CompilerParams(vmem_limit_bytes=16 * 1024 * 1024)
-
-
-def call(kernel, name, outs, scratch, smem, cost, *args, far=0):
-    specs = [SM] * smem + [VM] * (len(args) - smem - far) + [FAR] * far
+MIB = 1024 * 1024
+
+
+def call(kernel, outs, scratch, smem, cost, *args, grant=16):
+    specs = [SM] * smem + [VM] * (len(args) - smem)
     flops, moved = cost
     return pl.pallas_call(
         kernel,
-        name=name,
         out_shape=outs,
         in_specs=specs,
         out_specs=jax.tree.map(lambda _: VM, outs),
         scratch_shapes=scratch,
-        compiler_params=PARAMS,
+        compiler_params=pltpu.CompilerParams(vmem_limit_bytes=grant * MIB),
         cost_estimate=pl.CostEstimate(flops=flops, bytes_accessed=moved, transcendentals=0),
     )(*args)
+
+
+def exchange(value, axis):
+    return lax.all_to_all(value, axis, 0, 0)
 
 
 def spread_rows(pos, map_ref, load_ref, keep_ref, send_ref, contrib, rows):
@@ -71,14 +74,35 @@
 
     by_west = coupled(0, west_ref[...]).astype(BF16)
     by_east = coupled(1, east_ref[...]).astype(BF16)
-    width = out_ref.shape[2]
+    slim = out_ref.shape[2]
+    sides = n // slim
     for g in range(out_ref.shape[0]):
-        block = slice(g * width, (g + 1) * width)
-        out_ref[g, 0:count] = by_west[count:]
-        out_ref[g, count : 2 * count] = by_west[:count]
-        out_ref[g, 2 * count : 3 * count] = by_east[:count]
-        out_ref[g, 3 * count : 4 * count] = rows[count:, block].astype(BF16)
-        out_ref[g, 4 * count : 5 * count] = rows[:count, block].astype(BF16)
+        side = slice(g % sides * slim, (g % sides + 1) * slim)
+        out_ref[g, 0:count] = by_west[count:, side]
+        out_ref[g, count : 2 * count] = by_west[:count, side]
+        out_ref[g, 2 * count : 3 * count] = by_east[:count, side]
+        for k in range(sides):
+            block = slice((g * sides + k) * slim, (g * sides + k + 1) * slim)
+            at = 3 * count + k * count
+            out_ref[g, at : at + count] = rows[count:, block].astype(BF16)
+            at = at + sides * count
+            out_ref[g, at : at + count] = rows[:count, block].astype(BF16)
+
+
+def couple_rows(map_ref, west_ref, east_ref, out_ref, turned, *, stride):
+    parts, interface, slim = turned.shape
+    n = west_ref.shape[0]
+    for p in range(parts):
+        block = slice(p * slim, (p + 1) * slim)
+        for at in range(0, interface, n):
+            turned[p, at : at + n] = map_ref[block, at : at + n].astype(F32).T
+        for side, coupling in enumerate((west_ref, east_ref)):
+            picked = turned[p, pl.ds(side, n, stride=stride), :].T.astype(BF16)
+            high, low = halves(coupling[...])
+            out_ref[block, side * n : (side + 1) * n] = (
+                jnp.dot(picked, high, preferred_element_type=F32)
+                + jnp.dot(picked, low, preferred_element_type=F32)
+            ).astype(BF16)
 
 
 def lay_halves(target, slot, side, mine, other):
@@ -88,7 +112,8 @@
 
 
 def sort_maps(got_ref, maps_ref):
-    peers, _, n = got_ref.shape
+    peers = got_ref.shape[0]
+    n = maps_ref.shape[0] // 3
     nodes = n // peers
     for g in range(peers):
         for k in range(3):
@@ -103,11 +128,18 @@
         total = total + parts_ref[z].astype(F32)
     loads = total.astype(BF16)
     loads_ref[...] = loads
-    peers, five, _ = rows_ref.shape
-    nodes = five // 5
+    peers, high, slim = rows_ref.shape
+    sides = order.shape[1] // slim
+    nodes = high // (3 + 2 * sides)
     for g in range(peers):
-        order[g * nodes : (g + 1) * nodes] = rows_ref[g, 3 * nodes : 4 * nodes]
-        order[(peers + g) * nodes : (peers + g + 1) * nodes] = rows_ref[g, 4 * nodes : five]
+        for k in range(sides):
+            block = slice(k * slim, (k + 1) * slim)
+            at = (3 + k) * nodes
+            order[g * nodes : (g + 1) * nodes, block] = rows_ref[g, at : at + nodes]
+            at = at + sides * nodes
+            order[(peers + g) * nodes : (peers + g + 1) * nodes, block] = rows_ref[
+                g, at : at + nodes
+            ]
     lines = lax.dot_general(total.T.astype(BF16), order[...], NT, preferred_element_type=F32)
     part = out_ref.shape[1]
     for g in range(peers):
@@ -145,17 +177,14 @@
     return both[:rows] + both[rows:]
 
 
-def run_block(place, faces_ref, far_maps_ref, ends_ref, own_maps_ref, own_ref, *scratch):
-    state, right, through, given, sources, joined, maps_ref, done = scratch
+def run_block(place, faces_ref, mine_ref, other_ref, ends_ref, own_maps_ref, own_ref, *scratch):
+    state, right, through, given, sources, joined, maps_ref = scratch
     count, part, _ = faces_ref.shape
+    slim = mine_ref.shape[2]
     n = maps_ref.shape[2]
     here, side = place[0], place[1]
-
-    def fetch(j):
-        return pltpu.make_async_copy(far_maps_ref.at[j], maps_ref.at[j], done.at[j])
-
-    for j in range(count):
-        fetch(j).start()
+    maps_ref[:, :, pl.ds(pl.multiple_of(side * slim, slim), slim)] = mine_ref[...]
+    maps_ref[:, :, pl.ds(pl.multiple_of((1 - side) * slim, slim), slim)] = other_ref[...]
     unit = (
         lax.broadcasted_iota(jnp.int32, (n, n), 0) == lax.broadcasted_iota(jnp.int32, (n, n), 1)
     ).astype(F32)
@@ -173,7 +202,6 @@
             own_maps_ref[0:n] = value.astype(BF16)
             own_ref[:, 0:n] = east
 
-        fetch(j).wait()
         maps = maps_ref[j, 0 : 2 * n, :]
         both = exact_right(maps, value)
         moved = faces_ref[j].astype(F32) + exact_rows(east, maps)
@@ -301,22 +329,21 @@
 
     pieces = call(
         functools.partial(first_pieces, stride=stride),
-        "first_pieces",
-        jax.ShapeDtypeStruct((peers, 5 * nodes, width), BF16),
+        jax.ShapeDtypeStruct((peers, (3 + 2 * nc) * nodes, width // nc), BF16),
         [pltpu.VMEM((2 * nodes, interface), F32), pltpu.VMEM((interface, 2 * nodes), F32)],
         0,
         (8 * nodes * n * n, 2 * width * interface),
         rows_map,
         west,
         east,
-    )
-    pieces = lax.all_to_all(pieces, GRP, 0, 0)
+        grant=52,
+    )
+    pieces = exchange(pieces, GRP)
 
     owner = nodes_of // width
     pos = ((owner % nc) ^ side) * half + (owner // nc) * width + nodes_of % width
     keep, send = call(
         spread_rows,
-        "spread_rows",
         (jax.ShapeDtypeStruct((half, columns), BF16),) * 2,
         [pltpu.VMEM((leaf_nodes, columns), F32), pltpu.VMEM((interface, columns), F32)],
         1,
@@ -330,37 +357,29 @@
     pieces, paired = lax.optimization_barrier((pieces, paired))
     maps = call(
         sort_maps,
-        "sort_maps",
-        jax.ShapeDtypeStruct((3 * n, n), BF16),
+        jax.ShapeDtypeStruct((3 * n, n // nc), BF16),
         [],
         0,
-        (1000, 16 * n * n),
+        (1000, 8 * n * n),
         pieces,
     )
-    run_maps = lax.all_gather(maps, "y")
-
-    parts = lax.all_to_all(paired.reshape(nz, width, columns), "z", 0, 0)
+    run_half = lax.all_gather(maps, "y")
+
+    parts = exchange(paired.reshape(nz, width, columns), "z")
     late_map, _ = lax.optimization_barrier((rows_map, maps))
-    spot = lax.broadcasted_iota(jnp.int32, (interface, 2 * n), 0)
-    want = lax.broadcasted_iota(jnp.int32, (interface, 2 * n), 1)
-    want = jnp.where(want < n, want * stride, (want - n) * stride + 1)
-    face_map = jnp.dot(late_map, (spot == want).astype(BF16), preferred_element_type=F32)
-    face_map = face_map.astype(BF16)
-    west_high, west_low = halves(west)
-    east_high, east_low = halves(east)
-    coupled = jnp.concatenate(
-        [
-            jnp.dot(face_map[:, :n], west_high, preferred_element_type=F32)
-            + jnp.dot(face_map[:, :n], west_low, preferred_element_type=F32),
-            jnp.dot(face_map[:, n:], east_high, preferred_element_type=F32)
-            + jnp.dot(face_map[:, n:], east_low, preferred_element_type=F32),
-        ],
-        axis=1,
-    ).astype(BF16)
+    coupled = call(
+        functools.partial(couple_rows, stride=stride),
+        jax.ShapeDtypeStruct((width, 2 * n), BF16),
+        [pltpu.VMEM((width // 128, interface, 128), F32)],
+        0,
+        (8 * width * n * n, 4 * width * interface),
+        late_map,
+        west,
+        east,
+    )
 
     loads, faces = call(
         face_parts,
-        "face_parts",
         (
             jax.ShapeDtypeStruct((width, columns), BF16),
             jax.ShapeDtypeStruct((peers, part, 2 * n), BF16),
@@ -374,7 +393,6 @@
     faces = lax.all_to_all(faces, GRP, 0, 0)
     line = call(
         face_sum,
-        "face_sum",
         jax.ShapeDtypeStruct((ny, part, 2 * n), BF16),
         [],
         0,
@@ -384,10 +402,11 @@
 
     all_loads = lax.all_gather(loads, GRP, axis=0, tiled=True)
 
-    line = lax.all_to_all(line, "y", 0, 0)
+    run_half, line = lax.optimization_barrier((run_half, line))
+    run_other = lax.ppermute(run_half, "c", swap)
+    line = exchange(line, "y")
     ends, own_maps, own_values = call(
         run_block,
-        "run_block",
         (
             jax.ShapeDtypeStruct((nx, 3 * n // nc + 2 * part, n), BF16),
             jax.ShapeDtypeStruct((3 * n, n), BF16),
@@ -401,20 +420,18 @@
             pltpu.VMEM((ny, part, n), F32),
             pltpu.VMEM((3 * n, n), BF16),
             pltpu.VMEM((ny, 3 * n, n), BF16),
-            pltpu.SemaphoreType.DMA((ny,)),
         ],
         1,
         (16 * ny * n**3, 6 * ny * n * n),
         at_y,
         line,
-        run_maps,
-        far=1,
+        run_half,
+        run_other,
     )
     ends = lax.all_to_all(ends, "x", 0, 0)
     other_ends = lax.ppermute(ends, "c", swap)
     met = call(
         meet_values,
-        "meet_values",
         jax.ShapeDtypeStruct((peers, part, 2 * n), BF16),
         [pltpu.VMEM((part, 2 * n), F32), pltpu.VMEM((nx, 3 * n, n), BF16)],
         1,
@@ -436,7 +453,6 @@
     final_other = lax.ppermute(final_own, "c", swap)
     result = call(
         leaf_result,
-        "leaf_result",
         jax.ShapeDtypeStruct((leaf_nodes, columns), BF16),
         [pltpu.VMEM((interface, columns), F32), pltpu.VMEM((leaf_nodes, columns), F32)],
         1,

time: 180 us -> 188 us (1.044)
  blocking collectives: 40.7 us -> 67.5 us
  waiting for transfers between devices: 48.8 us -> 31.9 us
  matrix products: 8.72 us -> 2.33 us
    all_to_all x1 -> x3, blocking collectives: 20.3 us -> 47.1 us  [the longest x1 20.4 us: exchange(): return lax.all_to_all(value, axis, 0, 0)]
    all_to_all x4 -> x2, starting transfers between devices: 26.5 us -> 9.08 us  [exchange(): return lax.all_to_all(value, axis, 0, 0)]
    all_to_all x4 -> x2, waiting for transfers between devices: 38 us -> 22.7 us  [exchange(): return lax.all_to_all(value, axis, 0, 0)]
    ppermute x0 -> x1, starting transfers between devices: none -> 6.89 us  [on_device(): run_other = lax.ppermute(run_half, 'c', swap)]
    ppermute x1, starting transfers between devices: 2.02 us -> 8.75 us  [on_device(): got = lax.ppermute(send, 'c', swap)]
    dot_general x5 -> x0, matrix products: 6.38 us -> none  [the longest x1 2.27 us: on_device(): jnp.dot(late_map, (spot == want).astype(BF16), preferred_element_type=F32)]
    all_to_all x1, starting transfers between devices: 3.62 us -> 7.9 us  [on_device(): met_blocks = lax.all_to_all(met, GRP, 0, 0)]
    pallas_call x8 -> x9, Pallas kernels: 20.5 us -> 22.3 us  [call(): pl.pallas_call(kernel, out_shape=outs, in_specs=specs, out_specs=jax.tree...]
  transfers between devices with their start and end apart: 10 -> 9, of which waited for: 7 -> 6; matrix products, arithmetic and copies ran while one was open for 5% -> 1% of each run, Pallas kernels for 8% -> 9%
where the time goes in v6:
time: 188 us; the launch traced here: 187 us
  blocking collectives  67.5 us (36%)
  starting transfers between devices  39.6 us (21%)
  waiting for transfers between devices  31.9 us (17%)
  Pallas kernels  22.3 us (12%)
  between operations  15 us (8%)
  local copies, waits for them, and re-layouts  7.41 us (4%)
  matrix products  2.33 us (1%)
    all_to_all x2, waiting for transfers between devices, exchange(): return lax.all_to_all(value, axis, 0, 0)  22.7 us
    pallas_call x9, Pallas kernels, call(): pl.pallas_call(kernel, out_shape=outs, in_specs=specs, out_specs=jax.tree...  22.3 us
    all_to_all x1, blocking collectives, on_device(): final_own = lax.all_to_all(final, 'z', 0, 0).reshape(half, columns)  20.4 us
    all_to_all x1, blocking collectives, exchange(): return lax.all_to_all(value, axis, 0, 0)  20.4 us
    all_to_all x1, blocking collectives, on_device(): ends = lax.all_to_all(ends, 'x', 0, 0)  14.7 us
    all_to_all x1, blocking collectives, on_device(): faces = lax.all_to_all(faces, GRP, 0, 0)  12 us
    all_to_all x2, starting transfers between devices, exchange(): return lax.all_to_all(value, axis, 0, 0)  9.08 us
    ppermute x1, starting transfers between devices, on_device(): got = lax.ppermute(send, 'c', swap)  8.75 us
  transfers between devices with their start and end apart: 9, of which 6 were waited for; matrix products, arithmetic and copies ran while one was open for 1% of the time, Pallas kernels for 9%

profile of v6, /device:TPU:1, one launch (start us, length us, event | category | flops | bytes accessed | tf_op | source)
XLA Modules:
  0.0 187.0 jit_solution(18080331788190374817)
XLA Ops:
  7.4 0.7 fusion.5.pos
  8.1 1.6 copy-done.1
  9.7 0.9 copy-done.3
  10.6 2.6 %shard_map.65 = (bf16[2048,128]{1,0:T(8,128)(2,1)S(1)}, bf16[2048,128]{1,0:T(8,128)(2,1)S(1)}) custom-call(s32[1024]{0:T(1024)S(1)} %fusion.5.pos, bf16[1024,1024]{1,0:T(8,128)(2,1)S(1)} %bitcast.24, bf16[1024,128]{1,0:T(8,128)(2,1)S(1)} %bitcast.28), custom_call_target="tpu_custom_call" | custom-call | flops 268435456 | bytes 6291456 | tf_op jit(solution)/shard_map/pallas_call | solution.py:24
  13.2 8.7 %collective-permute-start = (bf16[2048,128]{1,0:T(8,128)(2,1)S(1)}, bf16[2048,128]{1,0:T(8,128)(2,1)S(1)}, u32[]{:S(2)}, u32[]{:S(2)}) collective-permute-start(bf16[2048,128]{1,0:T(8,128)(2,1)S(1)} %get-tuple-element.19), channel_id=1, source_target_pairs={{0,32},{32,0},{1,33},{33,1},{2,34},{34,2},{3,35},{35,3},{4,36},{36... | collective-permute-start | bytes 1572872 | tf_op jit(solution)/shard_map/ppermute | solution.py:355
  22.0 3.3 %shard_map.64 = bf16[16,112,128]{2,1,0:T(8,128)(2,1)} custom-call(bf16[256,4096]{1,0:T(8,128)(2,1)} %bitcast.22, f32[256,256]{1,0:T(8,128)S(1)} %bitcast.30, f32[256,256]{1,0:T(8,128)S(1)} %bitcast.32), custom_call_target="tpu_custom_call" | custom-call | flops 8388608 | bytes 2097152 | tf_op jit(solution)/shard_map/pallas_call | solution.py:24
  25.3 5.1 %all-to-all-start = ((bf16[16,112,128]{2,1,0:T(8,128)(2,1)}), bf16[16,112,128]{2,1,0:T(8,128)(2,1)S(1)}, u32[]{:S(2)}, u32[]{:S(2)}) async-start(bf16[16,112,128]{2,1,0:T(8,128)(2,1)} %shard_map.64), calls=%async_computation | async-start | bytes 917504 | tf_op jit(solution)/shard_map/all_to_all | solution.py:36
  30.6 15.7 %all-to-all-done.rows_ref.got_ref = bf16[16,112,128]{2,1,0:T(8,128)(2,1)S(1)} async-done(((bf16[16,112,128]{2,1,0:T(8,128)(2,1)}), bf16[16,112,128]{2,1,0:T(8,128)(2,1)S(1)}, u32[]{:S(2)}, u32[]{:S(2)}) %all-to-all-start) | async-done | bytes 458784 | tf_op jit(solution)/shard_map/all_to_all | solution.py:36
  46.2 0.7 shard_map.67
  47.0 20.4 %all_to_all.35.parts_ref = bf16[8,256,128]{2,1,0:T(8,128)(2,1)S(1)} all-to-all(bf16[8,256,128]{2,1,0:T(8,128)(2,1)S(1)} %bitcast.36), channel_id=1, replica_groups=mesh['z'=8,'c'=2,'x'=4,'y'=8] {'z'}, dimensions={0} | all-to-all | bytes 1048576 | tf_op jit(solution)/shard_map/all_to_all | solution.py:36
  67.4 0.7 shard_map.66
  68.1 12.0 %all_to_all.36.got_ref = bf16[16,8,512]{2,1,0:T(8,128)(2,1)S(1)} all-to-all(bf16[16,8,512]{2,1,0:T(8,128)(2,1)S(1)} %get-tuple-element.23), channel_id=1, replica_groups=mesh['z'=8,'c'=2,'x'=4,'y'=8] {'z','c'}, dimensions={0} | all-to-all | bytes 262144 | tf_op jit(solution)/shard_map/all_to_all | solution.py:393
  80.1 0.7 shard_map.68
  81.4 6.9 %collective-permute-start.1 = (bf16[8,768,128]{2,1,0:T(8,128)(2,1)}, bf16[8,768,128]{2,1,0:T(8,128)(2,1)S(1)}, u32[]{:S(2)}, u32[]{:S(2)}) collective-permute-start(bf16[8,768,128]{2,1,0:T(8,128)(2,1)} %bitcast.34), channel_id=1, source_target_pairs={{0,32},{32,0},{1,33},{33,1},{2,34},{34,2},{3,35},{35,3},{4,36},{36... | collective-permute-start | bytes 4718600 | tf_op jit(solution)/shard_map/ppermute | solution.py:406
  88.3 4.0 %all-to-all-start.3 = ((bf16[8,8,512]{2,1,0:T(8,128)(2,1)}), bf16[8,8,512]{2,1,0:T(8,128)(2,1)S(1)}, u32[]{:S(2)}, u32[]{:S(2)}) async-start(bf16[8,8,512]{2,1,0:T(8,128)(2,1)} %shard_map.68), calls=%async_computation.3 | async-start | bytes 131072 | tf_op jit(solution)/shard_map/all_to_all | solution.py:36
  92.4 7.1 %all-to-all-done.3.faces_ref = bf16[8,8,512]{2,1,0:T(8,128)(2,1)S(1)} async-done(((bf16[8,8,512]{2,1,0:T(8,128)(2,1)}), bf16[8,8,512]{2,1,0:T(8,128)(2,1)S(1)}, u32[]{:S(2)}, u32[]{:S(2)}) %all-to-all-start.3) | async-done | bytes 65568 | tf_op jit(solution)/shard_map/all_to_all | solution.py:36
  99.5 1.1 copy-done.12
  100.6 1.4 copy-done.11
  102.0 1.4 copy-done.13
  103.4 7.1 %shard_map.69 = (bf16[4,400,256]{2,1,0:T(8,128)(2,1)S(1)}, bf16[768,256]{1,0:T(8,128)(2,1)S(1)}, f32[8,512]{1,0:T(8,128)S(1)}) custom-call(s32[2]{0:T(128)S(1)} %pad_add_fusion.1.place, bf16[8,8,512]{2,1,0:T(8,128)(2,1)S(1)} %all-to-all-done.3.faces_ref, bf16[8,768,128]{2,1,0:T(8,128)(2,1)S(1)} %bitcast.35, bf16[8,768,128]{2,1,0:T(8,128)(2,1)S(1)} %copy-done.13), custom_call_target="tpu_custom_call" | custom-call | flops 2147483648 | bytes 3145728 | tf_op jit(solution)/shard_map/pallas_call | solution.py:24
  110.5 14.7 %all_to_all.37.ends_ref = bf16[4,400,256]{2,1,0:T(8,128)(2,1)S(1)} all-to-all(bf16[4,400,256]{2,1,0:T(8,128)(2,1)S(1)} %get-tuple-element.26), channel_id=1, replica_groups=mesh['z'=8,'c'=2,'x'=4,'y'=8] {'x'}, dimensions={0} | all-to-all | bytes 1638400 | tf_op jit(solution)/shard_map/all_to_all | solution.py:431
  125.2 4.6 %collective-permute-start.2 = (bf16[4,400,256]{2,1,0:T(8,128)(2,1)S(1)}, bf16[4,400,256]{2,1,0:T(8,128)(2,1)}, u32[]{:S(2)}, u32[]{:S(2)}) collective-permute-start(bf16[4,400,256]{2,1,0:T(8,128)(2,1)S(1)} %all_to_all.37.ends_ref), channel_id=1, source_target_pairs={{0,32},{32,0},{1,33},{33,1},{2,34},{34,2},{3,35},{35,3},{4,36},{36... | collective-permute-start | bytes 2457608 | tf_op jit(solution)/shard_map/ppermute | solution.py:432
  129.9 1.0 shard_map.71
  130.9 0.7 copy-done.7
  131.9 3.1 %shard_map.70 = bf16[16,8,512]{2,1,0:T(8,128)(2,1)} custom-call(s32[2]{0:T(128)S(1)} %pad_add_fusion.place, bf16[4,400,256]{2,1,0:T(8,128)(2,1)S(1)} %all_to_all.37.ends_ref, bf16[4,400,256]{2,1,0:T(8,128)(2,1)} %collective-permute-done.2.other_ref, bf16[768,256]{1,0:T(8,128)(2,1)S(1)} %copy-done.10, f32[8,512]{1,0:T(8,128)S(1)} %get-tuple-element.28.own_ref), custom_call_target="tpu_custom_call" | custom-call | flops 50331648 | bytes 1572864 | tf_op jit(solution)/shard_map/pallas_call | solution.py:24
  135.0 7.9 %all-to-all-start.5 = ((bf16[16,8,512]{2,1,0:T(8,128)(2,1)}), bf16[16,8,512]{2,1,0:T(8,128)(2,1)S(1)}, u32[]{:S(2)}, u32[]{:S(2)}) async-start(bf16[16,8,512]{2,1,0:T(8,128)(2,1)} %shard_map.70), calls=%async_computation.5 | async-start | bytes 262144 | tf_op jit(solution)/shard_map/all_to_all | solution.py:445
  142.9 2.1 %convolution_bitcast_fusion = f32[256,128]{0,1:T(8,128)S(1)} fusion(bf16[4096,128]{1,0:T(8,128)(2,1)} %all-gather.4.cloned.1.call-done, bf16[1,256,4096]{2,1,0:T(8,128)(2,1)S(1)} %copy-done), kind=kOutput, calls=%fused_computation.1 | convolution fusion | flops 268435456 | bytes 3276800 | tf_op jit(solution)/shard_map/dot_general | solution.py:448
  145.1 6.7 %all-to-all-done.5 = bf16[16,8,512]{2,1,0:T(8,128)(2,1)S(1)} async-done(((bf16[16,8,512]{2,1,0:T(8,128)(2,1)}), bf16[16,8,512]{2,1,0:T(8,128)(2,1)S(1)}, u32[]{:S(2)}, u32[]{:S(2)}) %all-to-all-start.5) | async-done | bytes 131104 | tf_op jit(solution)/shard_map/all_to_all | solution.py:445
  152.2 20.4 %all_to_all.38 = bf16[8,256,128]{2,1,0:T(8,128)(2,1)S(1)} all-to-all(bf16[8,256,128]{2,1,0:T(8,128)(2,1)S(1)} %broadcast_in_dim.6), channel_id=1, replica_groups=mesh['z'=8,'c'=2,'x'=4,'y'=8] {'z'}, dimensions={0} | all-to-all | bytes 1048576 | tf_op jit(solution)/shard_map/all_to_all | solution.py:452
  172.6 2.4 %collective-permute-start.3 = (bf16[2048,128]{1,0:T(8,128)(2,1)S(1)}, bf16[2048,128]{1,0:T(8,128)(2,1)S(1)}, u32[]{:S(2)}, u32[]{:S(2)}) collective-permute-start(bf16[2048,128]{1,0:T(8,128)(2,1)S(1)} %bitcast.26), channel_id=1, source_target_pairs={{0,32},{32,0},{1,33},{33,1},{2,34},{34,2},{3,35},{35,3},{4,36},{36... | collective-permute-start | bytes 1572872 | tf_op jit(solution)/shard_map/ppermute | solution.py:453
  175.0 1.5 collective-permute-done.3.other_ref
  176.5 3.1 %shard_map.72 = bf16[1024,128]{1,0:T(8,128)(2,1)} custom-call(s32[1024]{0:T(1024)S(1)} %fusion.5.pos, bf16[2048,128]{1,0:T(8,128)(2,1)S(1)} %bitcast.27, bf16[2048,128]{1,0:T(8,128)(2,1)S(1)} %collective-permute-done.3.other_ref, bf16[1024,1024]{1,0:T(8,128)(2,1)S(1)} %bitcast.25, bf16[1024,128]{1,0:T(8,128)(2,1)S(1)} %bitcast.29), custom_call_target="tpu_custom_call" | custom-call | flops 268435456 | bytes 2097152 | tf_op jit(solution)/shard_map/pallas_call | solution.py:24
  (37 shorter events, 1.7 us)
Async XLA Ops:
  8.1 1.6 copy-start.1
  9.7 0.9 copy-start.3
  10.6 11.3 %copy-start.5 = (f32[1,256,256]{2,1,0:T(8,128)S(1)}, f32[1,256,256]{2,1,0:T(8,128)}, u32[]{:S(2)}) copy-start(f32[1,256,256]{2,1,0:T(8,128)} %param.10) | copy-start | bytes 786436
  10.6 11.3 %copy-start.6 = (f32[1,256,256]{2,1,0:T(8,128)S(1)}, f32[1,256,256]{2,1,0:T(8,128)}, u32[]{:S(2)}) copy-start(f32[1,256,256]{2,1,0:T(8,128)} %param.11) | copy-start | bytes 786436
  13.2 17.2 %collective-permute-start = (bf16[2048,128]{1,0:T(8,128)(2,1)S(1)}, bf16[2048,128]{1,0:T(8,128)(2,1)S(1)}, u32[]{:S(2)}, u32[]{:S(2)}) collective-permute-start(bf16[2048,128]{1,0:T(8,128)(2,1)S(1)} %get-tuple-element.19), channel_id=1, source_target_pairs={{0,32},{32,0},{1,33},{33,1},{2,34},{34,2},{3,35},{35,3},{4,36},{36... | collective-permute-start | bytes 1572872 | tf_op jit(solution)/shard_map/ppermute | solution.py:355
  25.3 21.0 %all-to-all-start = ((bf16[16,112,128]{2,1,0:T(8,128)(2,1)}), bf16[16,112,128]{2,1,0:T(8,128)(2,1)S(1)}, u32[]{:S(2)}, u32[]{:S(2)}) async-start(bf16[16,112,128]{2,1,0:T(8,128)(2,1)} %shard_map.64), calls=%async_computation | async-start | bytes 917504 | tf_op jit(solution)/shard_map/all_to_all | solution.py:36
  30.4 51.1 %all-gather.6.cloned.1.call-start = ((), (), s32[]{:S(2)}) async-start(), calls=%async_computation.8 | async-start | bytes 1769472 | tf_op jit(solution)/shard_map/all_gather | solution.py:366
  46.9 96.0 %all-gather.4.cloned.1.call-start = ((), (), s32[]{:S(2)}) async-start(), calls=%async_computation.7 | async-start | bytes 1114112 | tf_op jit(solution)/shard_map/all_gather | solution.py:403
  81.4 18.0 %collective-permute-start.1 = (bf16[8,768,128]{2,1,0:T(8,128)(2,1)}, bf16[8,768,128]{2,1,0:T(8,128)(2,1)S(1)}, u32[]{:S(2)}, u32[]{:S(2)}) collective-permute-start(bf16[8,768,128]{2,1,0:T(8,128)(2,1)} %bitcast.34), channel_id=1, source_target_pairs={{0,32},{32,0},{1,33},{33,1},{2,34},{34,2},{3,35},{35,3},{4,36},{36... | collective-permute-start | bytes 4718600 | tf_op jit(solution)/shard_map/ppermute | solution.py:406
  88.3 11.1 %all-to-all-start.3 = ((bf16[8,8,512]{2,1,0:T(8,128)(2,1)}), bf16[8,8,512]{2,1,0:T(8,128)(2,1)S(1)}, u32[]{:S(2)}, u32[]{:S(2)}) async-start(bf16[8,8,512]{2,1,0:T(8,128)(2,1)} %shard_map.68), calls=%async_computation.3 | async-start | bytes 131072 | tf_op jit(solution)/shard_map/all_to_all | solution.py:36
  99.5 1.1 copy-start.12
  100.6 1.4 copy-start.11
  102.0 1.4 copy-start.13
  103.4 26.5 %copy-start = (bf16[1,256,4096]{2,1,0:T(8,128)(2,1)S(1)}, bf16[1,256,4096]{2,1,0:T(8,128)(2,1)}, u32[]{:S(2)}) copy-start(bf16[1,256,4096]{2,1,0:T(8,128)(2,1)} %param.8) | copy-start | bytes 6291460
  110.5 14.7 %copy-start.9 = (bf16[768,256]{1,0:T(8,128)(2,1)}, bf16[768,256]{1,0:T(8,128)(2,1)S(1)}, u32[]{:S(2)}) copy-start(bf16[768,256]{1,0:T(8,128)(2,1)S(1)} %get-tuple-element.27.maps_ref) | copy-start | bytes 1179652
  125.2 6.7 %collective-permute-start.2 = (bf16[4,400,256]{2,1,0:T(8,128)(2,1)S(1)}, bf16[4,400,256]{2,1,0:T(8,128)(2,1)}, u32[]{:S(2)}, u32[]{:S(2)}) collective-permute-start(bf16[4,400,256]{2,1,0:T(8,128)(2,1)S(1)} %all_to_all.37.ends_ref), channel_id=1, source_target_pairs={{0,32},{32,0},{1,33},{33,1},{2,34},{34,2},{3,35},{35,3},{4,36},{36... | collective-permute-start | bytes 2457608 | tf_op jit(solution)/shard_map/ppermute | solution.py:432
  129.8 2.1 %copy-start.10 = (bf16[768,256]{1,0:T(8,128)(2,1)S(1)}, bf16[768,256]{1,0:T(8,128)(2,1)}, u32[]{:S(2)}) copy-start(bf16[768,256]{1,0:T(8,128)(2,1)} %copy-done.9) | copy-start | bytes 1179652
  130.9 0.7 copy-start.7
  135.0 16.8 %copy-start.8 = (bf16[256,512]{1,0:T(8,128)(2,1)S(1)}, bf16[256,512]{1,0:T(8,128)(2,1)}, u32[]{:S(2)}) copy-start(bf16[256,512]{1,0:T(8,128)(2,1)} %copy-done.7) | copy-start | bytes 786436
  135.0 16.8 %all-to-all-start.5 = ((bf16[16,8,512]{2,1,0:T(8,128)(2,1)}), bf16[16,8,512]{2,1,0:T(8,128)(2,1)S(1)}, u32[]{:S(2)}, u32[]{:S(2)}) async-start(bf16[16,8,512]{2,1,0:T(8,128)(2,1)} %shard_map.70), calls=%async_computation.5 | async-start | bytes 262144 | tf_op jit(solution)/shard_map/all_to_all | solution.py:445
  142.9 33.6 %copy-start.4 = (bf16[1,1,1024,128]{3,2,1,0:T(8,128)(2,1)S(1)}, bf16[1,1,1024,128]{3,2,1,0:T(8,128)(2,1)}, u32[]{:S(2)}) copy-start(bf16[1,1,1024,128]{3,2,1,0:T(8,128)(2,1)} %param.6) | copy-start | bytes 786436
  145.0 31.4 %copy-start.2 = (bf16[1,1,1024,1024]{3,2,1,0:T(8,128)(2,1)S(1)}, bf16[1,1,1024,1024]{3,2,1,0:T(8,128)(2,1)}, u32[]{:S(2)}) copy-start(bf16[1,1,1024,1024]{3,2,1,0:T(8,128)(2,1)} %param.7) | copy-start | bytes 6291460
  172.6 3.9 %collective-permute-start.3 = (bf16[2048,128]{1,0:T(8,128)(2,1)S(1)}, bf16[2048,128]{1,0:T(8,128)(2,1)S(1)}, u32[]{:S(2)}, u32[]{:S(2)}) collective-permute-start(bf16[2048,128]{1,0:T(8,128)(2,1)S(1)} %bitcast.26), channel_id=1, source_target_pairs={{0,32},{32,0},{1,33},{33,1},{2,34},{34,2},{3,35},{35,3},{4,36},{36... | collective-permute-start | bytes 1572872 | tf_op jit(solution)/shard_map/ppermute | solution.py:453
Sparse Core Ops, SparseCore 0:
  47.0 34.3 all-gather.5
Sparse Core Ops, SparseCore 1:
  88.4 40.6 all-gather.3

commit v7 on v6

--- a/solution.py
+++ b/solution.py
@@ -178,13 +178,28 @@
 
 
 def run_block(place, faces_ref, mine_ref, other_ref, ends_ref, own_maps_ref, own_ref, *scratch):
-    state, right, through, given, sources, joined, maps_ref = scratch
+    state, right, through, given, sources, joined = scratch
     count, part, _ = faces_ref.shape
     slim = mine_ref.shape[2]
-    n = maps_ref.shape[2]
+    n = state.shape[0]
     here, side = place[0], place[1]
-    maps_ref[:, :, pl.ds(pl.multiple_of(side * slim, slim), slim)] = mine_ref[...]
-    maps_ref[:, :, pl.ds(pl.multiple_of((1 - side) * slim, slim), slim)] = other_ref[...]
+
+    def halves_at(start):
+        first = pl.multiple_of(start + side * slim, slim)
+        second = pl.multiple_of(start + (1 - side) * slim, slim)
+        return pl.ds(first, slim), pl.ds(second, slim)
+
+    def maps_at(j, rows):
+        return jnp.concatenate([mine_ref[j, rows, :], other_ref[j, rows, :]], axis=1)
+
+    def rows_met(ref):
+        first, second = halves_at(0)
+        return jnp.concatenate([ref[first, :], ref[second, :]], axis=0)
+
+    def lanes_met(start):
+        first, second = halves_at(start)
+        return jnp.concatenate([given[:, first], given[:, second]], axis=1)
+
     unit = (
         lax.broadcasted_iota(jnp.int32, (n, n), 0) == lax.broadcasted_iota(jnp.int32, (n, n), 1)
     ).astype(F32)
@@ -194,17 +209,14 @@
     given[...] = jnp.zeros_like(given)
 
     def onward(j, carry):
-        value = state[...]
-        east = given[:, 0:n]
-
         @pl.when(j == here)
         def _():
-            own_maps_ref[0:n] = value.astype(BF16)
-            own_ref[:, 0:n] = east
-
-        maps = maps_ref[j, 0 : 2 * n, :]
-        both = exact_right(maps, value)
-        moved = faces_ref[j].astype(F32) + exact_rows(east, maps)
+            own_maps_ref[0:n] = state[...].astype(BF16)
+            own_ref[:, 0:n] = given[:, 0:n]
+
+        maps = maps_at(j, slice(0, 2 * n))
+        both = exact_right(maps, rows_met(state))
+        moved = faces_ref[j].astype(F32) + exact_rows(lanes_met(0), maps)
         state[...] = both[:n]
         through[j] = both[n:]
         given[:, 0:n] = moved[:, 0:n]
@@ -215,18 +227,16 @@
 
     def back(turn, carry):
         j = count - 1 - turn
-        value = right[...]
-        west = given[:, n : 2 * n]
 
         @pl.when(j == here)
         def _():
-            own_maps_ref[n : 2 * n] = value[:, 0:n].astype(BF16)
-            own_maps_ref[2 * n : 3 * n] = value[:, n : 2 * n].astype(BF16)
-            own_ref[:, n : 2 * n] = west
-
-        maps = maps_ref[j, 2 * n : 3 * n, :]
-        both = exact_right(maps, value)
-        moved = sources[j] + exact_rows(west, maps)
+            own_maps_ref[n : 2 * n] = right[:, 0:n].astype(BF16)
+            own_maps_ref[2 * n : 3 * n] = right[:, n : 2 * n].astype(BF16)
+            own_ref[:, n : 2 * n] = given[:, n : 2 * n]
+
+        maps = maps_at(j, slice(2 * n, 3 * n))
+        both = exact_right(maps, rows_met(right))
+        moved = sources[j] + exact_rows(lanes_met(n), maps)
         right[:, 0:n] = both[:, 0:n]
         right[:, n : 2 * n] = both[:, n : 2 * n] + through[j]
         given[:, n : 2 * n] = moved
@@ -402,7 +412,6 @@
 
     all_loads = lax.all_gather(loads, GRP, axis=0, tiled=True)
 
-    run_half, line = lax.optimization_barrier((run_half, line))
     run_other = lax.ppermute(run_half, "c", swap)
     line = exchange(line, "y")
     ends, own_maps, own_values = call(
@@ -419,7 +428,6 @@
             pltpu.VMEM((part, 2 * n), F32),
             pltpu.VMEM((ny, part, n), F32),
             pltpu.VMEM((3 * n, n), BF16),
-            pltpu.VMEM((ny, 3 * n, n), BF16),
         ],
         1,
         (16 * ny * n**3, 6 * ny * n * n),

time: 188 us -> 223 us (1.19)
  waiting for transfers between devices: 31.9 us -> 75.5 us
  blocking collectives: 67.5 us -> 60 us
    all_gather x1, waiting for transfers between devices: 0.6 us -> 34.5 us  [on_device(): run_half = lax.all_gather(maps, 'y')]
    all_to_all x1 -> x0, blocking collectives: 12 us -> none  [on_device(): faces = lax.all_to_all(faces, GRP, 0, 0)]
    all_to_all x0 -> x1, waiting for transfers between devices: none -> 8.61 us  [on_device(): faces = lax.all_to_all(faces, GRP, 0, 0)]
    all_to_all x1, blocking collectives: 20.4 us -> 24.9 us  [exchange(): return lax.all_to_all(value, axis, 0, 0)]
    all_to_all x1, starting transfers between devices: 7.9 us -> 3.8 us  [on_device(): met_blocks = lax.all_to_all(met, GRP, 0, 0)]
    all_to_all x0 -> x1, starting transfers between devices: none -> 3.77 us  [on_device(): faces = lax.all_to_all(faces, GRP, 0, 0)]
  transfers between devices with their start and end apart: 9 -> 10, of which waited for: 6 -> 7; matrix products, arithmetic and copies ran while one was open for 1% -> 1% of each run, Pallas kernels for 9% -> 7%
where the time goes in v7:
time: 223 us; the launch traced here: 222 us
  waiting for transfers between devices  75.5 us (34%)
  blocking collectives  60 us (27%)
  starting transfers between devices  39.2 us (18%)
  Pallas kernels  21.7 us (10%)
  between operations  15 us (7%)
  local copies, waits for them, and re-layouts  7.42 us (3%)
  matrix products  2.33 us (1%)
    all_gather x1, waiting for transfers between devices, on_device(): run_half = lax.all_gather(maps, 'y')  34.5 us
    all_to_all x1, blocking collectives, exchange(): return lax.all_to_all(value, axis, 0, 0)  24.9 us
    all_to_all x2, waiting for transfers between devices, exchange(): return lax.all_to_all(value, axis, 0, 0)  23 us
    pallas_call x9, Pallas kernels, call(): pl.pallas_call(kernel, out_shape=outs, in_specs=specs, out_specs=jax.tree...  21.7 us
    all_to_all x1, blocking collectives, on_device(): final_own = lax.all_to_all(final, 'z', 0, 0).reshape(half, columns)  20.4 us
    all_to_all x1, blocking collectives, on_device(): ends = lax.all_to_all(ends, 'x', 0, 0)  14.7 us
    all_to_all x2, starting transfers between devices, exchange(): return lax.all_to_all(value, axis, 0, 0)  9.13 us
    ppermute x1, starting transfers between devices, on_device(): got = lax.ppermute(send, 'c', swap)  8.75 us
  transfers between devices with their start and end apart: 10, of which 7 were waited for; matrix products, arithmetic and copies ran while one was open for 1% of the time, Pallas kernels for 7%

profile of v7, /device:TPU:1, one launch (start us, length us, event | category | flops | bytes accessed | tf_op | source)
XLA Modules:
  0.0 222.1 jit_solution(10511229582215099874)
XLA Ops:
  7.4 0.7 fusion.5.pos
  8.1 1.6 copy-done.1
  9.7 0.9 copy-done.3
  10.6 2.6 %shard_map.65 = (bf16[2048,128]{1,0:T(8,128)(2,1)S(1)}, bf16[2048,128]{1,0:T(8,128)(2,1)S(1)}) custom-call(s32[1024]{0:T(1024)S(1)} %fusion.5.pos, bf16[1024,1024]{1,0:T(8,128)(2,1)S(1)} %bitcast.24, bf16[1024,128]{1,0:T(8,128)(2,1)S(1)} %bitcast.28), custom_call_target="tpu_custom_call" | custom-call | flops 268435456 | bytes 6291456 | tf_op jit(solution)/shard_map/pallas_call | solution.py:24
  13.2 8.7 %collective-permute-start = (bf16[2048,128]{1,0:T(8,128)(2,1)S(1)}, bf16[2048,128]{1,0:T(8,128)(2,1)S(1)}, u32[]{:S(2)}, u32[]{:S(2)}) collective-permute-start(bf16[2048,128]{1,0:T(8,128)(2,1)S(1)} %get-tuple-element.17), channel_id=1, source_target_pairs={{0,32},{32,0},{1,33},{33,1},{2,34},{34,2},{3,35},{35,3},{4,36},{36... | collective-permute-start | bytes 1572872 | tf_op jit(solution)/shard_map/ppermute | solution.py:365
  22.0 3.3 %shard_map.64 = bf16[16,112,128]{2,1,0:T(8,128)(2,1)} custom-call(bf16[256,4096]{1,0:T(8,128)(2,1)} %bitcast.22, f32[256,256]{1,0:T(8,128)S(1)} %bitcast.30, f32[256,256]{1,0:T(8,128)S(1)} %bitcast.32), custom_call_target="tpu_custom_call" | custom-call | flops 8388608 | bytes 2097152 | tf_op jit(solution)/shard_map/pallas_call | solution.py:24
  25.3 5.1 %all-to-all-start = ((bf16[16,112,128]{2,1,0:T(8,128)(2,1)}), bf16[16,112,128]{2,1,0:T(8,128)(2,1)S(1)}, u32[]{:S(2)}, u32[]{:S(2)}) async-start(bf16[16,112,128]{2,1,0:T(8,128)(2,1)} %shard_map.64), calls=%async_computation | async-start | bytes 917504 | tf_op jit(solution)/shard_map/all_to_all | solution.py:36
  30.6 15.7 %all-to-all-done.rows_ref.got_ref = bf16[16,112,128]{2,1,0:T(8,128)(2,1)S(1)} async-done(((bf16[16,112,128]{2,1,0:T(8,128)(2,1)}), bf16[16,112,128]{2,1,0:T(8,128)(2,1)S(1)}, u32[]{:S(2)}, u32[]{:S(2)}) %all-to-all-start) | async-done | bytes 458784 | tf_op jit(solution)/shard_map/all_to_all | solution.py:36
  46.9 34.5 %all-gather.6.cloned.1.call-done = bf16[6144,128]{1,0:T(8,128)(2,1)} async-done(((bf16[768,128]{1,0:T(8,128)(2,1)}), bf16[6144,128]{1,0:T(8,128)(2,1)}) %all-gather.6.cloned.1.call-update) | async-done | bytes 1572880 | tf_op jit(solution)/shard_map/all_gather | solution.py:376
  81.4 6.8 %collective-permute-start.1 = (bf16[8,768,128]{2,1,0:T(8,128)(2,1)}, bf16[8,768,128]{2,1,0:T(8,128)(2,1)S(1)}, u32[]{:S(2)}, u32[]{:S(2)}) collective-permute-start(bf16[8,768,128]{2,1,0:T(8,128)(2,1)} %bitcast.34), channel_id=1, source_target_pairs={{0,32},{32,0},{1,33},{33,1},{2,34},{34,2},{3,35},{35,3},{4,36},{36... | collective-permute-start | bytes 4718600 | tf_op jit(solution)/shard_map/ppermute | solution.py:415
  88.3 24.9 %all_to_all.35.parts_ref = bf16[8,256,128]{2,1,0:T(8,128)(2,1)S(1)} all-to-all(bf16[8,256,128]{2,1,0:T(8,128)(2,1)S(1)} %bitcast.36), channel_id=1, replica_groups=mesh['z'=8,'c'=2,'x'=4,'y'=8] {'z'}, dimensions={0} | all-to-all | bytes 1048576 | tf_op jit(solution)/shard_map/all_to_all | solution.py:36
  113.1 1.0 shard_map.66
  114.1 3.8 %all-to-all-start.2 = ((bf16[16,8,512]{2,1,0:T(8,128)(2,1)}), bf16[16,8,512]{2,1,0:T(8,128)(2,1)S(1)}, u32[]{:S(2)}, u32[]{:S(2)}) async-start(bf16[16,8,512]{2,1,0:T(8,128)(2,1)} %get-tuple-element.21), calls=%async_computation.2 | async-start | bytes 262144 | tf_op jit(solution)/shard_map/all_to_all | solution.py:403
  118.4 8.6 %all-to-all-done.2.got_ref = bf16[16,8,512]{2,1,0:T(8,128)(2,1)S(1)} async-done(((bf16[16,8,512]{2,1,0:T(8,128)(2,1)}), bf16[16,8,512]{2,1,0:T(8,128)(2,1)S(1)}, u32[]{:S(2)}, u32[]{:S(2)}) %all-to-all-start.2) | async-done | bytes 131104 | tf_op jit(solution)/shard_map/all_to_all | solution.py:403
  127.7 4.0 %all-to-all-start.3 = ((bf16[8,8,512]{2,1,0:T(8,128)(2,1)}), bf16[8,8,512]{2,1,0:T(8,128)(2,1)S(1)}, u32[]{:S(2)}, u32[]{:S(2)}) async-start(bf16[8,8,512]{2,1,0:T(8,128)(2,1)} %shard_map.67), calls=%async_computation.3 | async-start | bytes 131072 | tf_op jit(solution)/shard_map/all_to_all | solution.py:36
  131.8 7.4 %all-to-all-done.3.faces_ref = bf16[8,8,512]{2,1,0:T(8,128)(2,1)S(1)} async-done(((bf16[8,8,512]{2,1,0:T(8,128)(2,1)}), bf16[8,8,512]{2,1,0:T(8,128)(2,1)S(1)}, u32[]{:S(2)}, u32[]{:S(2)}) %all-to-all-start.3) | async-done | bytes 65568 | tf_op jit(solution)/shard_map/all_to_all | solution.py:36
  139.2 1.2 copy-done.12
  140.3 1.4 copy-done.11
  141.7 1.4 copy-done.13
  143.2 6.2 %shard_map.69 = (bf16[4,400,256]{2,1,0:T(8,128)(2,1)S(1)}, bf16[768,256]{1,0:T(8,128)(2,1)S(1)}, f32[8,512]{1,0:T(8,128)S(1)}) custom-call(s32[2]{0:T(128)S(1)} %pad_add_fusion.1.place, bf16[8,8,512]{2,1,0:T(8,128)(2,1)S(1)} %all-to-all-done.3.faces_ref, bf16[8,768,128]{2,1,0:T(8,128)(2,1)S(1)} %bitcast.35, bf16[8,768,128]{2,1,0:T(8,128)(2,1)S(1)} %copy-done.13), custom_call_target="tpu_custom_call" | custom-call | flops 2147483648 | bytes 3145728 | tf_op jit(solution)/shard_map/pallas_call | solution.py:24
  149.4 14.7 %all_to_all.36.ends_ref = bf16[4,400,256]{2,1,0:T(8,128)(2,1)S(1)} all-to-all(bf16[4,400,256]{2,1,0:T(8,128)(2,1)S(1)} %get-tuple-element.22), channel_id=1, replica_groups=mesh['z'=8,'c'=2,'x'=4,'y'=8] {'x'}, dimensions={0} | all-to-all | bytes 1638400 | tf_op jit(solution)/shard_map/all_to_all | solution.py:439
  164.1 4.5 %collective-permute-start.2 = (bf16[4,400,256]{2,1,0:T(8,128)(2,1)S(1)}, bf16[4,400,256]{2,1,0:T(8,128)(2,1)}, u32[]{:S(2)}, u32[]{:S(2)}) collective-permute-start(bf16[4,400,256]{2,1,0:T(8,128)(2,1)S(1)} %all_to_all.36.ends_ref), channel_id=1, source_target_pairs={{0,32},{32,0},{1,33},{33,1},{2,34},{34,2},{3,35},{35,3},{4,36},{36... | collective-permute-start | bytes 2457608 | tf_op jit(solution)/shard_map/ppermute | solution.py:440
  168.8 1.0 shard_map.71
  169.8 0.7 copy-done.7
  170.8 3.1 %shard_map.70 = bf16[16,8,512]{2,1,0:T(8,128)(2,1)} custom-call(s32[2]{0:T(128)S(1)} %pad_add_fusion.place, bf16[4,400,256]{2,1,0:T(8,128)(2,1)S(1)} %all_to_all.36.ends_ref, bf16[4,400,256]{2,1,0:T(8,128)(2,1)} %collective-permute-done.2.other_ref, bf16[768,256]{1,0:T(8,128)(2,1)S(1)} %copy-done.10, f32[8,512]{1,0:T(8,128)S(1)} %get-tuple-element.24.own_ref), custom_call_target="tpu_custom_call" | custom-call | flops 50331648 | bytes 1572864 | tf_op jit(solution)/shard_map/pallas_call | solution.py:24
  173.9 3.8 %all-to-all-start.5 = ((bf16[16,8,512]{2,1,0:T(8,128)(2,1)}), bf16[16,8,512]{2,1,0:T(8,128)(2,1)S(1)}, u32[]{:S(2)}, u32[]{:S(2)}) async-start(bf16[16,8,512]{2,1,0:T(8,128)(2,1)} %shard_map.70), calls=%async_computation.5 | async-start | bytes 262144 | tf_op jit(solution)/shard_map/all_to_all | solution.py:453
  177.7 2.1 convolution_bitcast_fusion
  179.8 7.0 %all-to-all-done.5 = bf16[16,8,512]{2,1,0:T(8,128)(2,1)S(1)} async-done(((bf16[16,8,512]{2,1,0:T(8,128)(2,1)}), bf16[16,8,512]{2,1,0:T(8,128)(2,1)S(1)}, u32[]{:S(2)}, u32[]{:S(2)}) %all-to-all-start.5) | async-done | bytes 131104 | tf_op jit(solution)/shard_map/all_to_all | solution.py:453
  187.3 20.4 %all_to_all.37 = bf16[8,256,128]{2,1,0:T(8,128)(2,1)S(1)} all-to-all(bf16[8,256,128]{2,1,0:T(8,128)(2,1)S(1)} %broadcast_in_dim.6), channel_id=1, replica_groups=mesh['z'=8,'c'=2,'x'=4,'y'=8] {'z'}, dimensions={0} | all-to-all | bytes 1048576 | tf_op jit(solution)/shard_map/all_to_all | solution.py:460
  207.7 2.3 %collective-permute-start.3 = (bf16[2048,128]{1,0:T(8,128)(2,1)S(1)}, bf16[2048,128]{1,0:T(8,128)(2,1)S(1)}, u32[]{:S(2)}, u32[]{:S(2)}) collective-permute-start(bf16[2048,128]{1,0:T(8,128)(2,1)S(1)} %bitcast.26), channel_id=1, source_target_pairs={{0,32},{32,0},{1,33},{33,1},{2,34},{34,2},{3,35},{35,3},{4,36},{36... | collective-permute-start | bytes 1572872 | tf_op jit(solution)/shard_map/ppermute | solution.py:461
  210.0 1.5 collective-permute-done.3.other_ref
  211.6 3.1 %shard_map.72 = bf16[1024,128]{1,0:T(8,128)(2,1)} custom-call(s32[1024]{0:T(1024)S(1)} %fusion.5.pos, bf16[2048,128]{1,0:T(8,128)(2,1)S(1)} %bitcast.27, bf16[2048,128]{1,0:T(8,128)(2,1)S(1)} %collective-permute-done.3.other_ref, bf16[1024,1024]{1,0:T(8,128)(2,1)S(1)} %bitcast.25, bf16[1024,128]{1,0:T(8,128)(2,1)S(1)} %bitcast.29), custom_call_target="tpu_custom_call" | custom-call | flops 268435456 | bytes 2097152 | tf_op jit(solution)/shard_map/pallas_call | solution.py:24
  (38 shorter events, 3.0 us)
Async XLA Ops:
  8.1 1.6 copy-start.1
  9.7 0.9 copy-start.3
  10.6 11.3 %copy-start.5 = (f32[1,256,256]{2,1,0:T(8,128)S(1)}, f32[1,256,256]{2,1,0:T(8,128)}, u32[]{:S(2)}) copy-start(f32[1,256,256]{2,1,0:T(8,128)} %param.10) | copy-start | bytes 786436
  10.6 11.3 %copy-start.6 = (f32[1,256,256]{2,1,0:T(8,128)S(1)}, f32[1,256,256]{2,1,0:T(8,128)}, u32[]{:S(2)}) copy-start(f32[1,256,256]{2,1,0:T(8,128)} %param.11) | copy-start | bytes 786436
  13.2 17.2 %collective-permute-start = (bf16[2048,128]{1,0:T(8,128)(2,1)S(1)}, bf16[2048,128]{1,0:T(8,128)(2,1)S(1)}, u32[]{:S(2)}, u32[]{:S(2)}) collective-permute-start(bf16[2048,128]{1,0:T(8,128)(2,1)S(1)} %get-tuple-element.17), channel_id=1, source_target_pairs={{0,32},{32,0},{1,33},{33,1},{2,34},{34,2},{3,35},{35,3},{4,36},{36... | collective-permute-start | bytes 1572872 | tf_op jit(solution)/shard_map/ppermute | solution.py:365
  25.3 21.0 %all-to-all-start = ((bf16[16,112,128]{2,1,0:T(8,128)(2,1)}), bf16[16,112,128]{2,1,0:T(8,128)(2,1)S(1)}, u32[]{:S(2)}, u32[]{:S(2)}) async-start(bf16[16,112,128]{2,1,0:T(8,128)(2,1)} %shard_map.64), calls=%async_computation | async-start | bytes 917504 | tf_op jit(solution)/shard_map/all_to_all | solution.py:36
  30.4 51.1 %all-gather.6.cloned.1.call-start = ((), (), s32[]{:S(2)}) async-start(), calls=%async_computation.8 | async-start | bytes 1769472 | tf_op jit(solution)/shard_map/all_gather | solution.py:376
  81.4 57.7 %collective-permute-start.1 = (bf16[8,768,128]{2,1,0:T(8,128)(2,1)}, bf16[8,768,128]{2,1,0:T(8,128)(2,1)S(1)}, u32[]{:S(2)}, u32[]{:S(2)}) collective-permute-start(bf16[8,768,128]{2,1,0:T(8,128)(2,1)} %bitcast.34), channel_id=1, source_target_pairs={{0,32},{32,0},{1,33},{33,1},{2,34},{34,2},{3,35},{35,3},{4,36},{36... | collective-permute-start | bytes 4718600 | tf_op jit(solution)/shard_map/ppermute | solution.py:415
  114.1 13.0 %all-to-all-start.2 = ((bf16[16,8,512]{2,1,0:T(8,128)(2,1)}), bf16[16,8,512]{2,1,0:T(8,128)(2,1)S(1)}, u32[]{:S(2)}, u32[]{:S(2)}) async-start(bf16[16,8,512]{2,1,0:T(8,128)(2,1)} %get-tuple-element.21), calls=%async_computation.2 | async-start | bytes 262144 | tf_op jit(solution)/shard_map/all_to_all | solution.py:403
  117.9 59.8 %all-gather.4.cloned.1.call-start = ((), (), s32[]{:S(2)}) async-start(), calls=%async_computation.7 | async-start | bytes 1114112 | tf_op jit(solution)/shard_map/all_gather | solution.py:413
  127.7 11.5 %all-to-all-start.3 = ((bf16[8,8,512]{2,1,0:T(8,128)(2,1)}), bf16[8,8,512]{2,1,0:T(8,128)(2,1)S(1)}, u32[]{:S(2)}, u32[]{:S(2)}) async-start(bf16[8,8,512]{2,1,0:T(8,128)(2,1)} %shard_map.67), calls=%async_computation.3 | async-start | bytes 131072 | tf_op jit(solution)/shard_map/all_to_all | solution.py:36
  139.2 1.2 copy-start.12
  140.3 1.4 copy-start.11
  141.7 1.4 copy-start.13
  143.2 25.6 %copy-start = (bf16[1,256,4096]{2,1,0:T(8,128)(2,1)S(1)}, bf16[1,256,4096]{2,1,0:T(8,128)(2,1)}, u32[]{:S(2)}) copy-start(bf16[1,256,4096]{2,1,0:T(8,128)(2,1)} %param.8) | copy-start | bytes 6291460
  149.4 14.7 %copy-start.9 = (bf16[768,256]{1,0:T(8,128)(2,1)}, bf16[768,256]{1,0:T(8,128)(2,1)S(1)}, u32[]{:S(2)}) copy-start(bf16[768,256]{1,0:T(8,128)(2,1)S(1)} %get-tuple-element.23.maps_ref) | copy-start | bytes 1179652
  164.1 6.6 %collective-permute-start.2 = (bf16[4,400,256]{2,1,0:T(8,128)(2,1)S(1)}, bf16[4,400,256]{2,1,0:T(8,128)(2,1)}, u32[]{:S(2)}, u32[]{:S(2)}) collective-permute-start(bf16[4,400,256]{2,1,0:T(8,128)(2,1)S(1)} %all_to_all.36.ends_ref), channel_id=1, source_target_pairs={{0,32},{32,0},{1,33},{33,1},{2,34},{34,2},{3,35},{35,3},{4,36},{36... | collective-permute-start | bytes 2457608 | tf_op jit(solution)/shard_map/ppermute | solution.py:440
  168.7 2.1 copy-start.10
  169.8 0.7 copy-start.7
  173.9 13.0 %copy-start.8 = (bf16[256,512]{1,0:T(8,128)(2,1)S(1)}, bf16[256,512]{1,0:T(8,128)(2,1)}, u32[]{:S(2)}) copy-start(bf16[256,512]{1,0:T(8,128)(2,1)} %copy-done.7) | copy-start | bytes 786436
  173.9 13.0 %all-to-all-start.5 = ((bf16[16,8,512]{2,1,0:T(8,128)(2,1)}), bf16[16,8,512]{2,1,0:T(8,128)(2,1)S(1)}, u32[]{:S(2)}, u32[]{:S(2)}) async-start(bf16[16,8,512]{2,1,0:T(8,128)(2,1)} %shard_map.70), calls=%async_computation.5 | async-start | bytes 262144 | tf_op jit(solution)/shard_map/all_to_all | solution.py:453
  177.7 33.9 %copy-start.4 = (bf16[1,1,1024,128]{3,2,1,0:T(8,128)(2,1)S(1)}, bf16[1,1,1024,128]{3,2,1,0:T(8,128)(2,1)}, u32[]{:S(2)}) copy-start(bf16[1,1,1024,128]{3,2,1,0:T(8,128)(2,1)} %param.6) | copy-start | bytes 786436
  179.8 31.7 %copy-start.2 = (bf16[1,1,1024,1024]{3,2,1,0:T(8,128)(2,1)S(1)}, bf16[1,1,1024,1024]{3,2,1,0:T(8,128)(2,1)}, u32[]{:S(2)}) copy-start(bf16[1,1,1024,1024]{3,2,1,0:T(8,128)(2,1)} %param.7) | copy-start | bytes 6291460
  207.7 3.9 %collective-permute-start.3 = (bf16[2048,128]{1,0:T(8,128)(2,1)S(1)}, bf16[2048,128]{1,0:T(8,128)(2,1)S(1)}, u32[]{:S(2)}, u32[]{:S(2)}) collective-permute-start(bf16[2048,128]{1,0:T(8,128)(2,1)S(1)} %bitcast.26), channel_id=1, source_target_pairs={{0,32},{32,0},{1,33},{33,1},{2,34},{34,2},{3,35},{35,3},{4,36},{36... | collective-permute-start | bytes 1572872 | tf_op jit(solution)/shard_map/ppermute | solution.py:461
Sparse Core Ops, SparseCore 0:
  47.1 34.3 all-gather.5
Sparse Core Ops, SparseCore 1:
  120.5 40.4 all-gather.3

commit v8 on v7

--- a/solution.py
+++ b/solution.py
@@ -27,7 +27,7 @@
         in_specs=specs,
         out_specs=jax.tree.map(lambda _: VM, outs),
         scratch_shapes=scratch,
-        compiler_params=pltpu.CompilerParams(vmem_limit_bytes=grant * MIB),
+        compiler_params=pltpu.CompilerParams(vmem_limit_bytes=int(grant * MIB)),
         cost_estimate=pl.CostEstimate(flops=flops, bytes_accessed=moved, transcendentals=0),
     )(*args)
 
@@ -103,12 +103,6 @@
                 jnp.dot(picked, high, preferred_element_type=F32)
                 + jnp.dot(picked, low, preferred_element_type=F32)
             ).astype(BF16)
-
-
-def lay_halves(target, slot, side, mine, other):
-    rows = mine.shape[0]
-    target[slot, pl.ds(pl.multiple_of(side * rows, rows), rows), :] = mine
-    target[slot, pl.ds(pl.multiple_of((1 - side) * rows, rows), rows), :] = other
 
 
 def sort_maps(got_ref, maps_ref):
@@ -247,20 +241,30 @@
     joined[0:n] = state[...].astype(BF16)
     joined[n : 2 * n] = right[:, 0:n].astype(BF16)
     joined[2 * n : 3 * n] = right[:, n : 2 * n].astype(BF16)
-    rows = ends_ref.shape[1] - 2 * part
-    half = joined[pl.ds(pl.multiple_of(side * rows, rows), rows), :]
+    half = joined[:, pl.ds(pl.multiple_of(side * slim, slim), slim)]
     for x in range(ends_ref.shape[0]):
-        ends_ref[x, 0:rows] = half
-        ends_ref[x, rows : rows + 2 * part] = ends
-
-
-def meet_values(place, ends_ref, other_ref, maps_ref, own_ref, out_ref, entering, joined_ref):
-    count, _, n = ends_ref.shape
+        ends_ref[x, 0 : 3 * n] = half
+        for k in range(n // slim):
+            at = 3 * n + 2 * part * k
+            ends_ref[x, at : at + 2 * part] = ends[:, k * slim : (k + 1) * slim]
+
+
+def meet_values(place, ends_ref, other_ref, maps_ref, own_ref, out_ref, entering):
+    count, _, slim = ends_ref.shape
+    n = maps_ref.shape[1]
     part = own_ref.shape[0]
     here, side = place[0], place[1]
-    rows = ends_ref.shape[1] - 2 * part
-    for b in range(count):
-        lay_halves(joined_ref, b, side, ends_ref[b, 0:rows], other_ref[b, 0:rows])
+
+    def through(value, b, rows):
+        turned = jnp.concatenate([value[:, slim:], value[:, :slim]], axis=1)
+        maps = jnp.concatenate([ends_ref[b, rows, :], other_ref[b, rows, :]], axis=1)
+        return exact_rows(jnp.where(side == 0, value, turned), maps)
+
+    def end_of(b):
+        both = ends_ref[b, 3 * n : 3 * n + 2 * part * (n // slim)].astype(F32)
+        pieces = [both[k * 2 * part : (k + 1) * 2 * part] for k in range(n // slim)]
+        return jnp.concatenate(pieces, axis=1)
+
     east = jnp.zeros((part, n), F32)
     sources = []
     for b in range(count):
@@ -269,12 +273,12 @@
         def _(east=east):
             entering[:, 0:n] = east
 
-        end = ends_ref[b, rows : rows + 2 * part].astype(F32)
+        end = end_of(b)
         source = end[part : 2 * part]
         if b:
-            source = source + exact_rows(east, joined_ref[b, 2 * n : 3 * n, :])
+            source = source + through(east, b, slice(2 * n, 3 * n))
         sources.append(source)
-        east = end[0:part] + (exact_rows(east, joined_ref[b, 0:n, :]) if b else 0.0)
+        east = end[0:part] + (through(east, b, slice(0, n)) if b else 0.0)
     west = jnp.zeros((part, n), F32)
     for b in range(count - 1, -1, -1):
 
@@ -282,9 +286,7 @@
         def _(west=west):
             entering[:, n : 2 * n] = west
 
-        west = sources[b] + (
-            exact_rows(west, joined_ref[b, n : 2 * n, :]) if b < count - 1 else 0.0
-        )
+        west = sources[b] + (through(west, b, slice(n, 2 * n)) if b < count - 1 else 0.0)
     east = entering[:, 0:n]
     west = entering[:, n : 2 * n]
     own = own_ref[...]
@@ -346,7 +348,7 @@
         rows_map,
         west,
         east,
-        grant=52,
+        grant=60.9,
     )
     pieces = exchange(pieces, GRP)
 
@@ -417,7 +419,7 @@
     ends, own_maps, own_values = call(
         run_block,
         (
-            jax.ShapeDtypeStruct((nx, 3 * n // nc + 2 * part, n), BF16),
+            jax.ShapeDtypeStruct((nx, 3 * n + 2 * part * nc, n // nc), BF16),
             jax.ShapeDtypeStruct((3 * n, n), BF16),
             jax.ShapeDtypeStruct((part, 2 * n), F32),
         ),
@@ -441,7 +443,7 @@
     met = call(
         meet_values,
         jax.ShapeDtypeStruct((peers, part, 2 * n), BF16),
-        [pltpu.VMEM((part, 2 * n), F32), pltpu.VMEM((nx, 3 * n, n), BF16)],
+        [pltpu.VMEM((part, 2 * n), F32)],
         1,
         (12 * nx * n * n * 16, 6 * nx * n * n),
         at_x,

time: 223 us -> 223 us (level)
  no operation moved by 1% of the time
where the time goes in v8:
time: 223 us; the launch traced here: 222 us
  waiting for transfers between devices  75.5 us (34%)
  blocking collectives  60 us (27%)
  starting transfers between devices  39.2 us (18%)
  Pallas kernels  21.7 us (10%)
  between operations  15 us (7%)
  local copies, waits for them, and re-layouts  7.42 us (3%)
  matrix products  2.32 us (1%)
    all_gather x1, waiting for transfers between devices, on_device(): run_half = lax.all_gather(maps, 'y')  34.5 us
    all_to_all x1, blocking collectives, exchange(): return lax.all_to_all(value, axis, 0, 0)  24.9 us
    all_to_all x2, waiting for transfers between devices, exchange(): return lax.all_to_all(value, axis, 0, 0)  23 us
    pallas_call x9, Pallas kernels, call(): pl.pallas_call(kernel, out_shape=outs, in_specs=specs, out_specs=jax.tree...  21.7 us
    all_to_all x1, blocking collectives, on_device(): final_own = lax.all_to_all(final, 'z', 0, 0).reshape(half, columns)  20.4 us
    all_to_all x1, blocking collectives, on_device(): ends = lax.all_to_all(ends, 'x', 0, 0)  14.7 us
    all_to_all x2, starting transfers between devices, exchange(): return lax.all_to_all(value, axis, 0, 0)  9.12 us
    ppermute x1, starting transfers between devices, on_device(): got = lax.ppermute(send, 'c', swap)  8.75 us
  transfers between devices with their start and end apart: 10, of which 7 were waited for; matrix products, arithmetic and copies ran while one was open for 1% of the time, Pallas kernels for 7%

profile of v8, /device:TPU:1, one launch (start us, length us, event | category | flops | bytes accessed | tf_op | source)
XLA Modules:
  0.0 222.2 jit_solution(11868428637537699422)
XLA Ops:
  7.4 0.7 fusion.5.pos
  8.1 1.6 copy-done.1
  9.7 0.9 copy-done.3
  10.6 2.6 %shard_map.65 = (bf16[2048,128]{1,0:T(8,128)(2,1)S(1)}, bf16[2048,128]{1,0:T(8,128)(2,1)S(1)}) custom-call(s32[1024]{0:T(1024)S(1)} %fusion.5.pos, bf16[1024,1024]{1,0:T(8,128)(2,1)S(1)} %bitcast.24, bf16[1024,128]{1,0:T(8,128)(2,1)S(1)} %bitcast.28), custom_call_target="tpu_custom_call" | custom-call | flops 268435456 | bytes 6291456 | tf_op jit(solution)/shard_map/pallas_call | solution.py:24
  13.2 8.7 %collective-permute-start = (bf16[2048,128]{1,0:T(8,128)(2,1)S(1)}, bf16[2048,128]{1,0:T(8,128)(2,1)S(1)}, u32[]{:S(2)}, u32[]{:S(2)}) collective-permute-start(bf16[2048,128]{1,0:T(8,128)(2,1)S(1)} %get-tuple-element.17), channel_id=1, source_target_pairs={{0,32},{32,0},{1,33},{33,1},{2,34},{34,2},{3,35},{35,3},{4,36},{36... | collective-permute-start | bytes 1572872 | tf_op jit(solution)/shard_map/ppermute | solution.py:367
  21.9 3.4 %shard_map.64 = bf16[16,112,128]{2,1,0:T(8,128)(2,1)} custom-call(bf16[256,4096]{1,0:T(8,128)(2,1)} %bitcast.22, f32[256,256]{1,0:T(8,128)} %bitcast.30, f32[256,256]{1,0:T(8,128)} %bitcast.32), custom_call_target="tpu_custom_call" | custom-call | flops 8388608 | bytes 2097152 | tf_op jit(solution)/shard_map/pallas_call | solution.py:24
  25.3 5.1 %all-to-all-start = ((bf16[16,112,128]{2,1,0:T(8,128)(2,1)}), bf16[16,112,128]{2,1,0:T(8,128)(2,1)S(1)}, u32[]{:S(2)}, u32[]{:S(2)}) async-start(bf16[16,112,128]{2,1,0:T(8,128)(2,1)} %shard_map.64), calls=%async_computation | async-start | bytes 917504 | tf_op jit(solution)/shard_map/all_to_all | solution.py:36
  30.6 15.7 %all-to-all-done.rows_ref.got_ref = bf16[16,112,128]{2,1,0:T(8,128)(2,1)S(1)} async-done(((bf16[16,112,128]{2,1,0:T(8,128)(2,1)}), bf16[16,112,128]{2,1,0:T(8,128)(2,1)S(1)}, u32[]{:S(2)}, u32[]{:S(2)}) %all-to-all-start) | async-done | bytes 458784 | tf_op jit(solution)/shard_map/all_to_all | solution.py:36
  47.0 34.5 %all-gather.6.cloned.1.call-done = bf16[6144,128]{1,0:T(8,128)(2,1)} async-done(((bf16[768,128]{1,0:T(8,128)(2,1)}), bf16[6144,128]{1,0:T(8,128)(2,1)}) %all-gather.6.cloned.1.call-update) | async-done | bytes 1572880 | tf_op jit(solution)/shard_map/all_gather | solution.py:378
  81.5 6.8 %collective-permute-start.1 = (bf16[8,768,128]{2,1,0:T(8,128)(2,1)}, bf16[8,768,128]{2,1,0:T(8,128)(2,1)S(1)}, u32[]{:S(2)}, u32[]{:S(2)}) collective-permute-start(bf16[8,768,128]{2,1,0:T(8,128)(2,1)} %bitcast.34), channel_id=1, source_target_pairs={{0,32},{32,0},{1,33},{33,1},{2,34},{34,2},{3,35},{35,3},{4,36},{36... | collective-permute-start | bytes 4718600 | tf_op jit(solution)/shard_map/ppermute | solution.py:417
  88.3 24.9 %all_to_all.35.parts_ref = bf16[8,256,128]{2,1,0:T(8,128)(2,1)S(1)} all-to-all(bf16[8,256,128]{2,1,0:T(8,128)(2,1)S(1)} %bitcast.36), channel_id=1, replica_groups=mesh['z'=8,'c'=2,'x'=4,'y'=8] {'z'}, dimensions={0} | all-to-all | bytes 1048576 | tf_op jit(solution)/shard_map/all_to_all | solution.py:36
  113.2 1.0 shard_map.66
  114.2 3.8 %all-to-all-start.2 = ((bf16[16,8,512]{2,1,0:T(8,128)(2,1)}), bf16[16,8,512]{2,1,0:T(8,128)(2,1)S(1)}, u32[]{:S(2)}, u32[]{:S(2)}) async-start(bf16[16,8,512]{2,1,0:T(8,128)(2,1)} %get-tuple-element.21), calls=%async_computation.2 | async-start | bytes 262144 | tf_op jit(solution)/shard_map/all_to_all | solution.py:405
  118.5 8.6 %all-to-all-done.2.got_ref = bf16[16,8,512]{2,1,0:T(8,128)(2,1)S(1)} async-done(((bf16[16,8,512]{2,1,0:T(8,128)(2,1)}), bf16[16,8,512]{2,1,0:T(8,128)(2,1)S(1)}, u32[]{:S(2)}, u32[]{:S(2)}) %all-to-all-start.2) | async-done | bytes 131104 | tf_op jit(solution)/shard_map/all_to_all | solution.py:405
  127.8 4.0 %all-to-all-start.3 = ((bf16[8,8,512]{2,1,0:T(8,128)(2,1)}), bf16[8,8,512]{2,1,0:T(8,128)(2,1)S(1)}, u32[]{:S(2)}, u32[]{:S(2)}) async-start(bf16[8,8,512]{2,1,0:T(8,128)(2,1)} %shard_map.67), calls=%async_computation.3 | async-start | bytes 131072 | tf_op jit(solution)/shard_map/all_to_all | solution.py:36
  131.9 7.4 %all-to-all-done.3.faces_ref = bf16[8,8,512]{2,1,0:T(8,128)(2,1)S(1)} async-done(((bf16[8,8,512]{2,1,0:T(8,128)(2,1)}), bf16[8,8,512]{2,1,0:T(8,128)(2,1)S(1)}, u32[]{:S(2)}, u32[]{:S(2)}) %all-to-all-start.3) | async-done | bytes 65568 | tf_op jit(solution)/shard_map/all_to_all | solution.py:36
  139.3 1.2 copy-done.12
  140.4 1.4 copy-done.11
  141.8 1.4 copy-done.13
  143.2 6.3 %shard_map.69 = (bf16[4,800,128]{2,1,0:T(8,128)(2,1)S(1)}, bf16[768,256]{1,0:T(8,128)(2,1)S(1)}, f32[8,512]{1,0:T(8,128)S(1)}) custom-call(s32[2]{0:T(128)S(1)} %pad_add_fusion.1.place, bf16[8,8,512]{2,1,0:T(8,128)(2,1)S(1)} %all-to-all-done.3.faces_ref, bf16[8,768,128]{2,1,0:T(8,128)(2,1)S(1)} %bitcast.35, bf16[8,768,128]{2,1,0:T(8,128)(2,1)S(1)} %copy-done.13), custom_call_target="tpu_custom_call" | custom-call | flops 2147483648 | bytes 3145728 | tf_op jit(solution)/shard_map/pallas_call | solution.py:24
  149.5 14.7 %all_to_all.36.ends_ref = bf16[4,800,128]{2,1,0:T(8,128)(2,1)S(1)} all-to-all(bf16[4,800,128]{2,1,0:T(8,128)(2,1)S(1)} %get-tuple-element.22), channel_id=1, replica_groups=mesh['z'=8,'c'=2,'x'=4,'y'=8] {'x'}, dimensions={0} | all-to-all | bytes 1638400 | tf_op jit(solution)/shard_map/all_to_all | solution.py:441
  164.3 4.5 %collective-permute-start.2 = (bf16[4,800,128]{2,1,0:T(8,128)(2,1)S(1)}, bf16[4,800,128]{2,1,0:T(8,128)(2,1)}, u32[]{:S(2)}, u32[]{:S(2)}) collective-permute-start(bf16[4,800,128]{2,1,0:T(8,128)(2,1)S(1)} %all_to_all.36.ends_ref), channel_id=1, source_target_pairs={{0,32},{32,0},{1,33},{33,1},{2,34},{34,2},{3,35},{35,3},{4,36},{36... | collective-permute-start | bytes 2457608 | tf_op jit(solution)/shard_map/ppermute | solution.py:442
  168.9 1.0 shard_map.71
  170.0 0.7 copy-done.7
  170.9 3.0 %shard_map.70 = bf16[16,8,512]{2,1,0:T(8,128)(2,1)} custom-call(s32[2]{0:T(128)S(1)} %pad_add_fusion.place, bf16[4,800,128]{2,1,0:T(8,128)(2,1)S(1)} %all_to_all.36.ends_ref, bf16[4,800,128]{2,1,0:T(8,128)(2,1)} %collective-permute-done.2.other_ref, bf16[768,256]{1,0:T(8,128)(2,1)S(1)} %copy-done.10, f32[8,512]{1,0:T(8,128)S(1)} %get-tuple-element.24.own_ref), custom_call_target="tpu_custom_call" | custom-call | flops 50331648 | bytes 1572864 | tf_op jit(solution)/shard_map/pallas_call | solution.py:24
  173.9 3.8 %all-to-all-start.5 = ((bf16[16,8,512]{2,1,0:T(8,128)(2,1)}), bf16[16,8,512]{2,1,0:T(8,128)(2,1)S(1)}, u32[]{:S(2)}, u32[]{:S(2)}) async-start(bf16[16,8,512]{2,1,0:T(8,128)(2,1)} %shard_map.70), calls=%async_computation.5 | async-start | bytes 262144 | tf_op jit(solution)/shard_map/all_to_all | solution.py:455
  177.8 2.1 convolution_bitcast_fusion
  179.9 7.0 %all-to-all-done.5 = bf16[16,8,512]{2,1,0:T(8,128)(2,1)S(1)} async-done(((bf16[16,8,512]{2,1,0:T(8,128)(2,1)}), bf16[16,8,512]{2,1,0:T(8,128)(2,1)S(1)}, u32[]{:S(2)}, u32[]{:S(2)}) %all-to-all-start.5) | async-done | bytes 131104 | tf_op jit(solution)/shard_map/all_to_all | solution.py:455
  187.3 20.4 %all_to_all.37 = bf16[8,256,128]{2,1,0:T(8,128)(2,1)S(1)} all-to-all(bf16[8,256,128]{2,1,0:T(8,128)(2,1)S(1)} %broadcast_in_dim.6), channel_id=1, replica_groups=mesh['z'=8,'c'=2,'x'=4,'y'=8] {'z'}, dimensions={0} | all-to-all | bytes 1048576 | tf_op jit(solution)/shard_map/all_to_all | solution.py:462
  207.8 2.3 %collective-permute-start.3 = (bf16[2048,128]{1,0:T(8,128)(2,1)S(1)}, bf16[2048,128]{1,0:T(8,128)(2,1)S(1)}, u32[]{:S(2)}, u32[]{:S(2)}) collective-permute-start(bf16[2048,128]{1,0:T(8,128)(2,1)S(1)} %bitcast.26), channel_id=1, source_target_pairs={{0,32},{32,0},{1,33},{33,1},{2,34},{34,2},{3,35},{35,3},{4,36},{36... | collective-permute-start | bytes 1572872 | tf_op jit(solution)/shard_map/ppermute | solution.py:463
  210.1 1.5 collective-permute-done.3.other_ref
  211.6 3.1 %shard_map.72 = bf16[1024,128]{1,0:T(8,128)(2,1)} custom-call(s32[1024]{0:T(1024)S(1)} %fusion.5.pos, bf16[2048,128]{1,0:T(8,128)(2,1)S(1)} %bitcast.27, bf16[2048,128]{1,0:T(8,128)(2,1)S(1)} %collective-permute-done.3.other_ref, bf16[1024,1024]{1,0:T(8,128)(2,1)S(1)} %bitcast.25, bf16[1024,128]{1,0:T(8,128)(2,1)S(1)} %bitcast.29), custom_call_target="tpu_custom_call" | custom-call | flops 268435456 | bytes 2097152 | tf_op jit(solution)/shard_map/pallas_call | solution.py:24
  (38 shorter events, 3.0 us)
Async XLA Ops:
  8.1 1.6 copy-start.1
  9.7 0.9 copy-start.3
  13.2 17.3 %collective-permute-start = (bf16[2048,128]{1,0:T(8,128)(2,1)S(1)}, bf16[2048,128]{1,0:T(8,128)(2,1)S(1)}, u32[]{:S(2)}, u32[]{:S(2)}) collective-permute-start(bf16[2048,128]{1,0:T(8,128)(2,1)S(1)} %get-tuple-element.17), channel_id=1, source_target_pairs={{0,32},{32,0},{1,33},{33,1},{2,34},{34,2},{3,35},{35,3},{4,36},{36... | collective-permute-start | bytes 1572872 | tf_op jit(solution)/shard_map/ppermute | solution.py:367
  25.3 20.9 %all-to-all-start = ((bf16[16,112,128]{2,1,0:T(8,128)(2,1)}), bf16[16,112,128]{2,1,0:T(8,128)(2,1)S(1)}, u32[]{:S(2)}, u32[]{:S(2)}) async-start(bf16[16,112,128]{2,1,0:T(8,128)(2,1)} %shard_map.64), calls=%async_computation | async-start | bytes 917504 | tf_op jit(solution)/shard_map/all_to_all | solution.py:36
  30.4 51.1 %all-gather.6.cloned.1.call-start = ((), (), s32[]{:S(2)}) async-start(), calls=%async_computation.8 | async-start | bytes 1769472 | tf_op jit(solution)/shard_map/all_gather | solution.py:378
  81.5 57.7 %collective-permute-start.1 = (bf16[8,768,128]{2,1,0:T(8,128)(2,1)}, bf16[8,768,128]{2,1,0:T(8,128)(2,1)S(1)}, u32[]{:S(2)}, u32[]{:S(2)}) collective-permute-start(bf16[8,768,128]{2,1,0:T(8,128)(2,1)} %bitcast.34), channel_id=1, source_target_pairs={{0,32},{32,0},{1,33},{33,1},{2,34},{34,2},{3,35},{35,3},{4,36},{36... | collective-permute-start | bytes 4718600 | tf_op jit(solution)/shard_map/ppermute | solution.py:417
  114.2 13.0 %all-to-all-start.2 = ((bf16[16,8,512]{2,1,0:T(8,128)(2,1)}), bf16[16,8,512]{2,1,0:T(8,128)(2,1)S(1)}, u32[]{:S(2)}, u32[]{:S(2)}) async-start(bf16[16,8,512]{2,1,0:T(8,128)(2,1)} %get-tuple-element.21), calls=%async_computation.2 | async-start | bytes 262144 | tf_op jit(solution)/shard_map/all_to_all | solution.py:405
  117.9 59.8 %all-gather.4.cloned.1.call-start = ((), (), s32[]{:S(2)}) async-start(), calls=%async_computation.7 | async-start | bytes 1114112 | tf_op jit(solution)/shard_map/all_gather | solution.py:415
  127.8 11.5 %all-to-all-start.3 = ((bf16[8,8,512]{2,1,0:T(8,128)(2,1)}), bf16[8,8,512]{2,1,0:T(8,128)(2,1)S(1)}, u32[]{:S(2)}, u32[]{:S(2)}) async-start(bf16[8,8,512]{2,1,0:T(8,128)(2,1)} %shard_map.67), calls=%async_computation.3 | async-start | bytes 131072 | tf_op jit(solution)/shard_map/all_to_all | solution.py:36
  131.9 37.0 %copy-start.5 = (f32[1,256,256]{2,1,0:T(8,128)S(1)}, f32[1,256,256]{2,1,0:T(8,128)}, u32[]{:S(2)}) copy-start(f32[1,256,256]{2,1,0:T(8,128)} %param.10) | copy-start | bytes 786436
  131.9 37.0 %copy-start.6 = (f32[1,256,256]{2,1,0:T(8,128)S(1)}, f32[1,256,256]{2,1,0:T(8,128)}, u32[]{:S(2)}) copy-start(f32[1,256,256]{2,1,0:T(8,128)} %param.11) | copy-start | bytes 786436
  139.2 1.2 copy-start.12
  140.4 1.4 copy-start.11
  141.8 1.4 copy-start.13
  143.2 25.7 %copy-start = (bf16[1,256,4096]{2,1,0:T(8,128)(2,1)S(1)}, bf16[1,256,4096]{2,1,0:T(8,128)(2,1)}, u32[]{:S(2)}) copy-start(bf16[1,256,4096]{2,1,0:T(8,128)(2,1)} %param.8) | copy-start | bytes 6291460
  149.5 14.7 %copy-start.9 = (bf16[768,256]{1,0:T(8,128)(2,1)}, bf16[768,256]{1,0:T(8,128)(2,1)S(1)}, u32[]{:S(2)}) copy-start(bf16[768,256]{1,0:T(8,128)(2,1)S(1)} %get-tuple-element.23.maps_ref) | copy-start | bytes 1179652
  164.3 6.6 %collective-permute-start.2 = (bf16[4,800,128]{2,1,0:T(8,128)(2,1)S(1)}, bf16[4,800,128]{2,1,0:T(8,128)(2,1)}, u32[]{:S(2)}, u32[]{:S(2)}) collective-permute-start(bf16[4,800,128]{2,1,0:T(8,128)(2,1)S(1)} %all_to_all.36.ends_ref), channel_id=1, source_target_pairs={{0,32},{32,0},{1,33},{33,1},{2,34},{34,2},{3,35},{35,3},{4,36},{36... | collective-permute-start | bytes 2457608 | tf_op jit(solution)/shard_map/ppermute | solution.py:442
  168.8 2.1 copy-start.10
  169.9 0.7 copy-start.7
  173.9 13.0 %copy-start.8 = (bf16[256,512]{1,0:T(8,128)(2,1)S(1)}, bf16[256,512]{1,0:T(8,128)(2,1)}, u32[]{:S(2)}) copy-start(bf16[256,512]{1,0:T(8,128)(2,1)} %copy-done.7) | copy-start | bytes 786436
  173.9 13.0 %all-to-all-start.5 = ((bf16[16,8,512]{2,1,0:T(8,128)(2,1)}), bf16[16,8,512]{2,1,0:T(8,128)(2,1)S(1)}, u32[]{:S(2)}, u32[]{:S(2)}) async-start(bf16[16,8,512]{2,1,0:T(8,128)(2,1)} %shard_map.70), calls=%async_computation.5 | async-start | bytes 262144 | tf_op jit(solution)/shard_map/all_to_all | solution.py:455
  177.7 33.9 %copy-start.4 = (bf16[1,1,1024,128]{3,2,1,0:T(8,128)(2,1)S(1)}, bf16[1,1,1024,128]{3,2,1,0:T(8,128)(2,1)}, u32[]{:S(2)}) copy-start(bf16[1,1,1024,128]{3,2,1,0:T(8,128)(2,1)} %param.6) | copy-start | bytes 786436
  179.9 31.7 %copy-start.2 = (bf16[1,1,1024,1024]{3,2,1,0:T(8,128)(2,1)S(1)}, bf16[1,1,1024,1024]{3,2,1,0:T(8,128)(2,1)}, u32[]{:S(2)}) copy-start(bf16[1,1,1024,1024]{3,2,1,0:T(8,128)(2,1)} %param.7) | copy-start | bytes 6291460
  207.8 3.9 %collective-permute-start.3 = (bf16[2048,128]{1,0:T(8,128)(2,1)S(1)}, bf16[2048,128]{1,0:T(8,128)(2,1)S(1)}, u32[]{:S(2)}, u32[]{:S(2)}) collective-permute-start(bf16[2048,128]{1,0:T(8,128)(2,1)S(1)} %bitcast.26), channel_id=1, source_target_pairs={{0,32},{32,0},{1,33},{33,1},{2,34},{34,2},{3,35},{35,3},{4,36},{36... | collective-permute-start | bytes 1572872 | tf_op jit(solution)/shard_map/ppermute | solution.py:463
Sparse Core Ops, SparseCore 0:
  47.1 34.3 all-gather.5
Sparse Core Ops, SparseCore 1:
  120.5 40.4 all-gather.3
